TPU v7x, 32 devices: a whole 2x2x4 slice. The times are simulated.
32 devices in a mesh: ctx: 8 (over z, y), dp: 4 (over x, core).
Axes of the slice: x: 2, y: 2, z: 4, core: 2. Of those that a mesh axis runs over, the one named last changes fastest.
Arguments:
- tokens: bfloat16 [4, 4096, 768], P('dp', 'ctx'), may hold values from -6 to 6
- cotangent: bfloat16 [4, 4096, 768], P('dp', 'ctx'), may hold values from -6 to 6
- attn_gain: bfloat16 [768], P('dp'), may hold values from 0.099609375 to 1.8984375
- mlp_gain: bfloat16 [768], P('dp'), may hold values from 0.099609375 to 1.8984375
- w_qkv: bfloat16 [768, 2304], P('dp'), may hold values from -0.21875 to 0.21875
- w_out: bfloat16 [768, 768], P('dp'), may hold values from -6 to 6
- w_in: bfloat16 [768, 2304], P('dp'), may hold values from -0.21875 to 0.21875
- w_mlp_out: bfloat16 [1152, 768], P('dp'), may hold values from -0.1875 to 0.1875
- block_offsets: int32 [4, 8], P('dp', 'ctx'), may hold values from 0 to 3584, as said below
Outputs:
- mixed: bfloat16 [4, 4096, 768], P('dp', 'ctx')
- tokens_grad: float32 [4, 4096, 768], P('dp', 'ctx')
- attn_gain_grad: float32 [768], P('dp')
- mlp_gain_grad: float32 [768], P('dp')
- w_qkv_grad: float32 [768, 2304], P('dp')
- w_out_grad: float32 [768, 768], P('dp')
- w_in_grad: float32 [768, 2304], P('dp')
- w_mlp_out_grad: float32 [1152, 768], P('dp')
Inputs may be any that keep to these rules, and one draw needn't show every extreme that they name: `block_offsets`: each row holds every multiple of 512 below 4096 exactly once.
All inputs are finite; a program needn't handle non-finite values.
Results may differ from a plain program's by a relative error of at most 0.022.
Values may be sent and summed in bfloat16 or wider, within the bound.
No kernel may reach another device: no remote copies, remote signals or barrier semaphores. Data moves between devices by JAX's collectives and lax.ppermute only.
A program may use at most 128 MiB of HBM per device.

v0:
```python
import jax
import jax.numpy as jnp
from jax import lax
from jax.sharding import PartitionSpec as P

HEADS = 12
HEAD_DIM = 64
FF = 1152


rope_base = 160000.0
norm_eps = 1e-05


def passed_along(x, axis, by):
    count = lax.axis_size(axis)
    return lax.ppermute(x, axis, [(i, (i + by) % count) for i in range(count)])


def layer_norm(values, gain):
    center = values - jnp.mean(values, axis=-1, keepdims=True)
    spread = jnp.mean(center * center, axis=-1, keepdims=True)
    return center * lax.rsqrt(spread + norm_eps) * gain


def norm_back(values, gain, upstream):
    _, pull = jax.vjp(layer_norm, values, gain)
    return pull(upstream)


def rotary_tables(positions, half_size):
    frequency = rope_base ** (-jnp.arange(half_size, dtype=jnp.float32) / half_size)
    angles = positions[:, None] * frequency[None, :]
    cosine = jnp.cos(angles)
    sine_table = jnp.sin(angles)
    return (jnp.concatenate([cosine, cosine], -1), jnp.concatenate([sine_table, sine_table], -1))


def rotate(values, cosine, sine_table):
    half_size = values.shape[-1] // 2
    turned = jnp.concatenate([-values[..., half_size:], values[..., :half_size]], -1)
    return values * cosine[:, None, :] + turned * sine_table[:, None, :]


def unrotate(upstream, cosine, sine_table):
    half_size = upstream.shape[-1] // 2
    turned = upstream * sine_table[:, None, :]
    return upstream * cosine[:, None, :] + jnp.concatenate(
        [turned[..., half_size:], -turned[..., :half_size]], -1
    )


def geglu(packed, hidden_size):
    return jax.nn.gelu(packed[:, :hidden_size], approximate=False) * packed[:, hidden_size:]


def product(left, right):
    return jnp.dot(left, right, preferred_element_type=jnp.float32)


def transposed_left(left, right):
    return lax.dot_general(
        left, right, (((0,), (0,)), ((), ())), preferred_element_type=jnp.float32
    )


def transposed_right(left, right):
    return lax.dot_general(
        left, right, (((1,), (1,)), ((), ())), preferred_element_type=jnp.float32
    )


def key_block():
    return 512


def body(tokens, cotangent, attn_gain, mlp_gain, w_qkv, w_out, w_in, w_mlp_out, block_offsets):
    head_count = HEADS
    head_size = HEAD_DIM
    hidden_size = FF
    model_width = head_count * head_size
    scale = head_size ** (-0.5)
    inputs = tokens[0].astype(jnp.float32)
    row_count = inputs.shape[0]
    positions = (block_offsets[0, 0] + jnp.arange(row_count, dtype=jnp.int32)).astype(jnp.float32)
    cosine, sine_table = rotary_tables(positions, head_size // 2)
    gain_one, gain_two, weight_qkv, weight_out, weight_in, weight_down = (
        lax.all_gather(attn_gain, "dp", axis=0, tiled=True),
        lax.all_gather(mlp_gain, "dp", axis=0, tiled=True),
        lax.all_gather(w_qkv, "dp", axis=0, tiled=True),
        lax.all_gather(w_out, "dp", axis=0, tiled=True),
        lax.all_gather(w_in, "dp", axis=0, tiled=True),
        lax.all_gather(w_mlp_out, "dp", axis=0, tiled=True),
    )
    first_gain = gain_one.astype(jnp.float32)
    second_gain = gain_two.astype(jnp.float32)
    normed = layer_norm(inputs, first_gain).astype(jnp.bfloat16)
    packed = product(normed, weight_qkv).reshape(row_count, 3, head_count, head_size)
    queries = rotate(packed[:, 0], cosine, sine_table).astype(jnp.bfloat16)
    keys_local = (
        rotate(packed[:, 1], cosine, sine_table)
        .astype(jnp.bfloat16)
        .reshape(row_count, model_width)
    )
    values_local = packed[:, 2].astype(jnp.bfloat16).reshape(row_count, model_width)

    def attend(carried, blocks):
        running_max, running_sum, running_out = carried
        key_part, value_part = blocks
        scores = (
            jnp.einsum("qhd,khd->hqk", queries, key_part, preferred_element_type=jnp.float32)
            * scale
        )
        new_max = jnp.maximum(running_max, jnp.max(scores, axis=-1))
        rescale = jnp.exp(running_max - new_max)
        weights = jnp.exp(scores - new_max[:, :, None])
        running_sum = running_sum * rescale + jnp.sum(weights, axis=-1)
        running_out = running_out * rescale.T[:, :, None] + jnp.einsum(
            "hqk,khd->qhd",
            weights.astype(jnp.bfloat16),
            value_part,
            preferred_element_type=jnp.float32,
        )
        return ((new_max, running_sum, running_out), None)

    initial = (
        jnp.full((head_count, row_count), -1e30, jnp.float32),
        jnp.zeros((head_count, row_count), jnp.float32),
        jnp.zeros((row_count, head_count, head_size), jnp.float32),
    )
    carried = initial
    shards = (
        lax.all_gather(keys_local, "ctx", axis=0, tiled=True),
        lax.all_gather(values_local, "ctx", axis=0, tiled=True),
    )
    key_count = shards[0].shape[0]
    block_size = key_block()
    split_keys = shards[0].reshape(key_count // block_size, block_size, head_count, head_size)
    split_values = shards[1].reshape(key_count // block_size, block_size, head_count, head_size)
    carried, _ = lax.scan(attend, carried, (split_keys, split_values))
    running_max, running_sum, running_out = carried
    attended = running_out / running_sum.T[:, :, None]
    log_total = running_max + jnp.log(running_sum)
    attended_low = attended.reshape(row_count, model_width).astype(jnp.bfloat16)
    residual = inputs + product(attended_low, weight_out)
    mlp_normed = layer_norm(residual, second_gain).astype(jnp.bfloat16)
    up_gate = product(mlp_normed, weight_in)
    joined = geglu(up_gate, hidden_size).astype(jnp.bfloat16)
    outputs = residual + product(joined, weight_down)
    mixed = outputs.astype(jnp.bfloat16)[None]
    gain_one, gain_two, weight_qkv, weight_out, weight_in, weight_down = (
        lax.all_gather(attn_gain, "dp", axis=0, tiled=True),
        lax.all_gather(mlp_gain, "dp", axis=0, tiled=True),
        lax.all_gather(w_qkv, "dp", axis=0, tiled=True),
        lax.all_gather(w_out, "dp", axis=0, tiled=True),
        lax.all_gather(w_in, "dp", axis=0, tiled=True),
        lax.all_gather(w_mlp_out, "dp", axis=0, tiled=True),
    )
    first_gain = gain_one.astype(jnp.float32)
    second_gain = gain_two.astype(jnp.float32)
    upstream = cotangent[0].astype(jnp.float32)
    upstream_low = upstream.astype(jnp.bfloat16)
    grad_down = transposed_left(joined, upstream_low)
    grad_joined = transposed_right(upstream_low, weight_down)
    _, glu_pull = jax.vjp(lambda packed_in: geglu(packed_in, hidden_size), up_gate)
    grad_up_gate = glu_pull(grad_joined)[0].astype(jnp.bfloat16)
    grad_in = transposed_left(mlp_normed, grad_up_gate)
    grad_mlp_normed = transposed_right(grad_up_gate, weight_in)
    grad_residual_norm, grad_gain_two = norm_back(residual, second_gain, grad_mlp_normed)
    grad_residual = upstream + grad_residual_norm
    residual_low = grad_residual.astype(jnp.bfloat16)
    grad_out = transposed_left(attended_low, residual_low)
    grad_attended = (
        transposed_right(residual_low, weight_out)
        .astype(jnp.bfloat16)
        .reshape(row_count, head_count, head_size)
    )
    row_delta = jnp.sum(grad_attended.astype(jnp.float32) * attended, axis=-1).T

    def block_grads(query_rows, grad_rows, log_rows, delta_rows, key_rows, value_rows):
        key_count = key_rows.shape[0]
        query_count = query_rows.shape[0]
        block_size = key_block()
        split_keys = key_rows.reshape(key_count // block_size, block_size, head_count, head_size)
        split_values = value_rows.reshape(
            key_count // block_size, block_size, head_count, head_size
        )

        def backward_block(query_grad, blocks):
            key_part, value_part = blocks
            scores = (
                jnp.einsum("qhd,khd->hqk", query_rows, key_part, preferred_element_type=jnp.float32)
                * scale
            )
            probs = jnp.exp(scores - log_rows[:, :, None])
            prob_grad = jnp.einsum(
                "qhd,khd->hqk", grad_rows, value_part, preferred_element_type=jnp.float32
            )
            score_grad = (probs * (prob_grad - delta_rows[:, :, None])).astype(jnp.bfloat16)
            value_grad = jnp.einsum(
                "hqk,qhd->khd",
                probs.astype(jnp.bfloat16),
                grad_rows,
                preferred_element_type=jnp.float32,
            )
            key_grad = (
                jnp.einsum(
                    "hqk,qhd->khd", score_grad, query_rows, preferred_element_type=jnp.float32
                )
                * scale
            )
            query_grad = (
                query_grad
                + jnp.einsum(
                    "hqk,khd->qhd", score_grad, key_part, preferred_element_type=jnp.float32
                )
                * scale
            )
            return (
                query_grad,
                (
                    key_grad.reshape(block_size, model_width),
                    value_grad.reshape(block_size, model_width),
                ),
            )

        query_start = jnp.zeros((query_count, head_count, head_size), jnp.float32)
        query_grad, (key_grad, value_grad) = lax.scan(
            backward_block, query_start, (split_keys, split_values)
        )
        return (
            query_grad,
            key_grad.reshape(key_count, model_width),
            value_grad.reshape(key_count, model_width),
        )

    zero_rows = jnp.zeros((row_count, model_width), jnp.float32)
    zero_heads = jnp.zeros((row_count, head_count, head_size), jnp.float32)

    def cycle_turn(turn_index, carried):
        key_rows, value_rows, key_sum, value_sum, query_sum = carried
        query_add, key_add, value_add = block_grads(
            queries, grad_attended, log_total, row_delta, key_rows, value_rows
        )
        key_sum = key_sum + key_add
        value_sum = value_sum + value_add
        key_rows, value_rows = passed_along((key_rows, value_rows), "ctx", 1)
        key_sum, value_sum = (
            passed_along(key_sum.astype(jnp.bfloat16), "ctx", 1).astype(key_sum.dtype),
            passed_along(value_sum.astype(jnp.bfloat16), "ctx", 1).astype(value_sum.dtype),
        )
        return (key_rows, value_rows, key_sum, value_sum, query_sum + query_add)

    start_state = (keys_local, values_local, zero_rows, zero_rows, zero_heads)
    _, _, grad_keys, grad_values, grad_queries = lax.fori_loop(
        0, lax.axis_size("ctx"), cycle_turn, start_state
    )
    query_back = unrotate(grad_queries, cosine, sine_table).reshape(row_count, model_width)
    key_back = unrotate(
        grad_keys.reshape(row_count, head_count, head_size), cosine, sine_table
    ).reshape(row_count, model_width)
    grad_packed = jnp.concatenate([query_back, key_back, grad_values], axis=1).astype(jnp.bfloat16)
    grad_qkv = transposed_left(normed, grad_packed)
    grad_normed = transposed_right(grad_packed, weight_qkv)
    grad_inputs_norm, grad_gain_one = norm_back(inputs, first_gain, grad_normed)
    tokens_grad = (grad_residual + grad_inputs_norm)[None]
    summed = (
        lax.psum_scatter(
            grad_gain_one.astype(jnp.bfloat16), "dp", scatter_dimension=0, tiled=True
        ).astype(jnp.float32),
        lax.psum_scatter(
            grad_gain_two.astype(jnp.bfloat16), "dp", scatter_dimension=0, tiled=True
        ).astype(jnp.float32),
        lax.psum_scatter(
            grad_qkv.astype(jnp.bfloat16), "dp", scatter_dimension=0, tiled=True
        ).astype(jnp.float32),
        lax.psum_scatter(
            grad_out.astype(jnp.bfloat16), "dp", scatter_dimension=0, tiled=True
        ).astype(jnp.float32),
        lax.psum_scatter(
            grad_in.astype(jnp.bfloat16), "dp", scatter_dimension=0, tiled=True
        ).astype(jnp.float32),
        lax.psum_scatter(
            grad_down.astype(jnp.bfloat16), "dp", scatter_dimension=0, tiled=True
        ).astype(jnp.float32),
    )
    totals = (
        lax.psum(summed[0].astype(jnp.bfloat16), "ctx").astype(jnp.float32),
        lax.psum(summed[1].astype(jnp.bfloat16), "ctx").astype(jnp.float32),
        lax.psum(summed[2].astype(jnp.bfloat16), "ctx").astype(jnp.float32),
        lax.psum(summed[3].astype(jnp.bfloat16), "ctx").astype(jnp.float32),
        lax.psum(summed[4].astype(jnp.bfloat16), "ctx").astype(jnp.float32),
        lax.psum(summed[5].astype(jnp.bfloat16), "ctx").astype(jnp.float32),
    )
    return (mixed, tokens_grad, totals[0], totals[1], totals[2], totals[3], totals[4], totals[5])


def solution(mesh):
    return jax.shard_map(
        body,
        mesh=mesh,
        in_specs=(
            P("dp", "ctx", None),
            P("dp", "ctx", None),
            P("dp"),
            P("dp"),
            P("dp", None),
            P("dp", None),
            P("dp", None),
            P("dp", None),
            P("dp", "ctx"),
        ),
        out_specs=(
            P("dp", "ctx", None),
            P("dp", "ctx", None),
            P("dp"),
            P("dp"),
            P("dp", None),
            P("dp", None),
            P("dp", None),
            P("dp", None),
        ),
        check_vma=False,
    )
```

profile of v0, /device:TPU:0, one launch (start us, length us, event | category | flops | bytes accessed | tf_op | source)
XLA Modules:
  0.0 1305.3 jit_solution(13983983818318694424)
XLA Ops:
  11.6 8.3 all-reduce.9
  21.6 21.4 %all-gather.7.cloned.1.call-done = bf16[768,2304]{1,0:T(8,128)(2,1)} async-done(((bf16[192,2304]{1,0:T(8,128)(2,1)}), bf16[768,2304]{1,0:T(8,128)(2,1)}) %all-gather.7.cloned.1.call-update) | async-done | bytes 3538960 | tf_op jit(solution)/shard_map/all_gather | solution.py:90
  62.2 94.7 %all-gather.9.cloned.1.call-done = bf16[4096,768]{0,1:T(8,128)(2,1)} async-done(((bf16[512,768]{0,1:T(8,128)(2,1)}), bf16[4096,768]{0,1:T(8,128)(2,1)}) %all-gather.9.cloned.1.call-update) | async-done | bytes 6291472 | tf_op jit(solution)/shard_map/all_gather | solution.py:133
  168.9 87.9 %all-gather.11.cloned.1.call-done = bf16[4096,768]{0,1:T(8,128)(2,1)} async-done(((bf16[512,768]{0,1:T(8,128)(2,1)}), bf16[4096,768]{0,1:T(8,128)(2,1)}) %all-gather.11.cloned.1.call-update) | async-done | bytes 6291472 | tf_op jit(solution)/shard_map/all_gather | solution.py:134
  268.8 145.6 %while.40 = (s32[]{:T(128)}, f32[12,512]{1,0:T(8,128)S(1)}, f32[12,512]{1,0:T(8,128)S(1)}, f32[512,12,64]{0,2,1:T(8,128)S(1)}, bf16[8,512,12,64]{1,3,2,0:T(8,128...) while((s32[]{:T(128)}, f32[12,512]{1,0:T(8,128)S(1)}, ...), condition=%wide.region_5.6_spmd.clone, body=%wide.region_2.5_spmd.clone.sunk | while | flops 831688704 | bytes 93979776 | solution.py:140
  268.8 7.4 bitcast_reduce_fusion.2
  287.9 7.4 bitcast_reduce_fusion.2
  306.1 7.4 bitcast_reduce_fusion.2
  324.5 7.4 bitcast_reduce_fusion.2
  342.5 7.4 bitcast_reduce_fusion.2
  360.4 7.4 bitcast_reduce_fusion.2
  378.4 7.4 bitcast_reduce_fusion.2
  396.4 7.4 bitcast_reduce_fusion.2
  426.4 7.9 fusion.72
  460.9 665.3 %while.41 = (s32[]{:T(128)}, bf16[512,768]{0,1:T(8,128)(2,1)}, bf16[512,768]{0,1:T(8,128)(2,1)}, f32[512,768]{0,1:T(8,128)}, f32[512,768]{0,1:T(8,128)}, /*index...) while((s32[]{:T(128)}, bf16[512,768]{0,1:T(8,128)(2,1)}, ...), condition=%wide.region_12.13_spmd.clone, body=%wide.region_11.12_spmd.clone.sunk | while | flops 2043150336 | bytes 191177200 | solution.py:255
  498.8 15.6 %collective-permute-done.3 = bf16[512,768]{0,1:T(8,128)(2,1)} collective-permute-done((bf16[512,768]{0,1:T(8,128)(2,1)}, bf16[512,768]{0,1:T(8,128)(2,1)}, u32[]{:S(2)}, u32[]{:S(2)}) %collective-permute-start.3) | collective-permute-done | bytes 786464 | tf_op jit(solution)/shard_map/while/body/eval_jaxpr/ppermute | solution.py:17
  516.9 14.3 %collective-permute-done = bf16[512,768]{0,1:T(8,128)(2,1)} collective-permute-done((bf16[512,768]{0,1:T(8,128)(2,1)S(1)}, bf16[512,768]{0,1:T(8,128)(2,1)}, u32[]{:S(2)}, u32[]{:S(2)}) %collective-permute-start) | collective-permute-done | bytes 786464 | tf_op jit(solution)/shard_map/while/body/eval_jaxpr/ppermute | solution.py:17
  531.2 14.9 %collective-permute-done.1 = bf16[512,768]{0,1:T(8,128)(2,1)} collective-permute-done((bf16[512,768]{0,1:T(8,128)(2,1)S(1)}, bf16[512,768]{0,1:T(8,128)(2,1)}, u32[]{:S(2)}, u32[]{:S(2)}) %collective-permute-start.1) | collective-permute-done | bytes 786464 | tf_op jit(solution)/shard_map/while/body/eval_jaxpr/ppermute | solution.py:17
  585.1 15.6 %collective-permute-done.3 = bf16[512,768]{0,1:T(8,128)(2,1)} collective-permute-done((bf16[512,768]{0,1:T(8,128)(2,1)}, bf16[512,768]{0,1:T(8,128)(2,1)}, u32[]{:S(2)}, u32[]{:S(2)}) %collective-permute-start.3) | collective-permute-done | bytes 786464 | tf_op jit(solution)/shard_map/while/body/eval_jaxpr/ppermute | solution.py:17
  603.1 14.4 %collective-permute-done = bf16[512,768]{0,1:T(8,128)(2,1)} collective-permute-done((bf16[512,768]{0,1:T(8,128)(2,1)S(1)}, bf16[512,768]{0,1:T(8,128)(2,1)}, u32[]{:S(2)}, u32[]{:S(2)}) %collective-permute-start) | collective-permute-done | bytes 786464 | tf_op jit(solution)/shard_map/while/body/eval_jaxpr/ppermute | solution.py:17
  617.5 14.1 %collective-permute-done.1 = bf16[512,768]{0,1:T(8,128)(2,1)} collective-permute-done((bf16[512,768]{0,1:T(8,128)(2,1)S(1)}, bf16[512,768]{0,1:T(8,128)(2,1)}, u32[]{:S(2)}, u32[]{:S(2)}) %collective-permute-start.1) | collective-permute-done | bytes 786464 | tf_op jit(solution)/shard_map/while/body/eval_jaxpr/ppermute | solution.py:17
  660.6 8.5 collective-permute-done.2
  670.5 15.6 %collective-permute-done.3 = bf16[512,768]{0,1:T(8,128)(2,1)} collective-permute-done((bf16[512,768]{0,1:T(8,128)(2,1)}, bf16[512,768]{0,1:T(8,128)(2,1)}, u32[]{:S(2)}, u32[]{:S(2)}) %collective-permute-start.3) | collective-permute-done | bytes 786464 | tf_op jit(solution)/shard_map/while/body/eval_jaxpr/ppermute | solution.py:17
  688.6 14.4 %collective-permute-done = bf16[512,768]{0,1:T(8,128)(2,1)} collective-permute-done((bf16[512,768]{0,1:T(8,128)(2,1)S(1)}, bf16[512,768]{0,1:T(8,128)(2,1)}, u32[]{:S(2)}, u32[]{:S(2)}) %collective-permute-start) | collective-permute-done | bytes 786464 | tf_op jit(solution)/shard_map/while/body/eval_jaxpr/ppermute | solution.py:17
  703.0 13.2 %collective-permute-done.1 = bf16[512,768]{0,1:T(8,128)(2,1)} collective-permute-done((bf16[512,768]{0,1:T(8,128)(2,1)S(1)}, bf16[512,768]{0,1:T(8,128)(2,1)}, u32[]{:S(2)}, u32[]{:S(2)}) %collective-permute-start.1) | collective-permute-done | bytes 786464 | tf_op jit(solution)/shard_map/while/body/eval_jaxpr/ppermute | solution.py:17
  744.4 9.3 collective-permute-done.2
  755.1 15.6 %collective-permute-done.3 = bf16[512,768]{0,1:T(8,128)(2,1)} collective-permute-done((bf16[512,768]{0,1:T(8,128)(2,1)}, bf16[512,768]{0,1:T(8,128)(2,1)}, u32[]{:S(2)}, u32[]{:S(2)}) %collective-permute-start.3) | collective-permute-done | bytes 786464 | tf_op jit(solution)/shard_map/while/body/eval_jaxpr/ppermute | solution.py:17
  773.2 14.4 %collective-permute-done = bf16[512,768]{0,1:T(8,128)(2,1)} collective-permute-done((bf16[512,768]{0,1:T(8,128)(2,1)S(1)}, bf16[512,768]{0,1:T(8,128)(2,1)}, u32[]{:S(2)}, u32[]{:S(2)}) %collective-permute-start) | collective-permute-done | bytes 786464 | tf_op jit(solution)/shard_map/while/body/eval_jaxpr/ppermute | solution.py:17
  787.5 12.4 collective-permute-done.1
  828.1 9.3 collective-permute-done.2
  838.8 15.6 %collective-permute-done.3 = bf16[512,768]{0,1:T(8,128)(2,1)} collective-permute-done((bf16[512,768]{0,1:T(8,128)(2,1)}, bf16[512,768]{0,1:T(8,128)(2,1)}, u32[]{:S(2)}, u32[]{:S(2)}) %collective-permute-start.3) | collective-permute-done | bytes 786464 | tf_op jit(solution)/shard_map/while/body/eval_jaxpr/ppermute | solution.py:17
  856.9 14.4 %collective-permute-done = bf16[512,768]{0,1:T(8,128)(2,1)} collective-permute-done((bf16[512,768]{0,1:T(8,128)(2,1)S(1)}, bf16[512,768]{0,1:T(8,128)(2,1)}, u32[]{:S(2)}, u32[]{:S(2)}) %collective-permute-start) | collective-permute-done | bytes 786464 | tf_op jit(solution)/shard_map/while/body/eval_jaxpr/ppermute | solution.py:17
  871.3 11.5 collective-permute-done.1
  911.0 9.3 collective-permute-done.2
  921.7 15.6 %collective-permute-done.3 = bf16[512,768]{0,1:T(8,128)(2,1)} collective-permute-done((bf16[512,768]{0,1:T(8,128)(2,1)}, bf16[512,768]{0,1:T(8,128)(2,1)}, u32[]{:S(2)}, u32[]{:S(2)}) %collective-permute-start.3) | collective-permute-done | bytes 786464 | tf_op jit(solution)/shard_map/while/body/eval_jaxpr/ppermute | solution.py:17
  939.7 14.4 %collective-permute-done = bf16[512,768]{0,1:T(8,128)(2,1)} collective-permute-done((bf16[512,768]{0,1:T(8,128)(2,1)S(1)}, bf16[512,768]{0,1:T(8,128)(2,1)}, u32[]{:S(2)}, u32[]{:S(2)}) %collective-permute-start) | collective-permute-done | bytes 786464 | tf_op jit(solution)/shard_map/while/body/eval_jaxpr/ppermute | solution.py:17
  954.1 10.6 collective-permute-done.1
  993.0 9.3 collective-permute-done.2
  1003.7 15.6 %collective-permute-done.3 = bf16[512,768]{0,1:T(8,128)(2,1)} collective-permute-done((bf16[512,768]{0,1:T(8,128)(2,1)}, bf16[512,768]{0,1:T(8,128)(2,1)}, u32[]{:S(2)}, u32[]{:S(2)}) %collective-permute-start.3) | collective-permute-done | bytes 786464 | tf_op jit(solution)/shard_map/while/body/eval_jaxpr/ppermute | solution.py:17
  1021.8 14.4 %collective-permute-done = bf16[512,768]{0,1:T(8,128)(2,1)} collective-permute-done((bf16[512,768]{0,1:T(8,128)(2,1)S(1)}, bf16[512,768]{0,1:T(8,128)(2,1)}, u32[]{:S(2)}, u32[]{:S(2)}) %collective-permute-start) | collective-permute-done | bytes 786464 | tf_op jit(solution)/shard_map/while/body/eval_jaxpr/ppermute | solution.py:17
  1036.1 9.8 collective-permute-done.1
  1074.2 9.3 collective-permute-done.2
  1084.8 15.6 %collective-permute-done.3 = bf16[512,768]{0,1:T(8,128)(2,1)} collective-permute-done((bf16[512,768]{0,1:T(8,128)(2,1)}, bf16[512,768]{0,1:T(8,128)(2,1)}, u32[]{:S(2)}, u32[]{:S(2)}) %collective-permute-start.3) | collective-permute-done | bytes 786464 | tf_op jit(solution)/shard_map/while/body/eval_jaxpr/ppermute | solution.py:17
  1102.9 14.4 %collective-permute-done = bf16[512,768]{0,1:T(8,128)(2,1)} collective-permute-done((bf16[512,768]{0,1:T(8,128)(2,1)S(1)}, bf16[512,768]{0,1:T(8,128)(2,1)}, u32[]{:S(2)}, u32[]{:S(2)}) %collective-permute-start) | collective-permute-done | bytes 786464 | tf_op jit(solution)/shard_map/while/body/eval_jaxpr/ppermute | solution.py:17
  1117.3 8.9 collective-permute-done.1
  1138.5 37.3 %reduce-scatter.5.cloned.1.call-done = bf16[192,2304]{1,0:T(8,128)(2,1)} async-done(((bf16[768,2304]{1,0:T(8,128)(2,1)}), bf16[192,2304]{1,0:T(8,128)(2,1)}) %reduce-scatter.5.cloned.1.call-update) | async-done | bytes 884752 | tf_op jit(solution)/shard_map/reduce_scatter | solution.py:274
  1188.6 22.7 %all-reduce.6 = (bf16[192]{0:T(256)(128)(2,1)S(1)}, bf16[192]{0:T(256)(128)(2,1)S(1)}) all-reduce(bf16[192]{0:T(256)(128)(2,1)S(1)} %dynamic-slice.3, bf16[192]{0:T(256)(128)(2,1)S(1)} %dynamic-slice.5), channel_id=1, replica_groups=mesh['ctx'=8,'dp'=4] {'ctx'}, use_global_device_ids=true, to_apply=%region_17.18 | all-reduce | flops 384 | bytes 1536 | tf_op jit(solution)/shard_map/psum | solution.py:288
  1218.0 74.8 %all-reduce.12.cloned.1.call-done = (bf16[192,2304]{1,0:T(8,128)(2,1)}, bf16[192,768]{1,0:T(8,128)(2,1)}, bf16[192,2304]{1,0:T(8,128)(2,1)}, bf16[288,768]{1,0:T(8,128)(2,1)}) async-done(((bf16[192,2304]{1,0:T(8,128)(2,1)}, bf16[192,768]{1,0:T(8,128)(2,1)}, bf16[192,2304]{1,0:T(8,128)(2,1)}, bf16[288,768]{1,0:T(8,128)(2,1)}), (bf16[192,2304]{1,0:T(8,128)(2,1)}, bf16[192,768]{1,0:T(8,128)(2,1)}, ...) | async-done | bytes 2506768 | tf_op jit(solution)/shard_map/psum | solution.py:290
  (481 shorter events, 482.6 us)
Async XLA Ops:
  7.2 35.9 %all-gather.7.cloned.1.call-start = ((), (), s32[]{:S(2)}) async-start(), calls=%async_computation.4 | async-start | bytes 4423680 | tf_op jit(solution)/shard_map/all_gather | solution.py:90
  7.9 149.1 %all-gather.9.cloned.1.call-start = ((), (), s32[]{:S(2)}) async-start(), calls=%async_computation.5 | async-start | bytes 7077888 | tf_op jit(solution)/shard_map/all_gather | solution.py:133
  57.3 199.4 %all-gather.11.cloned.1.call-start = ((), (), s32[]{:S(2)}) async-start(), calls=%async_computation.6 | async-start | bytes 7077888 | tf_op jit(solution)/shard_map/all_gather | solution.py:134
  59.9 355.8 %all-gather.13.cloned.1.call-start = ((), (), s32[]{:S(2)}) async-start(), calls=%async_computation.7 | async-start | bytes 1474560 | tf_op jit(solution)/shard_map/all_gather | solution.py:91
  60.5 359.1 %all-gather.15.cloned.1.call-start = ((), (), s32[]{:S(2)}) async-start(), calls=%async_computation.8 | async-start | bytes 4423680 | tf_op jit(solution)/shard_map/all_gather | solution.py:92
  61.1 365.4 %all-gather.17.cloned.1.call-start = ((), (), s32[]{:S(2)}) async-start(), calls=%async_computation.9 | async-start | bytes 2211840 | tf_op jit(solution)/shard_map/all_gather | solution.py:93
  61.6 1076.8 %reduce-scatter.7.cloned.1.call-start = ((), (), s32[]{:S(2)}) async-start(), calls=%async_computation.11 | async-start | bytes 1474560 | tf_op jit(solution)/shard_map/reduce_scatter | solution.py:277
  446.5 692.0 %reduce-scatter.11.cloned.1.call-start = ((), (), s32[]{:S(2)}) async-start(), calls=%async_computation.13 | async-start | bytes 2211840 | tf_op jit(solution)/shard_map/reduce_scatter | solution.py:283
  448.9 689.6 %reduce-scatter.9.cloned.1.call-start = ((), (), s32[]{:S(2)}) async-start(), calls=%async_computation.12 | async-start | bytes 4423680 | tf_op jit(solution)/shard_map/reduce_scatter | solution.py:280
  460.8 715.0 %reduce-scatter.5.cloned.1.call-start = ((), (), s32[]{:S(2)}) async-start(), calls=%async_computation.10 | async-start | bytes 4423680 | tf_op jit(solution)/shard_map/reduce_scatter | solution.py:274
  460.8 665.4 %copy-start.29 = (f32[512,64]{0,1:T(8,128)S(1)}, f32[512,64]{0,1:T(8,128)}, u32[]{:S(2)}) copy-start(f32[512,64]{0,1:T(8,128)} %copy-done.28) | copy-start | bytes 393220
  474.1 23.3 %collective-permute-start.2 = (bf16[512,768]{0,1:T(8,128)(2,1)}, bf16[512,768]{0,1:T(8,128)(2,1)S(1)}, u32[]{:S(2)}, u32[]{:S(2)}) collective-permute-start(bf16[512,768]{0,1:T(8,128)(2,1)} %fusion.151), channel_id=1, source_target_pairs={{0,4},{4,8},{8,12},{12,16},{16,20},{20,24},{24,28},{28,0},{1,5},{5... | collective-permute-start | bytes 2359304 | tf_op jit(solution)/shard_map/while/body/eval_jaxpr/ppermute | solution.py:17
  483.4 31.0 %collective-permute-start.3 = (bf16[512,768]{0,1:T(8,128)(2,1)}, bf16[512,768]{0,1:T(8,128)(2,1)}, u32[]{:S(2)}, u32[]{:S(2)}) collective-permute-start(bf16[512,768]{0,1:T(8,128)(2,1)} %fusion.153), channel_id=1, source_target_pairs={{0,4},{4,8},{8,12},{12,16},{16,20},{20,24},{24,28},{28,0},{1,5},{5... | collective-permute-start | bytes 2359304 | tf_op jit(solution)/shard_map/while/body/eval_jaxpr/ppermute | solution.py:17
  483.4 47.8 %collective-permute-start = (bf16[512,768]{0,1:T(8,128)(2,1)S(1)}, bf16[512,768]{0,1:T(8,128)(2,1)}, u32[]{:S(2)}, u32[]{:S(2)}) collective-permute-start(bf16[512,768]{0,1:T(8,128)(2,1)S(1)} %copy.58), channel_id=1, source_target_pairs={{0,4},{4,8},{8,12},{12,16},{16,20},{20,24},{24,28},{28,0},{1,5},{5... | collective-permute-start | bytes 2359304 | tf_op jit(solution)/shard_map/while/body/eval_jaxpr/ppermute | solution.py:17
  483.4 62.7 %collective-permute-start.1 = (bf16[512,768]{0,1:T(8,128)(2,1)S(1)}, bf16[512,768]{0,1:T(8,128)(2,1)}, u32[]{:S(2)}, u32[]{:S(2)}) collective-permute-start(bf16[512,768]{0,1:T(8,128)(2,1)S(1)} %copy-done.6), channel_id=1, source_target_pairs={{0,4},{4,8},{8,12},{12,16},{16,20},{20,24},{24,28},{28,0},{1,5},{5... | collective-permute-start | bytes 2359304 | tf_op jit(solution)/shard_map/while/body/eval_jaxpr/ppermute | solution.py:17
  498.8 47.4 %copy-start.4 = (bf16[512,12,64]{0,2,1:T(8,128)(2,1)S(1)}, bf16[512,12,64]{0,2,1:T(8,128)(2,1)}, u32[]{:S(2)}) copy-start(bf16[512,12,64]{0,2,1:T(8,128)(2,1)} %copy-done.3) | copy-start | bytes 2359300 | tf_op jit(solution)/shard_map/while
  560.4 23.3 %collective-permute-start.2 = (bf16[512,768]{0,1:T(8,128)(2,1)}, bf16[512,768]{0,1:T(8,128)(2,1)S(1)}, u32[]{:S(2)}, u32[]{:S(2)}) collective-permute-start(bf16[512,768]{0,1:T(8,128)(2,1)} %fusion.151), channel_id=1, source_target_pairs={{0,4},{4,8},{8,12},{12,16},{16,20},{20,24},{24,28},{28,0},{1,5},{5... | collective-permute-start | bytes 2359304 | tf_op jit(solution)/shard_map/while/body/eval_jaxpr/ppermute | solution.py:17
  567.9 32.7 %collective-permute-start.3 = (bf16[512,768]{0,1:T(8,128)(2,1)}, bf16[512,768]{0,1:T(8,128)(2,1)}, u32[]{:S(2)}, u32[]{:S(2)}) collective-permute-start(bf16[512,768]{0,1:T(8,128)(2,1)} %fusion.153), channel_id=1, source_target_pairs={{0,4},{4,8},{8,12},{12,16},{16,20},{20,24},{24,28},{28,0},{1,5},{5... | collective-permute-start | bytes 2359304 | tf_op jit(solution)/shard_map/while/body/eval_jaxpr/ppermute | solution.py:17
  568.8 48.7 %collective-permute-start = (bf16[512,768]{0,1:T(8,128)(2,1)S(1)}, bf16[512,768]{0,1:T(8,128)(2,1)}, u32[]{:S(2)}, u32[]{:S(2)}) collective-permute-start(bf16[512,768]{0,1:T(8,128)(2,1)S(1)} %copy.58), channel_id=1, source_target_pairs={{0,4},{4,8},{8,12},{12,16},{16,20},{20,24},{24,28},{28,0},{1,5},{5... | collective-permute-start | bytes 2359304 | tf_op jit(solution)/shard_map/while/body/eval_jaxpr/ppermute | solution.py:17
  568.9 62.7 %collective-permute-start.1 = (bf16[512,768]{0,1:T(8,128)(2,1)S(1)}, bf16[512,768]{0,1:T(8,128)(2,1)}, u32[]{:S(2)}, u32[]{:S(2)}) collective-permute-start(bf16[512,768]{0,1:T(8,128)(2,1)S(1)} %copy-done.6), channel_id=1, source_target_pairs={{0,4},{4,8},{8,12},{12,16},{16,20},{20,24},{24,28},{28,0},{1,5},{5... | collective-permute-start | bytes 2359304 | tf_op jit(solution)/shard_map/while/body/eval_jaxpr/ppermute | solution.py:17
  585.1 46.5 %copy-start.4 = (bf16[512,12,64]{0,2,1:T(8,128)(2,1)S(1)}, bf16[512,12,64]{0,2,1:T(8,128)(2,1)}, u32[]{:S(2)}) copy-start(bf16[512,12,64]{0,2,1:T(8,128)(2,1)} %copy-done.3) | copy-start | bytes 2359300 | tf_op jit(solution)/shard_map/while
  645.8 23.3 %collective-permute-start.2 = (bf16[512,768]{0,1:T(8,128)(2,1)}, bf16[512,768]{0,1:T(8,128)(2,1)S(1)}, u32[]{:S(2)}, u32[]{:S(2)}) collective-permute-start(bf16[512,768]{0,1:T(8,128)(2,1)} %fusion.151), channel_id=1, source_target_pairs={{0,4},{4,8},{8,12},{12,16},{16,20},{20,24},{24,28},{28,0},{1,5},{5... | collective-permute-start | bytes 2359304 | tf_op jit(solution)/shard_map/while/body/eval_jaxpr/ppermute | solution.py:17
  653.4 32.7 %collective-permute-start.3 = (bf16[512,768]{0,1:T(8,128)(2,1)}, bf16[512,768]{0,1:T(8,128)(2,1)}, u32[]{:S(2)}, u32[]{:S(2)}) collective-permute-start(bf16[512,768]{0,1:T(8,128)(2,1)} %fusion.153), channel_id=1, source_target_pairs={{0,4},{4,8},{8,12},{12,16},{16,20},{20,24},{24,28},{28,0},{1,5},{5... | collective-permute-start | bytes 2359304 | tf_op jit(solution)/shard_map/while/body/eval_jaxpr/ppermute | solution.py:17
  653.7 49.2 %collective-permute-start = (bf16[512,768]{0,1:T(8,128)(2,1)S(1)}, bf16[512,768]{0,1:T(8,128)(2,1)}, u32[]{:S(2)}, u32[]{:S(2)}) collective-permute-start(bf16[512,768]{0,1:T(8,128)(2,1)S(1)} %copy.58), channel_id=1, source_target_pairs={{0,4},{4,8},{8,12},{12,16},{16,20},{20,24},{24,28},{28,0},{1,5},{5... | collective-permute-start | bytes 2359304 | tf_op jit(solution)/shard_map/while/body/eval_jaxpr/ppermute | solution.py:17
  653.9 62.3 %collective-permute-start.1 = (bf16[512,768]{0,1:T(8,128)(2,1)S(1)}, bf16[512,768]{0,1:T(8,128)(2,1)}, u32[]{:S(2)}, u32[]{:S(2)}) collective-permute-start(bf16[512,768]{0,1:T(8,128)(2,1)S(1)} %copy-done.6), channel_id=1, source_target_pairs={{0,4},{4,8},{8,12},{12,16},{16,20},{20,24},{24,28},{28,0},{1,5},{5... | collective-permute-start | bytes 2359304 | tf_op jit(solution)/shard_map/while/body/eval_jaxpr/ppermute | solution.py:17
  670.5 45.7 %copy-start.4 = (bf16[512,12,64]{0,2,1:T(8,128)(2,1)S(1)}, bf16[512,12,64]{0,2,1:T(8,128)(2,1)}, u32[]{:S(2)}) copy-start(bf16[512,12,64]{0,2,1:T(8,128)(2,1)} %copy-done.3) | copy-start | bytes 2359300 | tf_op jit(solution)/shard_map/while
  730.4 23.3 %collective-permute-start.2 = (bf16[512,768]{0,1:T(8,128)(2,1)}, bf16[512,768]{0,1:T(8,128)(2,1)S(1)}, u32[]{:S(2)}, u32[]{:S(2)}) collective-permute-start(bf16[512,768]{0,1:T(8,128)(2,1)} %fusion.151), channel_id=1, source_target_pairs={{0,4},{4,8},{8,12},{12,16},{16,20},{20,24},{24,28},{28,0},{1,5},{5... | collective-permute-start | bytes 2359304 | tf_op jit(solution)/shard_map/while/body/eval_jaxpr/ppermute | solution.py:17
  737.9 32.7 %collective-permute-start.3 = (bf16[512,768]{0,1:T(8,128)(2,1)}, bf16[512,768]{0,1:T(8,128)(2,1)}, u32[]{:S(2)}, u32[]{:S(2)}) collective-permute-start(bf16[512,768]{0,1:T(8,128)(2,1)} %fusion.153), channel_id=1, source_target_pairs={{0,4},{4,8},{8,12},{12,16},{16,20},{20,24},{24,28},{28,0},{1,5},{5... | collective-permute-start | bytes 2359304 | tf_op jit(solution)/shard_map/while/body/eval_jaxpr/ppermute | solution.py:17
  737.9 49.6 %collective-permute-start = (bf16[512,768]{0,1:T(8,128)(2,1)S(1)}, bf16[512,768]{0,1:T(8,128)(2,1)}, u32[]{:S(2)}, u32[]{:S(2)}) collective-permute-start(bf16[512,768]{0,1:T(8,128)(2,1)S(1)} %copy.58), channel_id=1, source_target_pairs={{0,4},{4,8},{8,12},{12,16},{16,20},{20,24},{24,28},{28,0},{1,5},{5... | collective-permute-start | bytes 2359304 | tf_op jit(solution)/shard_map/while/body/eval_jaxpr/ppermute | solution.py:17
  737.9 61.9 %collective-permute-start.1 = (bf16[512,768]{0,1:T(8,128)(2,1)S(1)}, bf16[512,768]{0,1:T(8,128)(2,1)}, u32[]{:S(2)}, u32[]{:S(2)}) collective-permute-start(bf16[512,768]{0,1:T(8,128)(2,1)S(1)} %copy-done.6), channel_id=1, source_target_pairs={{0,4},{4,8},{8,12},{12,16},{16,20},{20,24},{24,28},{28,0},{1,5},{5... | collective-permute-start | bytes 2359304 | tf_op jit(solution)/shard_map/while/body/eval_jaxpr/ppermute | solution.py:17
  755.1 44.8 %copy-start.4 = (bf16[512,12,64]{0,2,1:T(8,128)(2,1)S(1)}, bf16[512,12,64]{0,2,1:T(8,128)(2,1)}, u32[]{:S(2)}) copy-start(bf16[512,12,64]{0,2,1:T(8,128)(2,1)} %copy-done.3) | copy-start | bytes 2359300 | tf_op jit(solution)/shard_map/while
  814.1 23.3 %collective-permute-start.2 = (bf16[512,768]{0,1:T(8,128)(2,1)}, bf16[512,768]{0,1:T(8,128)(2,1)S(1)}, u32[]{:S(2)}, u32[]{:S(2)}) collective-permute-start(bf16[512,768]{0,1:T(8,128)(2,1)} %fusion.151), channel_id=1, source_target_pairs={{0,4},{4,8},{8,12},{12,16},{16,20},{20,24},{24,28},{28,0},{1,5},{5... | collective-permute-start | bytes 2359304 | tf_op jit(solution)/shard_map/while/body/eval_jaxpr/ppermute | solution.py:17
  821.7 32.7 %collective-permute-start.3 = (bf16[512,768]{0,1:T(8,128)(2,1)}, bf16[512,768]{0,1:T(8,128)(2,1)}, u32[]{:S(2)}, u32[]{:S(2)}) collective-permute-start(bf16[512,768]{0,1:T(8,128)(2,1)} %fusion.153), channel_id=1, source_target_pairs={{0,4},{4,8},{8,12},{12,16},{16,20},{20,24},{24,28},{28,0},{1,5},{5... | collective-permute-start | bytes 2359304 | tf_op jit(solution)/shard_map/while/body/eval_jaxpr/ppermute | solution.py:17
  821.7 49.6 %collective-permute-start = (bf16[512,768]{0,1:T(8,128)(2,1)S(1)}, bf16[512,768]{0,1:T(8,128)(2,1)}, u32[]{:S(2)}, u32[]{:S(2)}) collective-permute-start(bf16[512,768]{0,1:T(8,128)(2,1)S(1)} %copy.58), channel_id=1, source_target_pairs={{0,4},{4,8},{8,12},{12,16},{16,20},{20,24},{24,28},{28,0},{1,5},{5... | collective-permute-start | bytes 2359304 | tf_op jit(solution)/shard_map/while/body/eval_jaxpr/ppermute | solution.py:17
  821.7 61.1 %collective-permute-start.1 = (bf16[512,768]{0,1:T(8,128)(2,1)S(1)}, bf16[512,768]{0,1:T(8,128)(2,1)}, u32[]{:S(2)}, u32[]{:S(2)}) collective-permute-start(bf16[512,768]{0,1:T(8,128)(2,1)S(1)} %copy-done.6), channel_id=1, source_target_pairs={{0,4},{4,8},{8,12},{12,16},{16,20},{20,24},{24,28},{28,0},{1,5},{5... | collective-permute-start | bytes 2359304 | tf_op jit(solution)/shard_map/while/body/eval_jaxpr/ppermute | solution.py:17
  897.0 23.3 %collective-permute-start.2 = (bf16[512,768]{0,1:T(8,128)(2,1)}, bf16[512,768]{0,1:T(8,128)(2,1)S(1)}, u32[]{:S(2)}, u32[]{:S(2)}) collective-permute-start(bf16[512,768]{0,1:T(8,128)(2,1)} %fusion.151), channel_id=1, source_target_pairs={{0,4},{4,8},{8,12},{12,16},{16,20},{20,24},{24,28},{28,0},{1,5},{5... | collective-permute-start | bytes 2359304 | tf_op jit(solution)/shard_map/while/body/eval_jaxpr/ppermute | solution.py:17
  904.5 32.7 %collective-permute-start.3 = (bf16[512,768]{0,1:T(8,128)(2,1)}, bf16[512,768]{0,1:T(8,128)(2,1)}, u32[]{:S(2)}, u32[]{:S(2)}) collective-permute-start(bf16[512,768]{0,1:T(8,128)(2,1)} %fusion.153), channel_id=1, source_target_pairs={{0,4},{4,8},{8,12},{12,16},{16,20},{20,24},{24,28},{28,0},{1,5},{5... | collective-permute-start | bytes 2359304 | tf_op jit(solution)/shard_map/while/body/eval_jaxpr/ppermute | solution.py:17
  904.5 49.6 %collective-permute-start = (bf16[512,768]{0,1:T(8,128)(2,1)S(1)}, bf16[512,768]{0,1:T(8,128)(2,1)}, u32[]{:S(2)}, u32[]{:S(2)}) collective-permute-start(bf16[512,768]{0,1:T(8,128)(2,1)S(1)} %copy.58), channel_id=1, source_target_pairs={{0,4},{4,8},{8,12},{12,16},{16,20},{20,24},{24,28},{28,0},{1,5},{5... | collective-permute-start | bytes 2359304 | tf_op jit(solution)/shard_map/while/body/eval_jaxpr/ppermute | solution.py:17
  904.5 60.2 %collective-permute-start.1 = (bf16[512,768]{0,1:T(8,128)(2,1)S(1)}, bf16[512,768]{0,1:T(8,128)(2,1)}, u32[]{:S(2)}, u32[]{:S(2)}) collective-permute-start(bf16[512,768]{0,1:T(8,128)(2,1)S(1)} %copy-done.6), channel_id=1, source_target_pairs={{0,4},{4,8},{8,12},{12,16},{16,20},{20,24},{24,28},{28,0},{1,5},{5... | collective-permute-start | bytes 2359304 | tf_op jit(solution)/shard_map/while/body/eval_jaxpr/ppermute | solution.py:17
  979.0 23.3 %collective-permute-start.2 = (bf16[512,768]{0,1:T(8,128)(2,1)}, bf16[512,768]{0,1:T(8,128)(2,1)S(1)}, u32[]{:S(2)}, u32[]{:S(2)}) collective-permute-start(bf16[512,768]{0,1:T(8,128)(2,1)} %fusion.151), channel_id=1, source_target_pairs={{0,4},{4,8},{8,12},{12,16},{16,20},{20,24},{24,28},{28,0},{1,5},{5... | collective-permute-start | bytes 2359304 | tf_op jit(solution)/shard_map/while/body/eval_jaxpr/ppermute | solution.py:17
  986.5 32.7 %collective-permute-start.3 = (bf16[512,768]{0,1:T(8,128)(2,1)}, bf16[512,768]{0,1:T(8,128)(2,1)}, u32[]{:S(2)}, u32[]{:S(2)}) collective-permute-start(bf16[512,768]{0,1:T(8,128)(2,1)} %fusion.153), channel_id=1, source_target_pairs={{0,4},{4,8},{8,12},{12,16},{16,20},{20,24},{24,28},{28,0},{1,5},{5... | collective-permute-start | bytes 2359304 | tf_op jit(solution)/shard_map/while/body/eval_jaxpr/ppermute | solution.py:17
  986.5 49.6 %collective-permute-start = (bf16[512,768]{0,1:T(8,128)(2,1)S(1)}, bf16[512,768]{0,1:T(8,128)(2,1)}, u32[]{:S(2)}, u32[]{:S(2)}) collective-permute-start(bf16[512,768]{0,1:T(8,128)(2,1)S(1)} %copy.58), channel_id=1, source_target_pairs={{0,4},{4,8},{8,12},{12,16},{16,20},{20,24},{24,28},{28,0},{1,5},{5... | collective-permute-start | bytes 2359304 | tf_op jit(solution)/shard_map/while/body/eval_jaxpr/ppermute | solution.py:17
  986.5 59.4 %collective-permute-start.1 = (bf16[512,768]{0,1:T(8,128)(2,1)S(1)}, bf16[512,768]{0,1:T(8,128)(2,1)}, u32[]{:S(2)}, u32[]{:S(2)}) collective-permute-start(bf16[512,768]{0,1:T(8,128)(2,1)S(1)} %copy-done.6), channel_id=1, source_target_pairs={{0,4},{4,8},{8,12},{12,16},{16,20},{20,24},{24,28},{28,0},{1,5},{5... | collective-permute-start | bytes 2359304 | tf_op jit(solution)/shard_map/while/body/eval_jaxpr/ppermute | solution.py:17
  1060.1 23.3 %collective-permute-start.2 = (bf16[512,768]{0,1:T(8,128)(2,1)}, bf16[512,768]{0,1:T(8,128)(2,1)S(1)}, u32[]{:S(2)}, u32[]{:S(2)}) collective-permute-start(bf16[512,768]{0,1:T(8,128)(2,1)} %fusion.151), channel_id=1, source_target_pairs={{0,4},{4,8},{8,12},{12,16},{16,20},{20,24},{24,28},{28,0},{1,5},{5... | collective-permute-start | bytes 2359304 | tf_op jit(solution)/shard_map/while/body/eval_jaxpr/ppermute | solution.py:17
  1067.7 32.7 %collective-permute-start.3 = (bf16[512,768]{0,1:T(8,128)(2,1)}, bf16[512,768]{0,1:T(8,128)(2,1)}, u32[]{:S(2)}, u32[]{:S(2)}) collective-permute-start(bf16[512,768]{0,1:T(8,128)(2,1)} %fusion.153), channel_id=1, source_target_pairs={{0,4},{4,8},{8,12},{12,16},{16,20},{20,24},{24,28},{28,0},{1,5},{5... | collective-permute-start | bytes 2359304 | tf_op jit(solution)/shard_map/while/body/eval_jaxpr/ppermute | solution.py:17
  1067.7 49.6 %collective-permute-start = (bf16[512,768]{0,1:T(8,128)(2,1)S(1)}, bf16[512,768]{0,1:T(8,128)(2,1)}, u32[]{:S(2)}, u32[]{:S(2)}) collective-permute-start(bf16[512,768]{0,1:T(8,128)(2,1)S(1)} %copy.58), channel_id=1, source_target_pairs={{0,4},{4,8},{8,12},{12,16},{16,20},{20,24},{24,28},{28,0},{1,5},{5... | collective-permute-start | bytes 2359304 | tf_op jit(solution)/shard_map/while/body/eval_jaxpr/ppermute | solution.py:17
  1067.7 58.5 %collective-permute-start.1 = (bf16[512,768]{0,1:T(8,128)(2,1)S(1)}, bf16[512,768]{0,1:T(8,128)(2,1)}, u32[]{:S(2)}, u32[]{:S(2)}) collective-permute-start(bf16[512,768]{0,1:T(8,128)(2,1)S(1)} %copy-done.6), channel_id=1, source_target_pairs={{0,4},{4,8},{8,12},{12,16},{16,20},{20,24},{24,28},{28,0},{1,5},{5... | collective-permute-start | bytes 2359304 | tf_op jit(solution)/shard_map/while/body/eval_jaxpr/ppermute | solution.py:17
  1138.2 154.6 %all-reduce.12.cloned.1.call-start = ((), (), s32[]{:S(2)}) async-start(), calls=%async_computation.14 | async-start | bytes 5013504 | tf_op jit(solution)/shard_map/psum | solution.py:290
  (103 other events, 788.8 us)
Sparse Core Ops, SparseCore 0:
  9.5 33.4 all-gather.6
  57.5 99.4 all-gather.8
  159.0 97.6 all-gather.10
  258.1 15.6 all-gather.12
  275.2 30.7 all-gather.14
  307.4 20.7 all-gather.16
  446.6 23.7 reduce-scatter.6
  473.6 29.1 reduce-scatter.10
  505.4 40.3 reduce-scatter.8
  1138.3 37.4 reduce-scatter.4
  1179.7 113.0 all-reduce.11
where the time goes:
time: 1310 us
  waiting for transfers between devices  720 us (55%)
  matrix products  312 us (24%)
  local copies, waits for them, and re-layouts  107 us (8%)
  other arithmetic  102 us (8%)
  blocking collectives  36.8 us (3%)
  between operations  16.7 us (1%)
    ppermute x32, waiting for transfers between devices, passed_along(): return lax.ppermute(x, axis, [(i, (i + by) % count) for i in range(count)])  402 us
    all_gather x1, waiting for transfers between devices, body(): lax.all_gather(keys_local, 'ctx', axis=0, tiled=True)  94.7 us
    all_gather x1, waiting for transfers between devices, body(): lax.all_gather(values_local, 'ctx', axis=0, tiled=True)  87.9 us
    psum x1, waiting for transfers between devices, body(): lax.psum(summed[2].astype(jnp.bfloat16), 'ctx').astype(jnp.float32)  74.8 us
    dot_general x8, matrix products, attend(): jnp.einsum('qhd,khd->hqk', queries, key_part, preferred_element_type=jnp....  59.3 us
    while x152, local copies, waits for them, and re-layouts  56.3 us
    dot_general x8, matrix products, attend(): jnp.einsum('hqk,khd->qhd', weights.astype(jnp.bfloat16), value_part, pref...  50.9 us
    dot_general x8, matrix products, backward_block(): jnp.einsum('hqk,khd->qhd', score_grad, key_part, preferred_element_type=j...  50.8 us
  transfers between devices with their start and end apart: 43, of which 37 were waited for; matrix products, arithmetic and copies ran while one was open for 33% of the time, Pallas kernels for 0%

commit v1 on v0

v1 whole, which is shorter than its diff:
```python
import functools

import jax
import jax.numpy as jnp
from jax import lax
from jax.experimental import pallas as pl
from jax.experimental.pallas import tpu as pltpu
from jax.sharding import PartitionSpec as P

HEADS = 12
HEAD_DIM = 64
FF = 1152
GROUPS = 4
CHUNKS = HEADS // GROUPS

rope_base = 160000.0
norm_eps = 1e-05


def layer_norm(values, gain):
    center = values - jnp.mean(values, axis=-1, keepdims=True)
    spread = jnp.mean(center * center, axis=-1, keepdims=True)
    return center * lax.rsqrt(spread + norm_eps) * gain


def norm_back(values, gain, upstream):
    _, pull = jax.vjp(layer_norm, values, gain)
    return pull(upstream)


def geglu(packed, hidden_size):
    return jax.nn.gelu(packed[:, :hidden_size], approximate=False) * packed[:, hidden_size:]


def product(left, right, left_dim=1, right_dim=0):
    return lax.dot_general(
        left, right, (((left_dim,), (right_dim,)), ((), ())), preferred_element_type=jnp.float32
    )


def rotate(values, cosine, sine):
    low_half, high_half = values[..., :32, :], values[..., 32:, :]
    return jnp.concatenate(
        [low_half * cosine - high_half * sine, high_half * cosine + low_half * sine], axis=-2
    )


def unrotate(values, cosine, sine):
    low_half, high_half = values[..., :32, :], values[..., 32:, :]
    return jnp.concatenate(
        [low_half * cosine + high_half * sine, high_half * cosine - low_half * sine], axis=-2
    )


def forward_kernel(m, own, *rest):
    others = rest[: m - 1]
    out, low, total, keys = rest[m - 1 :]
    n, _, d, t = own.shape
    parts = [(own, s, 1, 2) for s in range(n)] + [(r, s, 0, 1) for r in others for s in range(n)]
    for i, (ref, s, key_at, _) in enumerate(parts):
        keys[i] = ref[s, key_at].T

    def step(j, _):
        query = own[j, 0]
        top = jnp.full((1, t), -1e30, jnp.float32)
        sums = jnp.zeros((1, t), jnp.float32)
        acc = jnp.zeros((d, t), jnp.float32)
        for i, (ref, s, _, value_at) in enumerate(parts):
            scores = product(keys[i], query)
            new = jnp.maximum(top, jnp.max(scores, axis=0, keepdims=True))
            weights = jnp.exp(scores - new)
            rescale = jnp.exp(top - new)
            sums = sums * rescale + jnp.sum(weights, axis=0, keepdims=True)
            acc = acc * rescale + product(ref[s, value_at], weights.astype(jnp.bfloat16))
            top = new
        done = acc / sums
        out[j] = done
        low[j] = done.astype(jnp.bfloat16)
        total[j] = top + jnp.log(sums)
        return 0

    lax.fori_loop(0, n, step, 0)


def attend(own, others):
    n, _, d, t = own.shape
    m = 1 + len(others)
    pairs = n * t * m * n * t
    return pl.pallas_call(
        functools.partial(forward_kernel, m),
        out_shape=(
            jax.ShapeDtypeStruct((n, d, t), jnp.float32),
            jax.ShapeDtypeStruct((n, d, t), jnp.bfloat16),
            jax.ShapeDtypeStruct((n, 1, t), jnp.float32),
        ),
        scratch_shapes=[pltpu.VMEM((m * n, t, d), jnp.bfloat16)],
        cost_estimate=pl.CostEstimate(
            flops=4 * 4 * d * pairs, transcendentals=pairs, bytes_accessed=2 * 10**6
        ),
        name="attend",
    )(own, *others)


def backward_kernel(m, own, *rest):
    others = rest[: m - 1]
    upstream, out, total, query_grad, *more = rest[m - 1 :]
    grads = more[:m]
    acc, query_rows, upstream_rows, delta = more[m:]
    n, _, d, t = own.shape
    for s in range(n):
        query_rows[s] = own[s, 0].T
        upstream_rows[s] = upstream[s].T
        delta[s] = jnp.sum(upstream[s].astype(jnp.float32) * out[s], axis=0, keepdims=True)
        acc[s] = jnp.zeros((d, t), jnp.float32)
    places = [(1, 2)] + [(0, 1)] * (m - 1)
    for ref, (key_at, value_at), grad in zip((own,) + tuple(others), places, grads):

        def step(s, _):
            keys = ref[s, key_at]
            key_rows = keys.T
            value_rows = ref[s, value_at].T
            key_grad = jnp.zeros((t, d), jnp.float32)
            value_grad = jnp.zeros((t, d), jnp.float32)
            for j in range(n):
                probs = jnp.exp(product(key_rows, own[j, 0]) - total[j])
                prob_grad = product(value_rows, upstream[j])
                score_grad = (probs * (prob_grad - delta[j])).astype(jnp.bfloat16)
                value_grad = value_grad + product(probs.astype(jnp.bfloat16), upstream_rows[j])
                key_grad = key_grad + product(score_grad, query_rows[j])
                acc[j] += product(keys, score_grad)
            grad[s, 0] = key_grad.T.astype(jnp.bfloat16)
            grad[s, 1] = value_grad.T.astype(jnp.bfloat16)
            return 0

        lax.fori_loop(0, n, step, 0)
    for s in range(n):
        query_grad[s] = (acc[s] * d**-0.5).astype(jnp.bfloat16)


def attend_back(own, others, upstream, out, total):
    n, _, d, t = own.shape
    m = 1 + len(others)
    pairs = n * t * m * n * t
    return pl.pallas_call(
        functools.partial(backward_kernel, m),
        out_shape=(jax.ShapeDtypeStruct((n, d, t), jnp.bfloat16),)
        + tuple(jax.ShapeDtypeStruct((n, 2, d, t), jnp.bfloat16) for _ in range(m)),
        scratch_shapes=[
            pltpu.VMEM((n, d, t), jnp.float32),
            pltpu.VMEM((n, t, d), jnp.bfloat16),
            pltpu.VMEM((n, t, d), jnp.bfloat16),
            pltpu.VMEM((n, 1, t), jnp.float32),
        ],
        cost_estimate=pl.CostEstimate(
            flops=10 * 4 * d * pairs, transcendentals=pairs, bytes_accessed=4 * 10**6
        ),
        name="attend_back",
    )(own, *others, upstream, out, total)


def exchange(values):
    count = lax.axis_size("ctx") // GROUPS
    groups = [[g * count + y for g in range(GROUPS)] for y in range(count)]
    return lax.all_to_all(values, "ctx", 0, 0, axis_index_groups=groups)


def across(values, by):
    count = lax.axis_size("ctx") // GROUPS
    pairs = [
        (g * count + y, g * count + (y + by) % count) for g in range(GROUPS) for y in range(count)
    ]
    return lax.ppermute(values, "ctx", pairs)


def gathered(value):
    return lax.all_gather(value, "dp", axis=0, tiled=True)


def reduced(value):
    part = lax.psum_scatter(value.astype(jnp.bfloat16), "dp", scatter_dimension=0, tiled=True)
    return lax.psum(part, "ctx").astype(jnp.float32)


def body(tokens, cotangent, attn_gain, mlp_gain, w_qkv, w_out, w_in, w_mlp_out, block_offsets):
    width = HEADS * HEAD_DIM
    part = GROUPS * HEAD_DIM
    inputs = tokens[0].astype(jnp.float32)
    t = inputs.shape[0]
    m = lax.axis_size("ctx") // GROUPS
    positions = (block_offsets[0, 0] + jnp.arange(t, dtype=jnp.int32)).astype(jnp.float32)
    half = HEAD_DIM // 2
    frequency = rope_base ** (-jnp.arange(half, dtype=jnp.float32) / half)
    angles = frequency[:, None] * positions[None, :]
    cosine, sine = jnp.cos(angles), jnp.sin(angles)

    gains = lax.all_gather(jnp.stack([attn_gain, mlp_gain]), "dp", axis=1, tiled=True)
    local_qkv = w_qkv.reshape(-1, 3, CHUNKS, part)
    weights_qkv = [gathered(local_qkv[:, :, i].reshape(-1, 3 * part)) for i in range(CHUNKS)]
    weight_out, weight_in, weight_down = gathered(w_out), gathered(w_in), gathered(w_mlp_out)
    first_gain = gains[0].astype(jnp.float32)
    second_gain = gains[1].astype(jnp.float32)

    normed = layer_norm(inputs, first_gain).astype(jnp.bfloat16)
    kept, lows = [], []
    for i in range(CHUNKS):
        packed = product(weights_qkv[i], normed, 0, 1).reshape(3, GROUPS, HEAD_DIM, t)
        queries = rotate(packed[0], cosine, sine).astype(jnp.bfloat16) * HEAD_DIM**-0.5
        keys = rotate(packed[1], cosine, sine).astype(jnp.bfloat16)
        values = packed[2].astype(jnp.bfloat16)
        own = exchange(jnp.stack([queries, keys, values], axis=1))
        others = [across(own[:, 1:], by) for by in range(1, m)]
        out, low, total = attend(own, others)
        lows.append(exchange(low).reshape(part, t))
        kept.append((own, others, out, total))
    attended = jnp.concatenate(lows, axis=0)

    residual = inputs + product(attended, weight_out, 0, 0)
    mlp_normed = layer_norm(residual, second_gain).astype(jnp.bfloat16)
    up_gate = product(mlp_normed, weight_in)
    joined = geglu(up_gate, FF).astype(jnp.bfloat16)
    mixed = (residual + product(joined, weight_down)).astype(jnp.bfloat16)[None]

    upstream_low = cotangent[0]
    upstream = upstream_low.astype(jnp.float32)
    grad_joined = product(upstream_low, weight_down, 1, 1)
    _, glu_pull = jax.vjp(lambda packed_in: geglu(packed_in, FF), up_gate)
    grad_up_gate = glu_pull(grad_joined)[0].astype(jnp.bfloat16)
    grad_mlp_normed = product(grad_up_gate, weight_in, 1, 1)
    grad_residual_norm, grad_gain_two = norm_back(residual, second_gain, grad_mlp_normed)
    grad_residual = upstream + grad_residual_norm
    residual_low = grad_residual.astype(jnp.bfloat16)
    grad_attended = (
        product(weight_out, residual_low, 1, 1)
        .astype(jnp.bfloat16)
        .reshape(CHUNKS, GROUPS, HEAD_DIM, t)
    )
    total_down = reduced(product(joined, upstream_low, 0, 0))
    total_in = reduced(product(mlp_normed, grad_up_gate, 0, 0))
    total_out = reduced(product(attended, residual_low, 1, 0))

    grad_normed = 0.0
    totals_qkv = []
    for i in range(CHUNKS):
        own, others, out, total = kept[i]
        query_grad, own_grad, *other_grads = attend_back(
            own, others, exchange(grad_attended[i]), out, total
        )
        sums = own_grad.astype(jnp.float32)
        for by, grad in zip(range(1, m), other_grads):
            sums = sums + across(grad, -by).astype(jnp.float32)
        back = exchange(
            jnp.concatenate([query_grad[:, None], sums.astype(jnp.bfloat16)], axis=1)
        ).astype(jnp.float32)
        grad_packed = (
            jnp.stack(
                [
                    unrotate(back[:, 0], cosine, sine),
                    unrotate(back[:, 1], cosine, sine),
                    back[:, 2],
                ]
            )
            .astype(jnp.bfloat16)
            .reshape(3 * part, t)
        )
        totals_qkv.append(reduced(product(normed, grad_packed, 0, 1)).reshape(-1, 3, 1, part))
        grad_normed = grad_normed + product(grad_packed, weights_qkv[i], 0, 1)
    total_qkv = jnp.concatenate(totals_qkv, axis=2).reshape(-1, 3 * width)
    grad_inputs_norm, grad_gain_one = norm_back(inputs, first_gain, grad_normed)
    tokens_grad = (grad_residual + grad_inputs_norm)[None]

    gain_rows = attn_gain.shape[0]
    gain_sums = lax.psum(jnp.stack([grad_gain_one, grad_gain_two]), ("ctx", "dp"))
    gain_sums = lax.dynamic_slice_in_dim(gain_sums, lax.axis_index("dp") * gain_rows, gain_rows, 1)
    return (
        mixed,
        tokens_grad,
        gain_sums[0],
        gain_sums[1],
        total_qkv,
        total_out,
        total_in,
        total_down,
    )


def solution(mesh):
    return jax.shard_map(
        body,
        mesh=mesh,
        in_specs=(
            P("dp", "ctx", None),
            P("dp", "ctx", None),
            P("dp"),
            P("dp"),
            P("dp", None),
            P("dp", None),
            P("dp", None),
            P("dp", None),
            P("dp", "ctx"),
        ),
        out_specs=(
            P("dp", "ctx", None),
            P("dp", "ctx", None),
            P("dp"),
            P("dp"),
            P("dp", None),
            P("dp", None),
            P("dp", None),
            P("dp", None),
        ),
        check_vma=False,
    )
```

time: 1310 us -> 737 us (0.56)
  waiting for transfers between devices: 720 us -> 331 us
  matrix products: 312 us -> 52.5 us
  Pallas kernels: 0 us -> 130 us
  other arithmetic: 102 us -> 31.8 us
  local copies, waits for them, and re-layouts: 107 us -> 51 us
  starting transfers between devices: 9.82 us -> 55.5 us
  blocking collectives: 36.8 us -> 58.4 us
    ppermute x32 -> x6, waiting for transfers between devices: 402 us -> 16.4 us  [across(): return lax.ppermute(values, 'ctx', pairs)]
    dot_general x68 -> x18, matrix products: 312 us -> 52.5 us  [product(): lax.dot_general(left, right, (((left_dim,), (right_dim,)), ((), ())), pre...]
    all_gather x6, waiting for transfers between devices: 204 us -> 25.7 us  [gathered(): return lax.all_gather(value, 'dp', axis=0, tiled=True)]
    pallas_call x0 -> x6, Pallas kernels: none -> 130 us  [the longest x3 75.5 us: attend_back(): pl.pallas_call(functools.partial(backward_kernel, m), out_shape=(jax.Shap...]
    reduce_scatter x4 -> x6, waiting for transfers between devices: 37.3 us -> 154 us  [reduced(): lax.psum_scatter(value.astype(jnp.bfloat16), 'dp', scatter_dimension=0, t...]
    all_to_all x0 -> x11, waiting for transfers between devices: none -> 69.7 us  [exchange(): return lax.all_to_all(values, 'ctx', 0, 0, axis_index_groups=groups)]
    convert_element_type x44 -> x13, other arithmetic: 71.2 us -> 12.1 us  [the longest x3 3.99 us: body(): back = exchange(jnp.concatenate([query_grad[:, None], sums.astype(jnp.bfl...]
    while x152 -> x0, local copies, waits for them, and re-layouts: 56.3 us -> none
  transfers between devices with their start and end apart: 43 -> 30, of which waited for: 37 -> 17; matrix products, arithmetic and copies ran while one was open for 33% -> 12% of each run, Pallas kernels for 0% -> 14%
where the time goes in v1:
time: 737 us; the launch traced here: 726 us
  waiting for transfers between devices  331 us (45%)
  Pallas kernels  130 us (18%)
  blocking collectives  58.4 us (8%)
  starting transfers between devices  55.5 us (8%)
  matrix products  52.5 us (7%)
  local copies, waits for them, and re-layouts  51 us (7%)
  other arithmetic  31.8 us (4%)
  between operations  16 us (2%)
    reduce_scatter x6, waiting for transfers between devices, reduced(): lax.psum_scatter(value.astype(jnp.bfloat16), 'dp', scatter_dimension=0, t...  154 us
    pallas_call x3, Pallas kernels, attend_back(): pl.pallas_call(functools.partial(backward_kernel, m), out_shape=(jax.Shap...  75.5 us
    all_to_all x11, waiting for transfers between devices, exchange(): return lax.all_to_all(values, 'ctx', 0, 0, axis_index_groups=groups)  69.7 us
    psum x1, waiting for transfers between devices, reduced(): return lax.psum(part, 'ctx').astype(jnp.float32)  64.3 us
    pallas_call x3, Pallas kernels, attend(): pl.pallas_call(functools.partial(forward_kernel, m), out_shape=(jax.Shape...  54.2 us
    dot_general x18, matrix products, product(): lax.dot_general(left, right, (((left_dim,), (right_dim,)), ((), ())), pre...  52.5 us
    all_to_all x11, starting transfers between devices, exchange(): return lax.all_to_all(values, 'ctx', 0, 0, axis_index_groups=groups)  47.7 us
    psum x1, blocking collectives, body(): lax.psum(jnp.stack([grad_gain_one, grad_gain_two]), ('ctx', 'dp'))  41.7 us
  transfers between devices with their start and end apart: 30, of which 17 were waited for; matrix products, arithmetic and copies ran while one was open for 12% of the time, Pallas kernels for 14%

profile of v1, /device:TPU:0, one launch (start us, length us, event | category | flops | bytes accessed | tf_op | source)
XLA Modules:
  0.0 726.3 jit_solution(9220013622666057164)
XLA Ops:
  9.4 4.2 slice_reduce_fusion.2
  17.9 6.0 all-gather
  25.0 9.7 %all-gather.10.cloned.1.call-done = bf16[768,768]{1,0:T(8,128)(2,1)} async-done(((bf16[192,768]{1,0:T(8,128)(2,1)}), bf16[768,768]{1,0:T(8,128)(2,1)}) %all-gather.10.cloned.1.call-update) | async-done | bytes 1179664 | tf_op jit(solution)/shard_map/all_gather | solution.py:176
  38.4 15.9 %all-gather.8.cloned.1.call-done = bf16[768,768]{1,0:T(8,128)(2,1)} async-done(((bf16[192,768]{1,0:T(8,128)(2,1)}), bf16[768,768]{1,0:T(8,128)(2,1)}) %all-gather.8.cloned.1.call-update) | async-done | bytes 1179664 | tf_op jit(solution)/shard_map/all_gather | solution.py:176
  60.9 4.7 all-to-all-start
  67.9 18.2 %all-to-all-done.own = bf16[4,3,64,512]{3,2,1,0:T(8,128)(2,1)S(1)} async-done(((bf16[4,3,64,512]{3,2,1,0:T(8,128)(2,1)}), bf16[4,3,64,512]{3,2,1,0:T(8,128)(2,1)S(1)}, u32[]{:S(2)}, u32[]{:S(2)}) %all-to-all-start) | async-done | bytes 786464 | tf_op jit(solution)/shard_map/all_to_all | solution.py:164
  86.1 3.5 all-to-all-start.2
  98.5 10.8 %all-to-all-done.2.own = bf16[4,3,64,512]{3,2,1,0:T(8,128)(2,1)S(1)} async-done(((bf16[4,3,64,512]{3,2,1,0:T(8,128)(2,1)}), bf16[4,3,64,512]{3,2,1,0:T(8,128)(2,1)S(1)}, u32[]{:S(2)}, u32[]{:S(2)}) %all-to-all-start.2) | async-done | bytes 786464 | tf_op jit(solution)/shard_map/all_to_all | solution.py:164
  109.3 3.5 all-to-all-start.4
  116.1 16.3 %all-to-all-done.4.own = bf16[4,3,64,512]{3,2,1,0:T(8,128)(2,1)S(1)} async-done(((bf16[4,3,64,512]{3,2,1,0:T(8,128)(2,1)}), bf16[4,3,64,512]{3,2,1,0:T(8,128)(2,1)S(1)}, u32[]{:S(2)}, u32[]{:S(2)}) %all-to-all-start.4) | async-done | bytes 786464 | tf_op jit(solution)/shard_map/all_to_all | solution.py:164
  134.8 18.1 %attend.3 = (f32[4,64,512]{2,1,0:T(8,128)}, bf16[4,64,512]{2,1,0:T(8,128)(2,1)}, f32[4,1,512]{2,1,0:T(1,128)}) custom-call(bf16[4,3,64,512]{3,2,1,0:T(8,128)(2,1)} %copy-done.11, bf16[4,2,64,512]{3,2,1,0:T(8,128)(2,1)} %copy-done.56), custom_call_target="tpu_custom_call" | custom-call | flops 8589934592 | bytes 2000000 | tf_op jit(solution)/shard_map/attend/pallas_call | solution.py:89
  152.9 3.4 all-to-all-start.1
  156.3 18.0 %attend.4 = (f32[4,64,512]{2,1,0:T(8,128)}, bf16[4,64,512]{2,1,0:T(8,128)(2,1)}, f32[4,1,512]{2,1,0:T(1,128)}) custom-call(bf16[4,3,64,512]{3,2,1,0:T(8,128)(2,1)} %copy-done.9, bf16[4,2,64,512]{3,2,1,0:T(8,128)(2,1)} %collective-permute-done.1.rest_0_), custom_call_target="tpu_custom_call" | custom-call | flops 8589934592 | bytes 2000000 | tf_op jit(solution)/shard_map/attend/pallas_call | solution.py:89
  174.3 5.1 all-to-all-start.3
  179.4 18.1 %attend.5 = (f32[4,64,512]{2,1,0:T(8,128)}, bf16[4,64,512]{2,1,0:T(8,128)(2,1)}, f32[4,1,512]{2,1,0:T(1,128)}) custom-call(bf16[4,3,64,512]{3,2,1,0:T(8,128)(2,1)} %copy-done.10, bf16[4,2,64,512]{3,2,1,0:T(8,128)(2,1)} %collective-permute-done.2.rest_0_), custom_call_target="tpu_custom_call" | custom-call | flops 8589934592 | bytes 2000000 | tf_op jit(solution)/shard_map/attend/pallas_call | solution.py:89
  197.5 5.5 all-to-all-start.5
  203.0 6.7 all-to-all-done.5
  209.7 2.3 fusion.67
  212.4 6.3 fusion.53
  218.7 7.6 %fusion.29 = (f32[512,1152]{1,0:T(8,128)S(1)}, f32[512,1152]{1,0:T(8,128)S(1)}, f32[512,1152]{1,0:T(8,128)S(1)}) fusion(f32[512,2304]{1,0:T(8,128)} %fusion.53, bf16[1152,768]{1,0:T(8,128)(2,1)} %all-gather.18.cloned.1.call-done, bf16[1,512,768]{2,1,0:T(8,128)(2,1)S(1)} %copy-done.5), kind=kOutput, calls=%fused_computation.82 | convolution fusion | flops 944308224 | bytes 11993088 | tf_op jit(solution)/shard_map/dot_general | solution.py:36
  229.9 2.8 multiply_reduce_fusion
  238.1 10.6 %all_to_all.60.rest_1_ = bf16[4,64,512]{2,1,0:T(8,128)(2,1)} all-to-all(bf16[4,64,512]{2,1,0:T(8,128)(2,1)S(1)} %bitcast.193), channel_id=1, replica_groups={{0,8,16,24},{4,12,20,28},{1,9,17,25},{5,13,21,29},{2,10,18,26},{6,14,22..., dimensions={0} | all-to-all | bytes 524288 | tf_op jit(solution)/shard_map/all_to_all | solution.py:164
  248.8 25.2 %attend_back.3 = (bf16[4,64,512]{2,1,0:T(8,128)(2,1)}, bf16[4,2,64,512]{3,2,1,0:T(8,128)(2,1)}, bf16[4,2,64,512]{3,2,1,0:T(8,128)(2,1)}) custom-call(bf16[4,3,64,512]{3,2,1,0:T(8,128)(2,1)} %copy-done.11, bf16[4,2,64,512]{3,2,1,0:T(8,128)(2,1)} %copy-done.56, bf16[4,64,512]{2,1,0:T(8,128)(2,1)} %all_to_all.60.rest_1_, ...), custom_call_target="tpu_custom_call" | custom-call | flops 21474836480 | bytes 4000000 | tf_op jit(solution)/shard_map/attend_back/pallas_call | solution.py:144
  276.6 4.0 all-to-all-start.8
  281.5 6.0 all-to-all-done.8.rest_1_
  287.5 3.4 all-to-all-start.10
  293.3 4.5 all-to-all-done.10.rest_1_
  297.7 4.2 all-to-all-start.7
  301.9 25.1 %attend_back.4 = (bf16[4,64,512]{2,1,0:T(8,128)(2,1)}, bf16[4,2,64,512]{3,2,1,0:T(8,128)(2,1)}, bf16[4,2,64,512]{3,2,1,0:T(8,128)(2,1)}) custom-call(bf16[4,3,64,512]{3,2,1,0:T(8,128)(2,1)} %copy-done.9, bf16[4,2,64,512]{3,2,1,0:T(8,128)(2,1)} %collective-permute-done.1.rest_0_, bf16[4,64,512]{2,1,0:T(8,128)(2,1)} %all-to-all-done.8.rest_1_, ...), custom_call_target="tpu_custom_call" | custom-call | flops 21474836480 | bytes 4000000 | tf_op jit(solution)/shard_map/attend_back/pallas_call | solution.py:144
  328.3 8.2 %collective-permute-done.4 = bf16[4,2,64,512]{3,2,1,0:T(8,128)(2,1)S(1)} collective-permute-done((bf16[4,2,64,512]{3,2,1,0:T(8,128)(2,1)}, bf16[4,2,64,512]{3,2,1,0:T(8,128)(2,1)S(1)}, u32[]{:S(2)}, u32[]{:S(2)}) %collective-permute-start.4) | collective-permute-done | bytes 524320 | tf_op jit(solution)/shard_map/ppermute | solution.py:172
  338.7 5.3 all-to-all-start.9
  343.9 25.1 %attend_back.5 = (bf16[4,64,512]{2,1,0:T(8,128)(2,1)}, bf16[4,2,64,512]{3,2,1,0:T(8,128)(2,1)}, bf16[4,2,64,512]{3,2,1,0:T(8,128)(2,1)}) custom-call(bf16[4,3,64,512]{3,2,1,0:T(8,128)(2,1)} %copy-done.10, bf16[4,2,64,512]{3,2,1,0:T(8,128)(2,1)} %collective-permute-done.2.rest_0_, bf16[4,64,512]{2,1,0:T(8,128)(2,1)} %copy-done.39, ...), custom_call_target="tpu_custom_call" | custom-call | flops 21474836480 | bytes 4000000 | tf_op jit(solution)/shard_map/attend_back/pallas_call | solution.py:144
  370.3 8.2 %collective-permute-done.5 = bf16[4,2,64,512]{3,2,1,0:T(8,128)(2,1)S(1)} collective-permute-done((bf16[4,2,64,512]{3,2,1,0:T(8,128)(2,1)}, bf16[4,2,64,512]{3,2,1,0:T(8,128)(2,1)S(1)}, u32[]{:S(2)}, u32[]{:S(2)}) %collective-permute-start.5) | collective-permute-done | bytes 524320 | tf_op jit(solution)/shard_map/ppermute | solution.py:172
  380.6 5.1 all-to-all-start.11
  391.7 7.2 all-to-all-done.11
  418.6 3.2 convolution_convert_fusion.2
  421.8 3.7 convolution_convert_fusion.1
  426.2 6.3 convolution_convert_fusion
  434.5 25.7 %reduce-scatter.7.cloned.1.call-done = bf16[192,768]{1,0:T(8,128)(2,1)} async-done(((bf16[768,768]{1,0:T(8,128)(2,1)}), bf16[192,768]{1,0:T(8,128)(2,1)}) %reduce-scatter.7.cloned.1.call-update) | async-done | bytes 294928 | tf_op jit(solution)/shard_map/reduce_scatter | solution.py:180
  462.0 27.0 %reduce-scatter.11.cloned.1.call-done = bf16[192,768]{1,0:T(8,128)(2,1)} async-done(((bf16[768,768]{1,0:T(8,128)(2,1)}), bf16[192,768]{1,0:T(8,128)(2,1)}) %reduce-scatter.11.cloned.1.call-update) | async-done | bytes 294928 | tf_op jit(solution)/shard_map/reduce_scatter | solution.py:180
  490.8 26.2 %reduce-scatter.13.cloned.1.call-done = bf16[192,768]{1,0:T(8,128)(2,1)} async-done(((bf16[768,768]{1,0:T(8,128)(2,1)}), bf16[192,768]{1,0:T(8,128)(2,1)}) %reduce-scatter.13.cloned.1.call-update) | async-done | bytes 294928 | tf_op jit(solution)/shard_map/reduce_scatter | solution.py:180
  517.0 32.4 %reduce-scatter.17.cloned.1.call-done = bf16[288,768]{1,0:T(8,128)(2,1)} async-done(((bf16[1152,768]{1,0:T(8,128)(2,1)}), bf16[288,768]{1,0:T(8,128)(2,1)}) %reduce-scatter.17.cloned.1.call-update) | async-done | bytes 442384 | tf_op jit(solution)/shard_map/reduce_scatter | solution.py:180
  549.4 42.8 %reduce-scatter.15.cloned.1.call-done = bf16[192,2304]{1,0:T(8,128)(2,1)} async-done(((bf16[768,2304]{1,0:T(8,128)(2,1)}), bf16[192,2304]{1,0:T(8,128)(2,1)}) %reduce-scatter.15.cloned.1.call-update) | async-done | bytes 884752 | tf_op jit(solution)/shard_map/reduce_scatter | solution.py:180
  592.3 4.0 fusion.22
  601.4 41.7 %psum.49 = f32[2,768]{1,0:T(2,128)S(1)} all-reduce(f32[2,768]{1,0:T(2,128)S(1)} %pad_maximum_fusion.9), channel_id=1, replica_groups=mesh['ctx'=8,'dp'=4] {'ctx','dp'}, use_global_device_ids=true, to_apply=%region_10.0 | all-reduce | flops 1536 | bytes 12288 | tf_op jit(solution)/shard_map/psum | solution.py:272
  643.7 3.2 add_bitcast_fusion
  647.0 64.3 %all-reduce.5.cloned.1.call-done = (bf16[192,3,1,256]{3,0,2,1:T(8,128)(2,1)}, bf16[192,3,1,256]{3,0,2,1:T(8,128)(2,1)}, bf16[192,3,1,256]{3,0,2,1:T(8,128)(2,1)}...) async-done(((bf16[192,3,1,256]{3,0,2,1:T(8,128)(2,1)}, bf16[192,3,1,256]{3,0,2,1:T(8,128)(2,1)}, bf16[192,3,1,256]{3,0,2,1:T(8,128)(2,1)}, ...) | async-done | bytes 2506768 | tf_op jit(solution)/shard_map/psum | solution.py:181
  713.8 2.5 reshape.534
  (273 shorter events, 98.4 us)
Async XLA Ops:
  7.2 27.5 %all-gather.10.cloned.1.call-start = ((), (), s32[]{:S(2)}) async-start(), calls=%async_computation.19 | async-start | bytes 1474560 | tf_op jit(solution)/shard_map/all_gather | solution.py:176
  14.4 39.9 %all-gather.8.cloned.1.call-start = ((), (), s32[]{:S(2)}) async-start(), calls=%async_computation.18 | async-start | bytes 1474560 | tf_op jit(solution)/shard_map/all_gather | solution.py:176
  15.2 74.4 %all-gather.12.cloned.1.call-start = ((), (), s32[]{:S(2)}) async-start(), calls=%async_computation.20 | async-start | bytes 1474560 | tf_op jit(solution)/shard_map/all_gather | solution.py:176
  16.1 186.9 %all-gather.14.cloned.1.call-start = ((), (), s32[]{:S(2)}) async-start(), calls=%async_computation.21 | async-start | bytes 1474560 | tf_op jit(solution)/shard_map/all_gather | solution.py:176
  16.6 195.7 %all-gather.16.cloned.1.call-start = ((), (), s32[]{:S(2)}) async-start(), calls=%async_computation.22 | async-start | bytes 4423680 | tf_op jit(solution)/shard_map/all_gather | solution.py:176
  17.8 19.0 %copy-start.45 = (f32[512]{0:T(512)}, f32[512]{0:T(512)S(1)}, u32[]{:S(2)}) copy-start(f32[512]{0:T(512)S(1)} %fusion.17) | copy-start | bytes 6148
  25.0 207.7 %copy-start.47 = (f32[768]{0:T(1024)}, f32[768]{0:T(1024)S(1)}, u32[]{:S(2)}) copy-start(f32[768]{0:T(1024)S(1)} %get-tuple-element.51) | copy-start | bytes 9220
  60.9 6.0 copy-start.29
  60.9 6.0 copy-start.26
  60.9 6.1 copy-start.27
  60.9 25.2 %all-to-all-start = ((bf16[4,3,64,512]{3,2,1,0:T(8,128)(2,1)}), bf16[4,3,64,512]{3,2,1,0:T(8,128)(2,1)S(1)}, u32[]{:S(2)}, u32[]{:S(2)}) async-start(bf16[4,3,64,512]{3,2,1,0:T(8,128)(2,1)} %copy.130), calls=%async_computation | async-start | bytes 1572864 | tf_op jit(solution)/shard_map/all_to_all | solution.py:164
  86.1 26.9 %copy-start.11 = (bf16[4,3,64,512]{3,2,1,0:T(8,128)(2,1)}, bf16[4,3,64,512]{3,2,1,0:T(8,128)(2,1)S(1)}, u32[]{:S(2)}) copy-start(bf16[4,3,64,512]{3,2,1,0:T(8,128)(2,1)S(1)} %all-to-all-done.own) | copy-start | bytes 2359300
  86.1 23.1 %all-to-all-start.2 = ((bf16[4,3,64,512]{3,2,1,0:T(8,128)(2,1)}), bf16[4,3,64,512]{3,2,1,0:T(8,128)(2,1)S(1)}, u32[]{:S(2)}, u32[]{:S(2)}) async-start(bf16[4,3,64,512]{3,2,1,0:T(8,128)(2,1)} %copy.134), calls=%async_computation.2 | async-start | bytes 1572864 | tf_op jit(solution)/shard_map/all_to_all | solution.py:164
  109.3 6.2 copy-start.9
  109.3 23.1 %all-to-all-start.4 = ((bf16[4,3,64,512]{3,2,1,0:T(8,128)(2,1)}), bf16[4,3,64,512]{3,2,1,0:T(8,128)(2,1)S(1)}, u32[]{:S(2)}, u32[]{:S(2)}) async-start(bf16[4,3,64,512]{3,2,1,0:T(8,128)(2,1)} %pad_maximum_fusion.2), calls=%async_computation.4 | async-start | bytes 1572864 | tf_op jit(solution)/shard_map/all_to_all | solution.py:164
  112.8 106.0 %all-gather.18.cloned.1.call-start = ((), (), s32[]{:S(2)}) async-start(), calls=%async_computation.23 | async-start | bytes 2211840 | tf_op jit(solution)/shard_map/all_gather | solution.py:176
  113.9 20.1 %collective-permute-start = (bf16[4,2,64,512]{3,2,1,0:T(8,128)(2,1)}, bf16[4,2,64,512]{3,2,1,0:T(8,128)(2,1)S(1)}, u32[]{:S(2)}, u32[]{:S(2)}) collective-permute-start(bf16[4,2,64,512]{3,2,1,0:T(8,128)(2,1)} %slice.254), channel_id=1, source_target_pairs={{0,4},{4,0},{8,12},{12,8},{16,20},{20,16},{24,28},{28,24},{1,5},{5... | collective-permute-start | bytes 1572872 | tf_op jit(solution)/shard_map/ppermute | solution.py:172
  115.4 40.8 %collective-permute-start.1 = (bf16[4,2,64,512]{3,2,1,0:T(8,128)(2,1)S(1)}, bf16[4,2,64,512]{3,2,1,0:T(8,128)(2,1)}, u32[]{:S(2)}, u32[]{:S(2)}) collective-permute-start(bf16[4,2,64,512]{3,2,1,0:T(8,128)(2,1)S(1)} %slice.263), channel_id=1, source_target_pairs={{0,4},{4,0},{8,12},{12,8},{16,20},{20,16},{24,28},{28,24},{1,5},{5... | collective-permute-start | bytes 1572872 | tf_op jit(solution)/shard_map/ppermute | solution.py:172
  132.4 20.5 %copy-start.10 = (bf16[4,3,64,512]{3,2,1,0:T(8,128)(2,1)}, bf16[4,3,64,512]{3,2,1,0:T(8,128)(2,1)S(1)}, u32[]{:S(2)}) copy-start(bf16[4,3,64,512]{3,2,1,0:T(8,128)(2,1)S(1)} %all-to-all-done.4.own) | copy-start | bytes 2359300
  132.4 47.0 %collective-permute-start.2 = (bf16[4,2,64,512]{3,2,1,0:T(8,128)(2,1)S(1)}, bf16[4,2,64,512]{3,2,1,0:T(8,128)(2,1)}, u32[]{:S(2)}, u32[]{:S(2)}) collective-permute-start(bf16[4,2,64,512]{3,2,1,0:T(8,128)(2,1)S(1)} %slice.272), channel_id=1, source_target_pairs={{0,4},{4,0},{8,12},{12,8},{16,20},{20,16},{24,28},{28,24},{1,5},{5... | collective-permute-start | bytes 1572872 | tf_op jit(solution)/shard_map/ppermute | solution.py:172
  152.9 21.5 %all-to-all-start.1 = ((bf16[4,64,512]{2,1,0:T(8,128)(2,1)}), bf16[4,64,512]{2,1,0:T(8,128)(2,1)S(1)}, u32[]{:S(2)}, u32[]{:S(2)}) async-start(bf16[4,64,512]{2,1,0:T(8,128)(2,1)} %get-tuple-element.26), calls=%async_computation.1 | async-start | bytes 524288 | tf_op jit(solution)/shard_map/all_to_all | solution.py:164
  174.3 35.4 %copy-start.35 = (bf16[4,64,512]{2,1,0:T(8,128)(2,1)}, bf16[4,64,512]{2,1,0:T(8,128)(2,1)S(1)}, u32[]{:S(2)}) copy-start(bf16[4,64,512]{2,1,0:T(8,128)(2,1)S(1)} %all-to-all-done.1) | copy-start | bytes 786436
  174.3 23.1 %all-to-all-start.3 = ((bf16[4,64,512]{2,1,0:T(8,128)(2,1)}), bf16[4,64,512]{2,1,0:T(8,128)(2,1)S(1)}, u32[]{:S(2)}, u32[]{:S(2)}) async-start(bf16[4,64,512]{2,1,0:T(8,128)(2,1)} %get-tuple-element.27), calls=%async_computation.3 | async-start | bytes 524288 | tf_op jit(solution)/shard_map/all_to_all | solution.py:164
  197.5 14.5 %copy-start.37 = (bf16[4,64,512]{2,1,0:T(8,128)(2,1)}, bf16[4,64,512]{2,1,0:T(8,128)(2,1)S(1)}, u32[]{:S(2)}) copy-start(bf16[4,64,512]{2,1,0:T(8,128)(2,1)S(1)} %all-to-all-done.3) | copy-start | bytes 786436
  197.5 12.3 %all-to-all-start.5 = ((bf16[4,64,512]{2,1,0:T(8,128)(2,1)}), bf16[4,64,512]{2,1,0:T(8,128)(2,1)S(1)}, u32[]{:S(2)}, u32[]{:S(2)}) async-start(bf16[4,64,512]{2,1,0:T(8,128)(2,1)} %get-tuple-element.28), calls=%async_computation.5 | async-start | bytes 524288 | tf_op jit(solution)/shard_map/all_to_all | solution.py:164
  212.0 20.7 %copy-start.43 = (f32[512]{0:T(512)}, f32[512]{0:T(512)S(1)}, u32[]{:S(2)}) copy-start(f32[512]{0:T(512)S(1)} %broadcast_multiply_fusion) | copy-start | bytes 6148
  212.3 20.4 %copy-start.49 = (f32[512]{0:T(512)}, f32[512]{0:T(512)S(1)}, u32[]{:S(2)}) copy-start(f32[512]{0:T(512)S(1)} %fusion.47) | copy-start | bytes 6148
  212.4 6.4 copy-start.5
  218.7 7.7 %copy-start.4 = (f32[512,2304]{1,0:T(8,128)S(1)}, f32[512,2304]{1,0:T(8,128)}, u32[]{:S(2)}) copy-start(f32[512,2304]{1,0:T(8,128)} %fusion.53) | copy-start | bytes 14155780
  248.8 31.9 %copy-start.18 = (bf16[256,512]{0,1:T(8,128)(2,1)S(1)}, bf16[256,512]{0,1:T(8,128)(2,1)}, u32[]{:S(2)}) copy-start(bf16[256,512]{0,1:T(8,128)(2,1)} %get-tuple-element.77) | copy-start | bytes 786436
  274.0 16.9 %collective-permute-start.3 = (bf16[4,2,64,512]{3,2,1,0:T(8,128)(2,1)}, bf16[4,2,64,512]{3,2,1,0:T(8,128)(2,1)}, u32[]{:S(2)}, u32[]{:S(2)}) collective-permute-start(bf16[4,2,64,512]{3,2,1,0:T(8,128)(2,1)} %get-tuple-element.33), channel_id=1, source_target_pairs={{0,4},{4,0},{8,12},{12,8},{16,20},{20,16},{24,28},{28,24},{1,5},{5... | collective-permute-start | bytes 1572872 | tf_op jit(solution)/shard_map/ppermute | solution.py:172
  276.6 10.9 %all-to-all-start.8 = ((bf16[4,64,512]{2,1,0:T(8,128)(2,1)}), bf16[4,64,512]{2,1,0:T(8,128)(2,1)}, u32[]{:S(2)}, u32[]{:S(2)}) async-start(bf16[4,64,512]{2,1,0:T(8,128)(2,1)} %bitcast.45), calls=%async_computation.8 | async-start | bytes 524288 | tf_op jit(solution)/shard_map/all_to_all | solution.py:164
  287.5 10.2 %all-to-all-start.10 = ((bf16[4,64,512]{2,1,0:T(8,128)(2,1)}), bf16[4,64,512]{2,1,0:T(8,128)(2,1)S(1)}, u32[]{:S(2)}, u32[]{:S(2)}) async-start(bf16[4,64,512]{2,1,0:T(8,128)(2,1)} %bitcast.53), calls=%async_computation.10 | async-start | bytes 524288 | tf_op jit(solution)/shard_map/all_to_all | solution.py:164
  297.7 29.3 %copy-start.39 = (bf16[4,64,512]{2,1,0:T(8,128)(2,1)}, bf16[4,64,512]{2,1,0:T(8,128)(2,1)S(1)}, u32[]{:S(2)}) copy-start(bf16[4,64,512]{2,1,0:T(8,128)(2,1)S(1)} %all-to-all-done.10.rest_1_) | copy-start | bytes 786436
  297.7 40.9 %all-to-all-start.7 = ((bf16[4,3,64,512]{3,2,1,0:T(8,128)(2,1)}), bf16[4,3,64,512]{3,2,1,0:T(8,128)(2,1)}, u32[]{:S(2)}, u32[]{:S(2)}) async-start(bf16[4,3,64,512]{3,2,1,0:T(8,128)(2,1)} %pad_maximum_fusion.4), calls=%async_computation.7 | async-start | bytes 1572864 | tf_op jit(solution)/shard_map/all_to_all | solution.py:164
  327.1 10.6 %copy-start.41 = (bf16[4,64,512]{2,1,0:T(8,128)(2,1)S(1)}, bf16[4,64,512]{2,1,0:T(8,128)(2,1)}, u32[]{:S(2)}) copy-start(bf16[4,64,512]{2,1,0:T(8,128)(2,1)} %get-tuple-element.36) | copy-start | bytes 786436
  327.1 9.5 %collective-permute-start.4 = (bf16[4,2,64,512]{3,2,1,0:T(8,128)(2,1)}, bf16[4,2,64,512]{3,2,1,0:T(8,128)(2,1)S(1)}, u32[]{:S(2)}, u32[]{:S(2)}) collective-permute-start(bf16[4,2,64,512]{3,2,1,0:T(8,128)(2,1)} %get-tuple-element.38), channel_id=1, source_target_pairs={{0,4},{4,0},{8,12},{12,8},{16,20},{20,16},{24,28},{28,24},{1,5},{5... | collective-permute-start | bytes 1572872 | tf_op jit(solution)/shard_map/ppermute | solution.py:172
  338.7 41.9 %all-to-all-start.9 = ((bf16[4,3,64,512]{3,2,1,0:T(8,128)(2,1)}), bf16[4,3,64,512]{3,2,1,0:T(8,128)(2,1)}, u32[]{:S(2)}, u32[]{:S(2)}) async-start(bf16[4,3,64,512]{3,2,1,0:T(8,128)(2,1)} %pad_maximum_fusion.5), calls=%async_computation.9 | async-start | bytes 1572864 | tf_op jit(solution)/shard_map/all_to_all | solution.py:164
  369.1 10.6 %copy-start.42 = (bf16[4,64,512]{2,1,0:T(8,128)(2,1)S(1)}, bf16[4,64,512]{2,1,0:T(8,128)(2,1)}, u32[]{:S(2)}) copy-start(bf16[4,64,512]{2,1,0:T(8,128)(2,1)} %get-tuple-element.41) | copy-start | bytes 786436
  369.1 9.4 %collective-permute-start.5 = (bf16[4,2,64,512]{3,2,1,0:T(8,128)(2,1)}, bf16[4,2,64,512]{3,2,1,0:T(8,128)(2,1)S(1)}, u32[]{:S(2)}, u32[]{:S(2)}) collective-permute-start(bf16[4,2,64,512]{3,2,1,0:T(8,128)(2,1)} %get-tuple-element.43), channel_id=1, source_target_pairs={{0,4},{4,0},{8,12},{12,8},{16,20},{20,16},{24,28},{28,24},{1,5},{5... | collective-permute-start | bytes 1572872 | tf_op jit(solution)/shard_map/ppermute | solution.py:172
  380.6 18.3 %all-to-all-start.11 = ((bf16[4,3,64,512]{3,2,1,0:T(8,128)(2,1)}), bf16[4,3,64,512]{3,2,1,0:T(8,128)(2,1)}, u32[]{:S(2)}, u32[]{:S(2)}) async-start(bf16[4,3,64,512]{3,2,1,0:T(8,128)(2,1)} %pad_maximum_fusion.6), calls=%async_computation.11 | async-start | bytes 1572864 | tf_op jit(solution)/shard_map/all_to_all | solution.py:164
  385.7 47.0 %reduce-scatter.9.cloned.1.call-start = ((), (), s32[]{:S(2)}) async-start(), calls=%async_computation.25 | async-start | bytes 1474560 | tf_op jit(solution)/shard_map/reduce_scatter | solution.py:180
  408.1 52.1 %reduce-scatter.7.cloned.1.call-start = ((), (), s32[]{:S(2)}) async-start(), calls=%async_computation.24 | async-start | bytes 1474560 | tf_op jit(solution)/shard_map/reduce_scatter | solution.py:180
  413.3 75.7 %reduce-scatter.11.cloned.1.call-start = ((), (), s32[]{:S(2)}) async-start(), calls=%async_computation.26 | async-start | bytes 1474560 | tf_op jit(solution)/shard_map/reduce_scatter | solution.py:180
  418.5 98.5 %reduce-scatter.13.cloned.1.call-start = ((), (), s32[]{:S(2)}) async-start(), calls=%async_computation.27 | async-start | bytes 1474560 | tf_op jit(solution)/shard_map/reduce_scatter | solution.py:180
  421.8 127.6 %reduce-scatter.17.cloned.1.call-start = ((), (), s32[]{:S(2)}) async-start(), calls=%async_computation.29 | async-start | bytes 2211840 | tf_op jit(solution)/shard_map/reduce_scatter | solution.py:180
  425.6 166.7 %reduce-scatter.15.cloned.1.call-start = ((), (), s32[]{:S(2)}) async-start(), calls=%async_computation.28 | async-start | bytes 4423680 | tf_op jit(solution)/shard_map/reduce_scatter | solution.py:180
  432.6 278.7 %all-reduce.5.cloned.1.call-start = ((), (), s32[]{:S(2)}) async-start(), calls=%async_computation.30 | async-start | bytes 5013504 | tf_op jit(solution)/shard_map/psum | solution.py:181
  (42 other events, 80.8 us)
Sparse Core Ops, SparseCore 0:
  14.5 20.1 all-gather.9
  36.8 17.4 all-gather.7
  56.4 17.4 all-gather.11
  75.3 17.4 all-gather.13
  94.2 30.7 all-gather.15
  126.4 20.7 all-gather.17
  408.2 23.7 reduce-scatter.8
  434.5 25.6 reduce-scatter.6
  463.3 25.6 reduce-scatter.10
  491.4 25.5 reduce-scatter.12
  520.2 29.1 reduce-scatter.16
  551.8 40.3 reduce-scatter.14
  597.2 114.0 all-reduce.4

commit v2 on v1

--- a/solution.py
+++ b/solution.py
@@ -6,6 +6,7 @@
 from jax.experimental import pallas as pl
 from jax.experimental.pallas import tpu as pltpu
 from jax.sharding import PartitionSpec as P
+
 
 HEADS = 12
 HEAD_DIM = 64
@@ -134,7 +135,7 @@
 
         lax.fori_loop(0, n, step, 0)
     for s in range(n):
-        query_grad[s] = (acc[s] * d**-0.5).astype(jnp.bfloat16)
+        query_grad[s] = acc[s] * d**-0.5
 
 
 def attend_back(own, others, upstream, out, total):
@@ -143,7 +144,7 @@
     pairs = n * t * m * n * t
     return pl.pallas_call(
         functools.partial(backward_kernel, m),
-        out_shape=(jax.ShapeDtypeStruct((n, d, t), jnp.bfloat16),)
+        out_shape=(jax.ShapeDtypeStruct((n, d, t), jnp.float32),)
         + tuple(jax.ShapeDtypeStruct((n, 2, d, t), jnp.bfloat16) for _ in range(m)),
         scratch_shapes=[
             pltpu.VMEM((n, d, t), jnp.float32),
@@ -159,9 +160,12 @@
 
 
 def exchange(values):
+    return lax.all_to_all(values, "ctx", 0, 0, axis_index_groups=alike())
+
+
+def alike():
     count = lax.axis_size("ctx") // GROUPS
-    groups = [[g * count + y for g in range(GROUPS)] for y in range(count)]
-    return lax.all_to_all(values, "ctx", 0, 0, axis_index_groups=groups)
+    return [[g * count + y for g in range(GROUPS)] for y in range(count)]
 
 
 def across(values, by):
@@ -181,17 +185,64 @@
     return lax.psum(part, "ctx").astype(jnp.float32)
 
 
-def body(tokens, cotangent, attn_gain, mlp_gain, w_qkv, w_out, w_in, w_mlp_out, block_offsets):
+def swapped(values, axis, bit):
+    count = lax.axis_size(axis)
+    return lax.ppermute(values, axis, [(i, i ^ bit) for i in range(count)])
+
+
+def by_group(value):
+    count = lax.axis_size("ctx") // GROUPS
+    group = lax.axis_index("ctx") // count
+    value = value[None]
+    bit = 1
+    while bit < GROUPS:
+        other = swapped(value, "ctx", bit * count)
+        value = jnp.where(
+            (group // bit) % 2 == 0,
+            jnp.concatenate([value, other]),
+            jnp.concatenate([other, value]),
+        )
+        bit *= 2
+    return value
+
+
+def reduced_heads(value):
+    size = lax.axis_size("dp")
+    place = lax.axis_index("dp")
+    value = value.reshape(size, value.shape[0] // size, value.shape[1])
+    bit = 1
+    while bit < size:
+        value = value.reshape(value.shape[0] // 2, 2, *value.shape[1:])
+        mine = (place // bit) % 2
+        keep = lax.dynamic_index_in_dim(value, mine, 1, keepdims=False)
+        send = lax.dynamic_index_in_dim(value, 1 - mine, 1, keepdims=False)
+        value = keep + swapped(send.astype(jnp.bfloat16), "dp", bit).astype(jnp.float32)
+        bit *= 2
+    value = value[0]
+    count = lax.axis_size("ctx") // GROUPS
+    bit = 1
+    while bit < count:
+        value = value.astype(jnp.bfloat16)
+        value = value.astype(jnp.float32) + swapped(value, "ctx", bit).astype(jnp.float32)
+        bit *= 2
+    return by_group(value.astype(jnp.bfloat16)).astype(jnp.float32)
+
+
+def tables(positions):
+    half = HEAD_DIM // 2
+    frequency = rope_base ** (-jnp.arange(half, dtype=jnp.float32) / half)
+    angles = frequency[:, None] * positions[..., None, :]
+    return jnp.cos(angles), jnp.sin(angles)
+
+
+def layer(tokens, cotangent, attn_gain, mlp_gain, w_qkv, w_out, w_in, w_mlp_out, block_offsets):
     width = HEADS * HEAD_DIM
     part = GROUPS * HEAD_DIM
     inputs = tokens[0].astype(jnp.float32)
     t = inputs.shape[0]
     m = lax.axis_size("ctx") // GROUPS
-    positions = (block_offsets[0, 0] + jnp.arange(t, dtype=jnp.int32)).astype(jnp.float32)
-    half = HEAD_DIM // 2
-    frequency = rope_base ** (-jnp.arange(half, dtype=jnp.float32) / half)
-    angles = frequency[:, None] * positions[None, :]
-    cosine, sine = jnp.cos(angles), jnp.sin(angles)
+    steps = jnp.arange(t, dtype=jnp.int32)
+    cosine, sine = tables((block_offsets[0, 0] + steps).astype(jnp.float32))
 
     gains = lax.all_gather(jnp.stack([attn_gain, mlp_gain]), "dp", axis=1, tiled=True)
     local_qkv = w_qkv.reshape(-1, 3, CHUNKS, part)
@@ -213,6 +264,9 @@
         lows.append(exchange(low).reshape(part, t))
         kept.append((own, others, out, total))
     attended = jnp.concatenate(lows, axis=0)
+    normed_here = lax.all_gather(normed, "ctx", axis=0, axis_index_groups=alike())
+    offsets = by_group(block_offsets[0])[:, 0]
+    cosine_here, sine_here = tables((offsets[:, None] + steps).astype(jnp.float32))
 
     residual = inputs + product(attended, weight_out, 0, 0)
     mlp_normed = layer_norm(residual, second_gain).astype(jnp.bfloat16)
@@ -238,39 +292,54 @@
     total_in = reduced(product(mlp_normed, grad_up_gate, 0, 0))
     total_out = reduced(product(attended, residual_low, 1, 0))
 
+    ups = []
+    for i in range(CHUNKS):
+        ups.append(exchange(grad_attended[i]))
     grad_normed = 0.0
-    totals_qkv = []
+    totals_qkv, packs, grads = [], [], []
     for i in range(CHUNKS):
         own, others, out, total = kept[i]
-        query_grad, own_grad, *other_grads = attend_back(
-            own, others, exchange(grad_attended[i]), out, total
+        if i > 1:
+            ups[i], packs[i - 2], grads[i - 2] = lax.optimization_barrier(
+                (ups[i], packs[i - 2], grads[i - 2])
+            )
+        query_grad, own_grad, *other_grads = attend_back(own, others, ups[i], out, total)
+        sums = own_grad.astype(jnp.float32)
+        moved = [across(grad, -by) for by, grad in zip(range(1, m), other_grads)]
+        for grad in moved:
+            sums = sums + grad.astype(jnp.float32)
+        grad_packed = jnp.stack(
+            [
+                unrotate(query_grad, cosine_here, sine_here),
+                unrotate(sums[:, 0], cosine_here, sine_here),
+                sums[:, 1],
+            ],
+            axis=1,
+        ).astype(jnp.bfloat16)
+        packs.append(grad_packed)
+        heads_grad = lax.dot_general(
+            normed_here,
+            grad_packed.reshape(GROUPS, 3 * HEAD_DIM, t),
+            (((0, 1), (0, 2)), ((), ())),
+            preferred_element_type=jnp.float32,
         )
-        sums = own_grad.astype(jnp.float32)
-        for by, grad in zip(range(1, m), other_grads):
-            sums = sums + across(grad, -by).astype(jnp.float32)
-        back = exchange(
-            jnp.concatenate([query_grad[:, None], sums.astype(jnp.bfloat16)], axis=1)
-        ).astype(jnp.float32)
-        grad_packed = (
-            jnp.stack(
-                [
-                    unrotate(back[:, 0], cosine, sine),
-                    unrotate(back[:, 1], cosine, sine),
-                    back[:, 2],
-                ]
-            )
-            .astype(jnp.bfloat16)
-            .reshape(3 * part, t)
-        )
-        totals_qkv.append(reduced(product(normed, grad_packed, 0, 1)).reshape(-1, 3, 1, part))
-        grad_normed = grad_normed + product(grad_packed, weights_qkv[i], 0, 1)
-    total_qkv = jnp.concatenate(totals_qkv, axis=2).reshape(-1, 3 * width)
+        grads.append(heads_grad)
+    for i in range(CHUNKS):
+        back = exchange(packs[i])
+        totals_qkv.append(reduced_heads(grads[i]))
+        back = back.transpose(1, 0, 2, 3).reshape(3 * part, t)
+        grad_normed = grad_normed + product(back, weights_qkv[i], 0, 1)
+    total_qkv = jnp.stack(totals_qkv).reshape(CHUNKS, GROUPS, -1, 3, HEAD_DIM)
+    total_qkv = total_qkv.transpose(2, 3, 0, 1, 4).reshape(-1, 3 * width)
     grad_inputs_norm, grad_gain_one = norm_back(inputs, first_gain, grad_normed)
     tokens_grad = (grad_residual + grad_inputs_norm)[None]
 
     gain_rows = attn_gain.shape[0]
-    gain_sums = lax.psum(jnp.stack([grad_gain_one, grad_gain_two]), ("ctx", "dp"))
-    gain_sums = lax.dynamic_slice_in_dim(gain_sums, lax.axis_index("dp") * gain_rows, gain_rows, 1)
+    gain_parts = lax.all_gather(jnp.stack([grad_gain_one, grad_gain_two]), ("ctx", "dp"))
+    gain_parts = lax.dynamic_slice_in_dim(
+        gain_parts, lax.axis_index("dp") * gain_rows, gain_rows, 2
+    )
+    gain_sums = jnp.sum(gain_parts, axis=0)
     return (
         mixed,
         tokens_grad,
@@ -285,7 +354,7 @@
 
 def solution(mesh):
     return jax.shard_map(
-        body,
+        layer,
         mesh=mesh,
         in_specs=(
             P("dp", "ctx", None),

time: 737 us -> 611 us (0.83)
  waiting for transfers between devices: 331 us -> 168 us
  starting transfers between devices: 55.5 us -> 82.1 us
  blocking collectives: 58.4 us -> 47.2 us
  other arithmetic: 31.8 us -> 41.6 us
  local copies, waits for them, and re-layouts: 51 us -> 59.4 us
    reduce_scatter x6 -> x3, waiting for transfers between devices: 154 us -> 0.01 us  [reduced(): lax.psum_scatter(value.astype(jnp.bfloat16), 'dp', scatter_dimension=0, t...]
    psum x1 -> x0, blocking collectives: 41.7 us -> none  [body(): lax.psum(jnp.stack([grad_gain_one, grad_gain_two]), ('ctx', 'dp'))]
    all_gather x1 -> x2, blocking collectives: 6.02 us -> 47.2 us  [the longest x1 41.2 us: layer(): lax.all_gather(jnp.stack([grad_gain_one, grad_gain_two]), ('ctx', 'dp'))]
    ppermute x0 -> x17, waiting for transfers between devices: none -> 33.1 us  [swapped(): return lax.ppermute(values, axis, [(i, i ^ bit) for i in range(count)])]
    ppermute x0 -> x17, starting transfers between devices: none -> 22 us  [swapped(): return lax.ppermute(values, axis, [(i, i ^ bit) for i in range(count)])]
    psum x1, waiting for transfers between devices: 64.3 us -> 42.4 us  [reduced(): return lax.psum(part, 'ctx').astype(jnp.float32)]
    ppermute x6, waiting for transfers between devices: 16.4 us -> 0.02 us  [across(): return lax.ppermute(values, 'ctx', pairs)]
    all_to_all x1 -> x0, blocking collectives: 10.6 us -> none  [exchange(): return lax.all_to_all(values, 'ctx', 0, 0, axis_index_groups=groups)]
  transfers between devices with their start and end apart: 30 -> 46, of which waited for: 17 -> 19; matrix products, arithmetic and copies ran while one was open for 12% -> 23% of each run, Pallas kernels for 14% -> 22%
where the time goes in v2:
time: 611 us; the launch traced here: 600 us
  waiting for transfers between devices  168 us (27%)
  Pallas kernels  130 us (21%)
  starting transfers between devices  82.1 us (13%)
  local copies, waits for them, and re-layouts  59.4 us (10%)
  matrix products  55.5 us (9%)
  blocking collectives  47.2 us (8%)
  other arithmetic  41.6 us (7%)
  between operations  16.2 us (3%)
    pallas_call x3, Pallas kernels, attend_back(): pl.pallas_call(functools.partial(backward_kernel, m), out_shape=(jax.Shap...  75.6 us
    all_to_all x12, waiting for transfers between devices, exchange(): return lax.all_to_all(values, 'ctx', 0, 0, axis_index_groups=alike())  65.9 us
    pallas_call x3, Pallas kernels, attend(): pl.pallas_call(functools.partial(forward_kernel, m), out_shape=(jax.Shape...  54.2 us
    dot_general x15, matrix products, product(): lax.dot_general(left, right, (((left_dim,), (right_dim,)), ((), ())), pre...  52 us
    all_to_all x12, starting transfers between devices, exchange(): return lax.all_to_all(values, 'ctx', 0, 0, axis_index_groups=alike())  50.7 us
    psum x1, waiting for transfers between devices, reduced(): return lax.psum(part, 'ctx').astype(jnp.float32)  42.4 us
    all_gather x1, blocking collectives, layer(): lax.all_gather(jnp.stack([grad_gain_one, grad_gain_two]), ('ctx', 'dp'))  41.2 us
    ppermute x17, waiting for transfers between devices, swapped(): return lax.ppermute(values, axis, [(i, i ^ bit) for i in range(count)])  33.1 us
  transfers between devices with their start and end apart: 46, of which 19 were waited for; matrix products, arithmetic and copies ran while one was open for 23% of the time, Pallas kernels for 22%

profile of v2, /device:TPU:0, one launch (start us, length us, event | category | flops | bytes accessed | tf_op | source)
XLA Modules:
  0.0 600.1 jit_solution(4982061926915587228)
XLA Ops:
  9.4 4.2 slice_reduce_fusion.2
  17.9 6.0 %all-gather.1 = bf16[4,192,2]{1,2,0:T(2,128)(2,1)S(1)} all-gather(bf16[1,192,2]{1,2,0:T(2,128)(2,1)S(1)} %maximum_bitcast_fusion.7), channel_id=1, replica_groups=mesh['ctx'=8,'dp'=4] {'dp'}, dimensions={0}, use_global_device_ids=true | all-gather | bytes 3840 | tf_op jit(solution)/shard_map/all_gather | solution.py:247
  25.0 9.7 %all-gather.13.cloned.1.call-done = bf16[768,768]{1,0:T(8,128)(2,1)} async-done(((bf16[192,768]{1,0:T(8,128)(2,1)}), bf16[768,768]{1,0:T(8,128)(2,1)}) %all-gather.13.cloned.1.call-update) | async-done | bytes 1179664 | tf_op jit(solution)/shard_map/all_gather | solution.py:180
  38.4 15.9 %all-gather.11.cloned.1.call-done = bf16[768,768]{1,0:T(8,128)(2,1)} async-done(((bf16[192,768]{1,0:T(8,128)(2,1)}), bf16[768,768]{1,0:T(8,128)(2,1)}) %all-gather.11.cloned.1.call-update) | async-done | bytes 1179664 | tf_op jit(solution)/shard_map/all_gather | solution.py:180
  60.8 4.7 all-to-all-start
  67.8 18.2 %all-to-all-done.own = bf16[4,3,64,512]{3,2,1,0:T(8,128)(2,1)S(1)} async-done(((bf16[4,3,64,512]{3,2,1,0:T(8,128)(2,1)}), bf16[4,3,64,512]{3,2,1,0:T(8,128)(2,1)S(1)}, u32[]{:S(2)}, u32[]{:S(2)}) %all-to-all-start) | async-done | bytes 786464 | tf_op jit(solution)/shard_map/all_to_all | solution.py:163
  86.0 3.5 all-to-all-start.2
  98.4 10.8 %all-to-all-done.2.own = bf16[4,3,64,512]{3,2,1,0:T(8,128)(2,1)S(1)} async-done(((bf16[4,3,64,512]{3,2,1,0:T(8,128)(2,1)}), bf16[4,3,64,512]{3,2,1,0:T(8,128)(2,1)S(1)}, u32[]{:S(2)}, u32[]{:S(2)}) %all-to-all-start.2) | async-done | bytes 786464 | tf_op jit(solution)/shard_map/all_to_all | solution.py:163
  109.2 3.5 all-to-all-start.4
  116.0 16.3 %all-to-all-done.4.own = bf16[4,3,64,512]{3,2,1,0:T(8,128)(2,1)S(1)} async-done(((bf16[4,3,64,512]{3,2,1,0:T(8,128)(2,1)}), bf16[4,3,64,512]{3,2,1,0:T(8,128)(2,1)S(1)}, u32[]{:S(2)}, u32[]{:S(2)}) %all-to-all-start.4) | async-done | bytes 786464 | tf_op jit(solution)/shard_map/all_to_all | solution.py:163
  134.7 18.1 %attend.3 = (f32[4,64,512]{2,1,0:T(8,128)}, bf16[4,64,512]{2,1,0:T(8,128)(2,1)}, f32[4,1,512]{2,1,0:T(1,128)}) custom-call(bf16[4,3,64,512]{3,2,1,0:T(8,128)(2,1)} %copy-done.12, bf16[4,2,64,512]{3,2,1,0:T(8,128)(2,1)} %copy-done.49), custom_call_target="tpu_custom_call" | custom-call | flops 8589934592 | bytes 2000000 | tf_op jit(solution)/shard_map/attend/pallas_call | solution.py:90
  152.7 3.4 all-to-all-start.1
  156.1 18.1 %attend.4 = (f32[4,64,512]{2,1,0:T(8,128)}, bf16[4,64,512]{2,1,0:T(8,128)(2,1)}, f32[4,1,512]{2,1,0:T(1,128)}) custom-call(bf16[4,3,64,512]{3,2,1,0:T(8,128)(2,1)} %copy-done.10, bf16[4,2,64,512]{3,2,1,0:T(8,128)(2,1)} %collective-permute-done.1.rest_0_), custom_call_target="tpu_custom_call" | custom-call | flops 8589934592 | bytes 2000000 | tf_op jit(solution)/shard_map/attend/pallas_call | solution.py:90
  174.2 5.1 all-to-all-start.3
  179.3 18.1 %attend.5 = (f32[4,64,512]{2,1,0:T(8,128)}, bf16[4,64,512]{2,1,0:T(8,128)(2,1)}, f32[4,1,512]{2,1,0:T(1,128)}) custom-call(bf16[4,3,64,512]{3,2,1,0:T(8,128)(2,1)} %copy-done.11, bf16[4,2,64,512]{3,2,1,0:T(8,128)(2,1)} %collective-permute-done.2.rest_0_), custom_call_target="tpu_custom_call" | custom-call | flops 8589934592 | bytes 2000000 | tf_op jit(solution)/shard_map/attend/pallas_call | solution.py:90
  197.3 5.1 all-to-all-start.5
  204.1 5.1 all-to-all-done.5
  211.8 6.8 %fusion.111 = f32[512,2304]{1,0:T(8,128)} fusion(bf16[768,2304]{1,0:T(8,128)(2,1)} %all-gather.19.cloned.1.call-done, f32[512,768]{1,0:T(8,128)S(1)} %get-tuple-element.154, f32[768]{0:T(1024)S(1)} %get-tuple-element.89, f32[512]{0:T(512)S(1)} %fusion.105, f32[512]{0:T(512)S(1)} %broadcast_multiply_fusion), kind=kOutput, calls=%fused_computation.239 | convolution fusion | flops 1813512192 | bytes 9837568 | tf_op jit(solution)/shard_map/dot_general | solution.py:37
  218.6 7.7 %fusion.32 = (f32[512,1152]{1,0:T(8,128)S(1)}, f32[512,1152]{1,0:T(8,128)S(1)}, f32[512,1152]{1,0:T(8,128)S(1)}) fusion(f32[512,2304]{1,0:T(8,128)} %fusion.111, bf16[1152,768]{1,0:T(8,128)(2,1)} %all-gather.21.cloned.1.call-done, bf16[1,512,768]{2,1,0:T(8,128)(2,1)S(1)} %copy-done.5), kind=kOutput, calls=%fused_computation.80 | convolution fusion | flops 944308224 | bytes 11993088 | tf_op jit(solution)/shard_map/dot_general | solution.py:37
  239.2 3.5 collective-permute-done.3
  244.2 5.0 collective-permute-done.4
  249.3 2.3 fusion.27
  254.3 4.0 all-to-all-start.7
  258.6 3.6 convolution_convert_fusion.1
  262.2 10.1 %all-to-all-done.7.rest_1_ = bf16[4,64,512]{2,1,0:T(8,128)(2,1)} async-done(((bf16[4,64,512]{2,1,0:T(8,128)(2,1)}), bf16[4,64,512]{2,1,0:T(8,128)(2,1)}, u32[]{:S(2)}, u32[]{:S(2)}) %all-to-all-start.7) | async-done | bytes 262176 | tf_op jit(solution)/shard_map/all_to_all | solution.py:163
  272.3 25.2 %attend_back.3 = (f32[4,64,512]{2,1,0:T(8,128)}, bf16[4,2,64,512]{3,2,1,0:T(8,128)(2,1)}, bf16[4,2,64,512]{3,2,1,0:T(8,128)(2,1)}) custom-call(bf16[4,3,64,512]{3,2,1,0:T(8,128)(2,1)} %copy-done.12, bf16[4,2,64,512]{3,2,1,0:T(8,128)(2,1)} %copy-done.49, bf16[4,64,512]{2,1,0:T(8,128)(2,1)} %all-to-all-done.7.rest_1_, ...), custom_call_target="tpu_custom_call" | custom-call | flops 21474836480 | bytes 4000000 | tf_op jit(solution)/shard_map/attend_back/pallas_call | solution.py:145
  300.0 4.7 copy.260
  305.6 4.0 all-to-all-start.6
  310.5 7.2 %convolution_convert_fusion = bf16[768,2304]{1,0:T(8,128)(2,1)} fusion(f32[512,1152]{1,0:T(8,128)} %copy-done.9, f32[512,1152]{1,0:T(8,128)} %copy-done.52, f32[512,768]{1,0:T(8,128)} %copy-done.2, f32[768]{0:T(1024)S(1)} %copy-done.41, f32[512]{0:T(512)S(1)} %fusion.105, f32[512]{0:T(512)S(1)} %broadcast_multiply_fusion), kind=kOutput, calls=%fused_computation | convolution fusion | flops 1817640960 | bytes 9837568 | tf_op jit(solution)/shard_map/dot_general | solution.py:37
  324.0 5.0 all-to-all-start.9
  329.2 2.7 reshape_reshape.2
  333.5 4.4 fusion.26
  342.3 25.2 %attend_back.4 = (f32[4,64,512]{2,1,0:T(8,128)}, bf16[4,2,64,512]{3,2,1,0:T(8,128)(2,1)}, bf16[4,2,64,512]{3,2,1,0:T(8,128)(2,1)}) custom-call(bf16[4,3,64,512]{3,2,1,0:T(8,128)(2,1)} %copy-done.10, bf16[4,2,64,512]{3,2,1,0:T(8,128)(2,1)} %collective-permute-done.1.rest_0_, bf16[4,64,512]{2,1,0:T(8,128)(2,1)} %all-to-all-done.9.rest_1_, ...), custom_call_target="tpu_custom_call" | custom-call | flops 21474836480 | bytes 4000000 | tf_op jit(solution)/shard_map/attend_back/pallas_call | solution.py:145
  373.0 25.2 %attend_back.5 = (f32[4,64,512]{2,1,0:T(8,128)}, bf16[4,2,64,512]{3,2,1,0:T(8,128)(2,1)}, bf16[4,2,64,512]{3,2,1,0:T(8,128)(2,1)}) custom-call(bf16[4,3,64,512]{3,2,1,0:T(8,128)(2,1)} %copy-done.11, bf16[4,2,64,512]{3,2,1,0:T(8,128)(2,1)} %collective-permute-done.2.rest_0_, bf16[4,64,512]{2,1,0:T(8,128)(2,1)} %all-to-all-done.6.rest_1_, ...), custom_call_target="tpu_custom_call" | custom-call | flops 21474836480 | bytes 4000000 | tf_op jit(solution)/shard_map/attend_back/pallas_call | solution.py:145
  405.4 3.0 collective-permute-start.12
  410.9 3.7 all-to-all-start.8
  428.1 5.4 all-to-all-done.8
  433.6 4.4 all-to-all-start.11
  451.4 2.5 collective-permute-done.16
  454.6 4.6 collective-permute-start.17
  461.3 4.2 all-to-all-start.10
  467.8 10.3 %collective-permute-done.17 = bf16[2,192,192]{1,2,0:T(8,128)(2,1)} collective-permute-done((bf16[2,192,192]{1,2,0:T(8,128)(2,1)}, bf16[2,192,192]{1,2,0:T(8,128)(2,1)}, u32[]{:S(2)}, u32[]{:S(2)}) %collective-permute-start.17) | collective-permute-done | bytes 147488 | tf_op jit(solution)/shard_map/ppermute | solution.py:190
  479.3 5.2 collective-permute-done.22
  487.3 2.9 copy.280
  498.3 3.4 fusion.22
  502.6 41.2 %all-gather.2 = f32[32,2,768]{2,1,0:T(2,128)S(1)} all-gather(f32[1,2,768]{2,1,0:T(2,128)S(1)} %maximum_bitcast_fusion.6), channel_id=2, replica_groups=mesh['ctx'=8,'dp'=4] {'ctx','dp'}, dimensions={0}, use_global_device_ids=true | all-gather | bytes 202752 | tf_op jit(solution)/shard_map/all_gather | solution.py:338
  546.3 42.4 %all-reduce.5.cloned.1.call-done = (bf16[192,768]{1,0:T(8,128)(2,1)}, bf16[192,2304]{1,0:T(8,128)(2,1)}, bf16[288,768]{1,0:T(8,128)(2,1)}) async-done(((bf16[192,768]{1,0:T(8,128)(2,1)}, bf16[192,2304]{1,0:T(8,128)(2,1)}, bf16[288,768]{1,0:T(8,128)(2,1)}), (bf16[192,768]{1,0:T(8,128)(2,1)}, bf16[192,2304]{1,0:T(8,128)(2,1)}, bf16[288,768]{1,0:T(8,128)(2,1)})) %all-reduce.5.cloned.1.call-update) | async-done | bytes 1622032 | tf_op jit(solution)/shard_map/psum | solution.py:185
  588.8 2.6 convert_element_type.384
  (322 shorter events, 136.1 us)
Async XLA Ops:
  7.2 27.5 %all-gather.13.cloned.1.call-start = ((), (), s32[]{:S(2)}) async-start(), calls=%async_computation.16 | async-start | bytes 1474560 | tf_op jit(solution)/shard_map/all_gather | solution.py:180
  14.4 39.9 %all-gather.11.cloned.1.call-start = ((), (), s32[]{:S(2)}) async-start(), calls=%async_computation.15 | async-start | bytes 1474560 | tf_op jit(solution)/shard_map/all_gather | solution.py:180
  15.2 74.3 %all-gather.15.cloned.1.call-start = ((), (), s32[]{:S(2)}) async-start(), calls=%async_computation.17 | async-start | bytes 1474560 | tf_op jit(solution)/shard_map/all_gather | solution.py:180
  16.1 188.1 %all-gather.17.cloned.1.call-start = ((), (), s32[]{:S(2)}) async-start(), calls=%async_computation.18 | async-start | bytes 1474560 | tf_op jit(solution)/shard_map/all_gather | solution.py:180
  16.6 195.2 %all-gather.19.cloned.1.call-start = ((), (), s32[]{:S(2)}) async-start(), calls=%async_computation.19 | async-start | bytes 4423680 | tf_op jit(solution)/shard_map/all_gather | solution.py:180
  17.8 184.6 %copy-start.34 = (f32[512]{0:T(512)}, f32[512]{0:T(512)S(1)}, u32[]{:S(2)}) copy-start(f32[512]{0:T(512)S(1)} %fusion.104) | copy-start | bytes 6148
  25.0 207.2 %copy-start.40 = (f32[768]{0:T(1024)}, f32[768]{0:T(1024)S(1)}, u32[]{:S(2)}) copy-start(f32[768]{0:T(1024)S(1)} %get-tuple-element.89) | copy-start | bytes 9220
  60.8 25.2 %all-to-all-start = ((bf16[4,3,64,512]{3,2,1,0:T(8,128)(2,1)}), bf16[4,3,64,512]{3,2,1,0:T(8,128)(2,1)S(1)}, u32[]{:S(2)}, u32[]{:S(2)}) async-start(bf16[4,3,64,512]{3,2,1,0:T(8,128)(2,1)} %copy.227), calls=%async_computation | async-start | bytes 1572864 | tf_op jit(solution)/shard_map/all_to_all | solution.py:163
  86.0 23.1 %all-to-all-start.2 = ((bf16[4,3,64,512]{3,2,1,0:T(8,128)(2,1)}), bf16[4,3,64,512]{3,2,1,0:T(8,128)(2,1)S(1)}, u32[]{:S(2)}, u32[]{:S(2)}) async-start(bf16[4,3,64,512]{3,2,1,0:T(8,128)(2,1)} %copy.231), calls=%async_computation.2 | async-start | bytes 1572864 | tf_op jit(solution)/shard_map/all_to_all | solution.py:163
  109.2 23.1 %all-to-all-start.4 = ((bf16[4,3,64,512]{3,2,1,0:T(8,128)(2,1)}), bf16[4,3,64,512]{3,2,1,0:T(8,128)(2,1)S(1)}, u32[]{:S(2)}, u32[]{:S(2)}) async-start(bf16[4,3,64,512]{3,2,1,0:T(8,128)(2,1)} %pad_maximum_fusion.2), calls=%async_computation.4 | async-start | bytes 1572864 | tf_op jit(solution)/shard_map/all_to_all | solution.py:163
  112.7 106.0 %all-gather.21.cloned.1.call-start = ((), (), s32[]{:S(2)}) async-start(), calls=%async_computation.20 | async-start | bytes 2211840 | tf_op jit(solution)/shard_map/all_gather | solution.py:180
  113.8 20.1 %collective-permute-start = (bf16[4,2,64,512]{3,2,1,0:T(8,128)(2,1)}, bf16[4,2,64,512]{3,2,1,0:T(8,128)(2,1)S(1)}, u32[]{:S(2)}, u32[]{:S(2)}) collective-permute-start(bf16[4,2,64,512]{3,2,1,0:T(8,128)(2,1)} %slice.244), channel_id=1, source_target_pairs={{0,4},{4,0},{8,12},{12,8},{16,20},{20,16},{24,28},{28,24},{1,5},{5... | collective-permute-start | bytes 1572872 | tf_op jit(solution)/shard_map/ppermute | solution.py:176
  115.3 40.8 %collective-permute-start.1 = (bf16[4,2,64,512]{3,2,1,0:T(8,128)(2,1)S(1)}, bf16[4,2,64,512]{3,2,1,0:T(8,128)(2,1)}, u32[]{:S(2)}, u32[]{:S(2)}) collective-permute-start(bf16[4,2,64,512]{3,2,1,0:T(8,128)(2,1)S(1)} %slice.253), channel_id=1, source_target_pairs={{0,4},{4,0},{8,12},{12,8},{16,20},{20,16},{24,28},{28,24},{1,5},{5... | collective-permute-start | bytes 1572872 | tf_op jit(solution)/shard_map/ppermute | solution.py:176
  132.3 46.9 %collective-permute-start.2 = (bf16[4,2,64,512]{3,2,1,0:T(8,128)(2,1)S(1)}, bf16[4,2,64,512]{3,2,1,0:T(8,128)(2,1)}, u32[]{:S(2)}, u32[]{:S(2)}) collective-permute-start(bf16[4,2,64,512]{3,2,1,0:T(8,128)(2,1)S(1)} %slice.262), channel_id=1, source_target_pairs={{0,4},{4,0},{8,12},{12,8},{16,20},{20,16},{24,28},{28,24},{1,5},{5... | collective-permute-start | bytes 1572872 | tf_op jit(solution)/shard_map/ppermute | solution.py:176
  152.7 21.5 %all-to-all-start.1 = ((bf16[4,64,512]{2,1,0:T(8,128)(2,1)}), bf16[4,64,512]{2,1,0:T(8,128)(2,1)S(1)}, u32[]{:S(2)}, u32[]{:S(2)}) async-start(bf16[4,64,512]{2,1,0:T(8,128)(2,1)} %get-tuple-element.29), calls=%async_computation.1 | async-start | bytes 524288 | tf_op jit(solution)/shard_map/all_to_all | solution.py:163
  174.2 23.1 %all-to-all-start.3 = ((bf16[4,64,512]{2,1,0:T(8,128)(2,1)}), bf16[4,64,512]{2,1,0:T(8,128)(2,1)S(1)}, u32[]{:S(2)}, u32[]{:S(2)}) async-start(bf16[4,64,512]{2,1,0:T(8,128)(2,1)} %get-tuple-element.30), calls=%async_computation.3 | async-start | bytes 524288 | tf_op jit(solution)/shard_map/all_to_all | solution.py:163
  197.3 11.9 %all-to-all-start.5 = ((bf16[4,64,512]{2,1,0:T(8,128)(2,1)}), bf16[4,64,512]{2,1,0:T(8,128)(2,1)S(1)}, u32[]{:S(2)}, u32[]{:S(2)}) async-start(bf16[4,64,512]{2,1,0:T(8,128)(2,1)} %get-tuple-element.31), calls=%async_computation.5 | async-start | bytes 524288 | tf_op jit(solution)/shard_map/all_to_all | solution.py:163
  202.4 97.6 %all-gather.23.cloned.1.call-start = ((), (), s32[]{:S(2)}) async-start(), calls=%async_computation.21 | async-start | bytes 3932160 | tf_op jit(solution)/shard_map/all_gather | solution.py:267
  203.6 294.6 %reduce-scatter.4.cloned.1.call-start = ((), (), s32[]{:S(2)}) async-start(), calls=%async_computation.22 | async-start | bytes 1474560 | tf_op jit(solution)/shard_map/reduce_scatter | solution.py:184
  237.6 5.1 collective-permute-start.3
  243.4 5.8 collective-permute-start.4
  254.3 18.0 %all-to-all-start.7 = ((bf16[4,64,512]{2,1,0:T(8,128)(2,1)}), bf16[4,64,512]{2,1,0:T(8,128)(2,1)}, u32[]{:S(2)}, u32[]{:S(2)}) async-start(bf16[4,64,512]{2,1,0:T(8,128)(2,1)} %bitcast.38), calls=%async_computation.7 | async-start | bytes 524288 | tf_op jit(solution)/shard_map/all_to_all | solution.py:163
  258.3 239.9 %reduce-scatter.8.cloned.1.call-start = ((), (), s32[]{:S(2)}) async-start(), calls=%async_computation.24 | async-start | bytes 2211840 | tf_op jit(solution)/shard_map/reduce_scatter | solution.py:184
  298.6 19.1 %collective-permute-start.5 = (bf16[4,2,64,512]{3,2,0,1:T(8,128)(2,1)S(1)}, bf16[4,2,64,512]{3,2,0,1:T(8,128)(2,1)}, u32[]{:S(2)}, u32[]{:S(2)}) collective-permute-start(bf16[4,2,64,512]{3,2,0,1:T(8,128)(2,1)S(1)} %copy.240), channel_id=1, source_target_pairs={{0,4},{4,0},{8,12},{12,8},{16,20},{20,16},{24,28},{28,24},{1,5},{5... | collective-permute-start | bytes 1572872 | tf_op jit(solution)/shard_map/ppermute | solution.py:176
  305.6 18.4 %all-to-all-start.6 = ((bf16[4,64,512]{2,1,0:T(8,128)(2,1)}), bf16[4,64,512]{2,1,0:T(8,128)(2,1)}, u32[]{:S(2)}, u32[]{:S(2)}) async-start(bf16[4,64,512]{2,1,0:T(8,128)(2,1)} %bitcast.37), calls=%async_computation.6 | async-start | bytes 524288 | tf_op jit(solution)/shard_map/all_to_all | solution.py:163
  324.0 18.3 %all-to-all-start.9 = ((bf16[4,64,512]{2,1,0:T(8,128)(2,1)}), bf16[4,64,512]{2,1,0:T(8,128)(2,1)}, u32[]{:S(2)}, u32[]{:S(2)}) async-start(bf16[4,64,512]{2,1,0:T(8,128)(2,1)} %bitcast.48), calls=%async_computation.9 | async-start | bytes 524288 | tf_op jit(solution)/shard_map/all_to_all | solution.py:163
  329.0 169.2 %reduce-scatter.6.cloned.1.call-start = ((), (), s32[]{:S(2)}) async-start(), calls=%async_computation.23 | async-start | bytes 4423680 | tf_op jit(solution)/shard_map/reduce_scatter | solution.py:184
  333.4 6.5 %collective-permute-start.8 = (bf16[2,192,192]{1,2,0:T(8,128)(2,1)S(1)}, bf16[2,192,192]{1,2,0:T(8,128)(2,1)}, u32[]{:S(2)}, u32[]{:S(2)}) collective-permute-start(bf16[2,192,192]{1,2,0:T(8,128)(2,1)S(1)} %bitcast.309), channel_id=1, source_target_pairs={{0,1},{1,0},{2,3},{3,2},{4,5},{5,4},{6,7},{7,6},{8,9},{9,8},{10,11... | collective-permute-start | bytes 442376 | tf_op jit(solution)/shard_map/ppermute | solution.py:190
  341.6 29.4 %collective-permute-start.9 = (bf16[1,192,192]{1,2,0:T(8,128)(2,1)}, bf16[1,192,192]{1,2,0:T(8,128)(2,1)}, u32[]{:S(2)}, u32[]{:S(2)}) collective-permute-start(bf16[1,192,192]{1,2,0:T(8,128)(2,1)} %dynamic-slice_convert_fusion.4), channel_id=1, source_target_pairs={{0,2},{1,3},{2,0},{3,1},{4,6},{5,7},{6,4},{7,5},{8,10},{9,11},{10,... | collective-permute-start | bytes 221192 | tf_op jit(solution)/shard_map/ppermute | solution.py:190
  369.4 33.4 %collective-permute-start.6 = (bf16[4,2,64,512]{3,2,0,1:T(8,128)(2,1)}, bf16[4,2,64,512]{3,2,0,1:T(8,128)(2,1)}, u32[]{:S(2)}, u32[]{:S(2)}) collective-permute-start(bf16[4,2,64,512]{3,2,0,1:T(8,128)(2,1)} %copy.246), channel_id=1, source_target_pairs={{0,4},{4,0},{8,12},{12,8},{16,20},{20,16},{24,28},{28,24},{1,5},{5... | collective-permute-start | bytes 1572872 | tf_op jit(solution)/shard_map/ppermute | solution.py:176
  372.5 27.2 %collective-permute-start.10 = (bf16[192,192]{0,1:T(8,128)(2,1)}, bf16[192,192]{0,1:T(8,128)(2,1)S(1)}, u32[]{:S(2)}, u32[]{:S(2)}) collective-permute-start(bf16[192,192]{0,1:T(8,128)(2,1)} %fusion.99), channel_id=1, source_target_pairs={{0,4},{4,0},{8,12},{12,8},{16,20},{20,16},{24,28},{28,24},{1,5},{5... | collective-permute-start | bytes 221192 | tf_op jit(solution)/shard_map/ppermute | solution.py:190
  398.2 19.4 %collective-permute-start.7 = (bf16[4,2,64,512]{3,2,1,0:T(8,128)(2,1)}, bf16[4,2,64,512]{3,2,1,0:T(8,128)(2,1)}, u32[]{:S(2)}, u32[]{:S(2)}) collective-permute-start(bf16[4,2,64,512]{3,2,1,0:T(8,128)(2,1)} %get-tuple-element.48), channel_id=1, source_target_pairs={{0,4},{4,0},{8,12},{12,8},{16,20},{20,16},{24,28},{28,24},{1,5},{5... | collective-permute-start | bytes 1572872 | tf_op jit(solution)/shard_map/ppermute | solution.py:176
  400.7 4.7 collective-permute-start.11
  405.4 11.1 %collective-permute-start.12 = (bf16[2,192,192]{1,2,0:T(8,128)(2,1)S(1)}, bf16[2,192,192]{1,2,0:T(8,128)(2,1)}, u32[]{:S(2)}, u32[]{:S(2)}) collective-permute-start(bf16[2,192,192]{1,2,0:T(8,128)(2,1)S(1)} %maximum_select_fusion.3), channel_id=1, source_target_pairs={{0,16},{4,20},{8,24},{12,28},{16,0},{20,4},{24,8},{28,12},{1,17},{... | collective-permute-start | bytes 442376 | tf_op jit(solution)/shard_map/ppermute | solution.py:190
  410.9 22.6 %all-to-all-start.8 = ((bf16[4,3,64,512]{3,2,1,0:T(8,128)(2,1)}), bf16[4,3,64,512]{3,2,1,0:T(8,128)(2,1)S(1)}, u32[]{:S(2)}, u32[]{:S(2)}) async-start(bf16[4,3,64,512]{3,2,1,0:T(8,128)(2,1)} %copy.242), calls=%async_computation.8 | async-start | bytes 1572864 | tf_op jit(solution)/shard_map/all_to_all | solution.py:163
  424.0 1.9 collective-permute-start.13
  425.3 2.0 collective-permute-start.18
  426.7 13.0 %collective-permute-start.14 = (bf16[1,192,192]{1,2,0:T(8,128)(2,1)}, bf16[1,192,192]{1,2,0:T(8,128)(2,1)}, u32[]{:S(2)}, u32[]{:S(2)}) collective-permute-start(bf16[1,192,192]{1,2,0:T(8,128)(2,1)} %dynamic-slice_convert_fusion.3), channel_id=1, source_target_pairs={{0,2},{1,3},{2,0},{3,1},{4,6},{5,7},{6,4},{7,5},{8,10},{9,11},{10,... | collective-permute-start | bytes 221192 | tf_op jit(solution)/shard_map/ppermute | solution.py:190
  433.6 27.8 %all-to-all-start.11 = ((bf16[4,3,64,512]{3,2,1,0:T(8,128)(2,1)}), bf16[4,3,64,512]{3,2,1,0:T(8,128)(2,1)}, u32[]{:S(2)}, u32[]{:S(2)}) async-start(bf16[4,3,64,512]{3,2,1,0:T(8,128)(2,1)} %copy-done.8), calls=%async_computation.11 | async-start | bytes 1572864 | tf_op jit(solution)/shard_map/all_to_all | solution.py:163
  438.9 4.7 collective-permute-start.19
  440.7 4.7 collective-permute-start.15
  444.6 4.7 collective-permute-start.20
  445.4 8.4 %collective-permute-start.16 = (bf16[1,192,192]{1,2,0:T(8,128)(2,1)S(1)}, bf16[1,192,192]{1,2,0:T(8,128)(2,1)S(1)}, u32[]{:S(2)}, u32[]{:S(2)}) collective-permute-start(bf16[1,192,192]{1,2,0:T(8,128)(2,1)S(1)} %bitcast.289), channel_id=1, source_target_pairs={{0,8},{4,12},{8,0},{12,4},{16,24},{20,28},{24,16},{28,20},{1,9},{5... | collective-permute-start | bytes 221192 | tf_op jit(solution)/shard_map/ppermute | solution.py:190
  449.3 9.9 %collective-permute-start.21 = (bf16[1,192,192]{1,2,0:T(8,128)(2,1)S(1)}, bf16[1,192,192]{1,2,0:T(8,128)(2,1)S(1)}, u32[]{:S(2)}, u32[]{:S(2)}) collective-permute-start(bf16[1,192,192]{1,2,0:T(8,128)(2,1)S(1)} %bitcast.292), channel_id=1, source_target_pairs={{0,8},{4,12},{8,0},{12,4},{16,24},{20,28},{24,16},{28,20},{1,9},{5... | collective-permute-start | bytes 221192 | tf_op jit(solution)/shard_map/ppermute | solution.py:190
  454.6 23.6 %collective-permute-start.17 = (bf16[2,192,192]{1,2,0:T(8,128)(2,1)}, bf16[2,192,192]{1,2,0:T(8,128)(2,1)}, u32[]{:S(2)}, u32[]{:S(2)}) collective-permute-start(bf16[2,192,192]{1,2,0:T(8,128)(2,1)} %maximum_select_fusion.5), channel_id=1, source_target_pairs={{0,16},{4,20},{8,24},{12,28},{16,0},{20,4},{24,8},{28,12},{1,17},{... | collective-permute-start | bytes 442376 | tf_op jit(solution)/shard_map/ppermute | solution.py:190
  459.9 24.5 %collective-permute-start.22 = (bf16[2,192,192]{1,2,0:T(8,128)(2,1)}, bf16[2,192,192]{1,2,0:T(8,128)(2,1)}, u32[]{:S(2)}, u32[]{:S(2)}) collective-permute-start(bf16[2,192,192]{1,2,0:T(8,128)(2,1)} %maximum_select_fusion.7), channel_id=1, source_target_pairs={{0,16},{4,20},{8,24},{12,28},{16,0},{20,4},{24,8},{28,12},{1,17},{... | collective-permute-start | bytes 442376 | tf_op jit(solution)/shard_map/ppermute | solution.py:190
  461.3 33.3 %all-to-all-start.10 = ((bf16[4,3,64,512]{3,2,1,0:T(8,128)(2,1)}), bf16[4,3,64,512]{3,2,1,0:T(8,128)(2,1)}, u32[]{:S(2)}, u32[]{:S(2)}) async-start(bf16[4,3,64,512]{3,2,1,0:T(8,128)(2,1)} %copy-done.7), calls=%async_computation.10 | async-start | bytes 1572864 | tf_op jit(solution)/shard_map/all_to_all | solution.py:163
  465.5 123.2 %all-reduce.5.cloned.1.call-start = ((), (), s32[]{:S(2)}) async-start(), calls=%async_computation.25 | async-start | bytes 3244032 | tf_op jit(solution)/shard_map/psum | solution.py:185
  (51 other events, 332.6 us)
Sparse Core Ops, SparseCore 0:
  14.5 20.1 all-gather.12
  36.8 17.4 all-gather.10
  56.4 17.4 all-gather.14
  75.3 17.4 all-gather.16
  94.2 30.7 all-gather.18
  126.4 20.7 all-gather.20
  204.8 68.8 all-gather.22
  276.2 24.0 reduce-scatter.3
  303.5 29.1 reduce-scatter.7
  338.6 41.2 reduce-scatter.5
  498.4 90.3 all-reduce.4

commit v3 on v2

--- a/solution.py
+++ b/solution.py
@@ -246,27 +246,37 @@
 
     gains = lax.all_gather(jnp.stack([attn_gain, mlp_gain]), "dp", axis=1, tiled=True)
     local_qkv = w_qkv.reshape(-1, 3, CHUNKS, part)
-    weights_qkv = [gathered(local_qkv[:, :, i].reshape(-1, 3 * part)) for i in range(CHUNKS)]
-    weight_out, weight_in, weight_down = gathered(w_out), gathered(w_in), gathered(w_mlp_out)
+    weights_qkv = []
+    for i in range(CHUNKS):
+        weights_qkv.append(gathered(local_qkv[:, :, i].reshape(-1, 3 * part)))
+    weight_out = gathered(w_out)
+    weight_in = gathered(w_in)
+    weight_down = gathered(w_mlp_out)
+    offsets = by_group(block_offsets[0])
     first_gain = gains[0].astype(jnp.float32)
     second_gain = gains[1].astype(jnp.float32)
 
     normed = layer_norm(inputs, first_gain).astype(jnp.bfloat16)
+    normed_next = normed
     kept, lows = [], []
     for i in range(CHUNKS):
-        packed = product(weights_qkv[i], normed, 0, 1).reshape(3, GROUPS, HEAD_DIM, t)
+        packed = product(weights_qkv[i], normed_next, 0, 1).reshape(3, GROUPS, HEAD_DIM, t)
         queries = rotate(packed[0], cosine, sine).astype(jnp.bfloat16) * HEAD_DIM**-0.5
         keys = rotate(packed[1], cosine, sine).astype(jnp.bfloat16)
         values = packed[2].astype(jnp.bfloat16)
-        own = exchange(jnp.stack([queries, keys, values], axis=1))
+        sent, normed_next = lax.optimization_barrier(
+            (jnp.stack([queries, keys, values], axis=1), normed_next)
+        )
+        own = exchange(sent)
+        if i == 0:
+            own, offsets = lax.optimization_barrier((own, offsets))
         others = [across(own[:, 1:], by) for by in range(1, m)]
         out, low, total = attend(own, others)
         lows.append(exchange(low).reshape(part, t))
         kept.append((own, others, out, total))
     attended = jnp.concatenate(lows, axis=0)
     normed_here = lax.all_gather(normed, "ctx", axis=0, axis_index_groups=alike())
-    offsets = by_group(block_offsets[0])[:, 0]
-    cosine_here, sine_here = tables((offsets[:, None] + steps).astype(jnp.float32))
+    cosine_here, sine_here = tables((offsets + steps).astype(jnp.float32))
 
     residual = inputs + product(attended, weight_out, 0, 0)
     mlp_normed = layer_norm(residual, second_gain).astype(jnp.bfloat16)
@@ -276,6 +286,9 @@
 
     upstream_low = cotangent[0]
     upstream = upstream_low.astype(jnp.float32)
+    grad_down = product(joined, upstream_low, 0, 0).astype(jnp.bfloat16)
+    upstream_low, grad_down = lax.optimization_barrier((upstream_low, grad_down))
+    total_down = reduced(grad_down)
     grad_joined = product(upstream_low, weight_down, 1, 1)
     _, glu_pull = jax.vjp(lambda packed_in: geglu(packed_in, FF), up_gate)
     grad_up_gate = glu_pull(grad_joined)[0].astype(jnp.bfloat16)
@@ -288,7 +301,6 @@
         .astype(jnp.bfloat16)
         .reshape(CHUNKS, GROUPS, HEAD_DIM, t)
     )
-    total_down = reduced(product(joined, upstream_low, 0, 0))
     total_in = reduced(product(mlp_normed, grad_up_gate, 0, 0))
     total_out = reduced(product(attended, residual_low, 1, 0))
 
@@ -296,7 +308,29 @@
     for i in range(CHUNKS):
         ups.append(exchange(grad_attended[i]))
     grad_normed = 0.0
-    totals_qkv, packs, grads = [], [], []
+    totals_qkv, packs, grads, parts = [], [], [], []
+
+    def finish(query_grad, own_grad, moved):
+        sums = own_grad.astype(jnp.float32)
+        for grad in moved:
+            sums = sums + grad.astype(jnp.float32)
+        packed = jnp.stack(
+            [
+                unrotate(query_grad, cosine_here, sine_here),
+                unrotate(sums[:, 0], cosine_here, sine_here),
+                sums[:, 1],
+            ],
+            axis=1,
+        ).astype(jnp.bfloat16)
+        heads_grad = lax.dot_general(
+            normed_here,
+            packed.reshape(GROUPS, 3 * HEAD_DIM, t),
+            (((0, 1), (0, 2)), ((), ())),
+            preferred_element_type=jnp.float32,
+        )
+        packs.append(packed)
+        grads.append(heads_grad)
+
     for i in range(CHUNKS):
         own, others, out, total = kept[i]
         if i > 1:
@@ -304,26 +338,14 @@
                 (ups[i], packs[i - 2], grads[i - 2])
             )
         query_grad, own_grad, *other_grads = attend_back(own, others, ups[i], out, total)
-        sums = own_grad.astype(jnp.float32)
         moved = [across(grad, -by) for by, grad in zip(range(1, m), other_grads)]
-        for grad in moved:
-            sums = sums + grad.astype(jnp.float32)
-        grad_packed = jnp.stack(
-            [
-                unrotate(query_grad, cosine_here, sine_here),
-                unrotate(sums[:, 0], cosine_here, sine_here),
-                sums[:, 1],
-            ],
-            axis=1,
-        ).astype(jnp.bfloat16)
-        packs.append(grad_packed)
-        heads_grad = lax.dot_general(
-            normed_here,
-            grad_packed.reshape(GROUPS, 3 * HEAD_DIM, t),
-            (((0, 1), (0, 2)), ((), ())),
-            preferred_element_type=jnp.float32,
-        )
-        grads.append(heads_grad)
+        if i > 0:
+            if i > 1:
+                parts[-1], query_grad = lax.optimization_barrier((parts[-1], query_grad))
+            finish(*parts[-1])
+        parts.append((query_grad, own_grad, moved))
+    parts[-1], grads[-1] = lax.optimization_barrier((parts[-1], grads[-1]))
+    finish(*parts[-1])
     for i in range(CHUNKS):
         back = exchange(packs[i])
         totals_qkv.append(reduced_heads(grads[i]))
@@ -335,11 +357,13 @@
     tokens_grad = (grad_residual + grad_inputs_norm)[None]
 
     gain_rows = attn_gain.shape[0]
-    gain_parts = lax.all_gather(jnp.stack([grad_gain_one, grad_gain_two]), ("ctx", "dp"))
-    gain_parts = lax.dynamic_slice_in_dim(
-        gain_parts, lax.axis_index("dp") * gain_rows, gain_rows, 2
-    )
-    gain_sums = jnp.sum(gain_parts, axis=0)
+    gain_sums = jnp.stack([grad_gain_one, grad_gain_two])
+    for axis in ("dp", "ctx"):
+        bit = 1
+        while bit < lax.axis_size(axis):
+            gain_sums = gain_sums + swapped(gain_sums, axis, bit)
+            bit *= 2
+    gain_sums = lax.dynamic_slice_in_dim(gain_sums, lax.axis_index("dp") * gain_rows, gain_rows, 1)
     return (
         mixed,
         tokens_grad,

time: 611 us -> 659 us (1.079)
  waiting for transfers between devices: 168 us -> 256 us
  blocking collectives: 47.2 us -> 6.02 us
  starting transfers between devices: 82.1 us -> 89.6 us
    all_gather x1 -> x0, blocking collectives: 41.2 us -> none  [layer(): lax.all_gather(jnp.stack([grad_gain_one, grad_gain_two]), ('ctx', 'dp'))]
    ppermute x17 -> x22, waiting for transfers between devices: 33.1 us -> 63.5 us  [swapped(): return lax.ppermute(values, axis, [(i, i ^ bit) for i in range(count)])]
    all_gather x1, waiting for transfers between devices: 0.01 us -> 29.7 us  [layer(): lax.all_gather(normed, 'ctx', axis=0, axis_index_groups=alike())]
    psum x1, waiting for transfers between devices: 42.4 us -> 68.5 us  [reduced(): return lax.psum(part, 'ctx').astype(jnp.float32)]
    all_gather x6, waiting for transfers between devices: 25.6 us -> 39.6 us  [gathered(): return lax.all_gather(value, 'dp', axis=0, tiled=True)]
    all_to_all x12, waiting for transfers between devices: 65.9 us -> 53.2 us  [exchange(): return lax.all_to_all(values, 'ctx', 0, 0, axis_index_groups=alike())]
    ppermute x17 -> x22, starting transfers between devices: 22 us -> 30.6 us  [swapped(): return lax.ppermute(values, axis, [(i, i ^ bit) for i in range(count)])]
    dot_general x15, matrix products: 52 us -> 44.8 us  [product(): lax.dot_general(left, right, (((left_dim,), (right_dim,)), ((), ())), pre...]
  transfers between devices with their start and end apart: 46 -> 51, of which waited for: 19 -> 23; matrix products, arithmetic and copies ran while one was open for 23% -> 19% of each run, Pallas kernels for 22% -> 20%
where the time goes in v3:
time: 659 us; the launch traced here: 648 us
  waiting for transfers between devices  256 us (39%)
  Pallas kernels  130 us (20%)
  starting transfers between devices  89.6 us (14%)
  local copies, waits for them, and re-layouts  57.8 us (9%)
  matrix products  51.3 us (8%)
  other arithmetic  40.2 us (6%)
  between operations  16.6 us (3%)
    pallas_call x3, Pallas kernels, attend_back(): pl.pallas_call(functools.partial(backward_kernel, m), out_shape=(jax.Shap...  76.1 us
    psum x1, waiting for transfers between devices, reduced(): return lax.psum(part, 'ctx').astype(jnp.float32)  68.5 us
    ppermute x22, waiting for transfers between devices, swapped(): return lax.ppermute(values, axis, [(i, i ^ bit) for i in range(count)])  63.5 us
    pallas_call x3, Pallas kernels, attend(): pl.pallas_call(functools.partial(forward_kernel, m), out_shape=(jax.Shape...  54.2 us
    all_to_all x12, waiting for transfers between devices, exchange(): return lax.all_to_all(values, 'ctx', 0, 0, axis_index_groups=alike())  53.2 us
    all_to_all x12, starting transfers between devices, exchange(): return lax.all_to_all(values, 'ctx', 0, 0, axis_index_groups=alike())  50.4 us
    dot_general x15, matrix products, product(): lax.dot_general(left, right, (((left_dim,), (right_dim,)), ((), ())), pre...  44.8 us
    all_gather x6, waiting for transfers between devices, gathered(): return lax.all_gather(value, 'dp', axis=0, tiled=True)  39.6 us
  transfers between devices with their start and end apart: 51, of which 23 were waited for; matrix products, arithmetic and copies ran while one was open for 19% of the time, Pallas kernels for 20%

profile of v3, /device:TPU:0, one launch (start us, length us, event | category | flops | bytes accessed | tf_op | source)
XLA Modules:
  0.0 648.2 jit_solution(9346801703352221512)
XLA Ops:
  9.4 4.2 slice_reduce_fusion
  17.3 6.0 all-gather
  25.9 8.8 %all-gather.9.cloned.1.call-done = bf16[768,768]{1,0:T(8,128)(2,1)} async-done(((bf16[192,768]{1,0:T(8,128)(2,1)}), bf16[768,768]{1,0:T(8,128)(2,1)}) %all-gather.9.cloned.1.call-update) | async-done | bytes 1179664 | tf_op jit(solution)/shard_map/all_gather | solution.py:180
  37.7 16.6 %all-gather.11.cloned.1.call-done = bf16[768,768]{1,0:T(8,128)(2,1)} async-done(((bf16[192,768]{1,0:T(8,128)(2,1)}), bf16[768,768]{1,0:T(8,128)(2,1)}) %all-gather.11.cloned.1.call-update) | async-done | bytes 1179664 | tf_op jit(solution)/shard_map/all_gather | solution.py:180
  59.6 14.3 %all-gather.13.cloned.1.call-done = bf16[768,768]{1,0:T(8,128)(2,1)} async-done(((bf16[192,768]{1,0:T(8,128)(2,1)}), bf16[768,768]{1,0:T(8,128)(2,1)}) %all-gather.13.cloned.1.call-update) | async-done | bytes 1179664 | tf_op jit(solution)/shard_map/all_gather | solution.py:180
  83.7 4.6 all-to-all-start.4
  89.2 19.5 %all-to-all-done.4.own = bf16[4,3,64,512]{3,2,1,0:T(8,128)(2,1)S(1)} async-done(((bf16[4,3,64,512]{3,2,1,0:T(8,128)(2,1)}), bf16[4,3,64,512]{3,2,1,0:T(8,128)(2,1)S(1)}, u32[]{:S(2)}, u32[]{:S(2)}) %all-to-all-start.4) | async-done | bytes 786464 | tf_op jit(solution)/shard_map/all_to_all | solution.py:163
  108.8 3.5 all-to-all-start.2
  113.2 18.7 %all-to-all-done.2.own = bf16[4,3,64,512]{3,2,1,0:T(8,128)(2,1)S(1)} async-done(((bf16[4,3,64,512]{3,2,1,0:T(8,128)(2,1)}), bf16[4,3,64,512]{3,2,1,0:T(8,128)(2,1)S(1)}, u32[]{:S(2)}, u32[]{:S(2)}) %all-to-all-start.2) | async-done | bytes 786464 | tf_op jit(solution)/shard_map/all_to_all | solution.py:163
  131.9 3.5 all-to-all-start
  140.0 7.9 %collective-permute-done = s32[1,1]{0,1:T(1,128)} collective-permute-done((s32[1,1]{0,1:T(1,128)}, s32[1,1]{0,1:T(1,128)}, u32[]{:S(2)}, u32[]{:S(2)}) %collective-permute-start) | collective-permute-done | bytes 36 | tf_op jit(solution)/shard_map/ppermute | solution.py:190
  148.7 4.5 collective-permute-start.1
  158.8 18.1 %attend.5 = (f32[4,64,512]{2,1,0:T(8,128)}, bf16[4,64,512]{2,1,0:T(8,128)(2,1)}, f32[4,1,512]{2,1,0:T(1,128)}) custom-call(bf16[4,3,64,512]{3,2,1,0:T(8,128)(2,1)} %copy-done.13, bf16[4,2,64,512]{3,2,1,0:T(8,128)(2,1)} %copy-done.62), custom_call_target="tpu_custom_call" | custom-call | flops 8589934592 | bytes 2000000 | tf_op jit(solution)/shard_map/attend/pallas_call | solution.py:90
  176.8 3.7 all-to-all-start.5
  180.5 18.1 %attend.4 = (f32[4,64,512]{2,1,0:T(8,128)}, bf16[4,64,512]{2,1,0:T(8,128)(2,1)}, f32[4,1,512]{2,1,0:T(1,128)}) custom-call(bf16[4,3,64,512]{3,2,1,0:T(8,128)(2,1)} %copy-done.14, bf16[4,2,64,512]{3,2,1,0:T(8,128)(2,1)} %collective-permute-done.3.rest_0_), custom_call_target="tpu_custom_call" | custom-call | flops 8589934592 | bytes 2000000 | tf_op jit(solution)/shard_map/attend/pallas_call | solution.py:90
  198.6 5.1 all-to-all-start.3
  203.7 18.1 %attend.3 = (f32[4,64,512]{2,1,0:T(8,128)}, bf16[4,64,512]{2,1,0:T(8,128)(2,1)}, f32[4,1,512]{2,1,0:T(1,128)}) custom-call(bf16[4,3,64,512]{3,2,1,0:T(8,128)(2,1)} %copy-done.15, bf16[4,2,64,512]{3,2,1,0:T(8,128)(2,1)} %collective-permute-done.2.rest_0_), custom_call_target="tpu_custom_call" | custom-call | flops 8589934592 | bytes 2000000 | tf_op jit(solution)/shard_map/attend/pallas_call | solution.py:90
  221.8 5.1 all-to-all-start.1
  228.6 5.0 all-to-all-done.1
  236.9 4.3 fusion.106
  241.2 6.0 multiply_convert_fusion
  249.5 5.6 fusion.27
  263.5 29.7 %all-gather.21.cloned.1.call-done = bf16[4,512,768]{2,1,0:T(8,128)(2,1)} async-done(((bf16[1,512,768]{2,1,0:T(8,128)(2,1)}), bf16[4,512,768]{2,1,0:T(8,128)(2,1)}) %all-gather.21.cloned.1.call-update) | async-done | bytes 3145744 | tf_op jit(solution)/shard_map/all_gather | solution.py:278
  293.2 4.7 copy.286
  302.6 3.4 all-to-all-start.7
  306.9 6.4 convolution_convert_fusion
  313.3 3.5 fusion.24
  316.8 5.0 all-to-all-start.9
  321.9 25.3 %attend_back.3 = (f32[4,64,512]{2,1,0:T(8,128)}, bf16[4,2,64,512]{3,2,1,0:T(8,128)(2,1)}, bf16[4,2,64,512]{3,2,1,0:T(8,128)(2,1)}) custom-call(bf16[4,3,64,512]{3,2,1,0:T(8,128)(2,1)} %copy-done.15, bf16[4,2,64,512]{3,2,1,0:T(8,128)(2,1)} %collective-permute-done.2.rest_0_, bf16[4,64,512]{2,1,0:T(8,128)(2,1)} %copy-done.35, ...), custom_call_target="tpu_custom_call" | custom-call | flops 21474836480 | bytes 4000000 | tf_op jit(solution)/shard_map/attend_back/pallas_call | solution.py:145
  349.7 5.3 all-to-all-start.6
  355.1 25.3 %attend_back.4 = (f32[4,64,512]{2,1,0:T(8,128)}, bf16[4,2,64,512]{3,2,1,0:T(8,128)(2,1)}, bf16[4,2,64,512]{3,2,1,0:T(8,128)(2,1)}) custom-call(bf16[4,3,64,512]{3,2,1,0:T(8,128)(2,1)} %copy-done.14, bf16[4,2,64,512]{3,2,1,0:T(8,128)(2,1)} %collective-permute-done.3.rest_0_, bf16[4,64,512]{2,1,0:T(8,128)(2,1)} %copy-done.36, ...), custom_call_target="tpu_custom_call" | custom-call | flops 21474836480 | bytes 4000000 | tf_op jit(solution)/shard_map/attend_back/pallas_call | solution.py:145
  389.7 25.5 %attend_back.5 = (f32[4,64,512]{2,1,0:T(8,128)}, bf16[4,2,64,512]{3,2,1,0:T(8,128)(2,1)}, bf16[4,2,64,512]{3,2,1,0:T(8,128)(2,1)}) custom-call(bf16[4,3,64,512]{3,2,1,0:T(8,128)(2,1)} %copy-done.13, bf16[4,2,64,512]{3,2,1,0:T(8,128)(2,1)} %copy-done.62, bf16[4,64,512]{2,1,0:T(8,128)(2,1)} %copy-done.34, f32[4,64,512]{2,1,0:T(8,128)} %get-tuple-element.69.rest_2_, ...), custom_call_target="tpu_custom_call" | custom-call | flops 21474836480 | bytes 4000000 | tf_op jit(solution)/shard_map/attend_back/pallas_call | solution.py:145
  428.4 3.7 collective-permute-done.14
  433.9 3.0 collective-permute-done.15
  440.9 4.2 all-to-all-start.8
  451.0 21.3 %collective-permute-done.17 = bf16[2,192,192]{1,2,0:T(8,128)(2,1)S(1)} collective-permute-done((bf16[2,192,192]{1,2,0:T(8,128)(2,1)S(1)}, bf16[2,192,192]{1,2,0:T(8,128)(2,1)S(1)}, u32[]{:S(2)}, u32[]{:S(2)}) %collective-permute-start.17) | collective-permute-done | bytes 147488 | tf_op jit(solution)/shard_map/ppermute | solution.py:190
  481.8 3.5 all-to-all-start.10
  487.7 3.5 collective-permute-done.24
  493.4 3.2 collective-permute-done.25
  498.7 7.6 %all-to-all-done.10 = bf16[4,3,64,512]{3,2,1,0:T(8,128)(2,1)S(1)} async-done(((bf16[4,3,64,512]{3,2,1,0:T(8,128)(2,1)}), bf16[4,3,64,512]{3,2,1,0:T(8,128)(2,1)S(1)}, u32[]{:S(2)}, u32[]{:S(2)}) %all-to-all-start.10) | async-done | bytes 786464 | tf_op jit(solution)/shard_map/all_to_all | solution.py:163
  506.4 3.5 all-to-all-start.11
  514.8 11.2 %collective-permute-done.21 = bf16[1,192,192]{1,2,0:T(8,128)(2,1)S(1)} collective-permute-done((bf16[1,192,192]{1,2,0:T(8,128)(2,1)S(1)}, bf16[1,192,192]{1,2,0:T(8,128)(2,1)S(1)}, u32[]{:S(2)}, u32[]{:S(2)}) %collective-permute-start.21) | collective-permute-done | bytes 73760 | tf_op jit(solution)/shard_map/ppermute | solution.py:190
  526.7 4.8 collective-permute-start.22
  539.6 3.3 fusion.20
  554.2 3.0 copy.297
  557.3 4.2 collective-permute-done.11
  561.6 3.2 add_bitcast_fusion
  567.4 68.5 %all-reduce.5.cloned.1.call-done = (bf16[192,768]{1,0:T(8,128)(2,1)}, bf16[192,2304]{1,0:T(8,128)(2,1)}, bf16[288,768]{1,0:T(8,128)(2,1)}) async-done(((bf16[192,768]{1,0:T(8,128)(2,1)}, bf16[192,2304]{1,0:T(8,128)(2,1)}, bf16[288,768]{1,0:T(8,128)(2,1)}), (bf16[192,768]{1,0:T(8,128)(2,1)}, bf16[192,2304]{1,0:T(8,128)(2,1)}, bf16[288,768]{1,0:T(8,128)(2,1)})) %all-reduce.5.cloned.1.call-update) | async-done | bytes 1622032 | tf_op jit(solution)/shard_map/psum | solution.py:185
  (367 shorter events, 144.8 us)
Async XLA Ops:
  7.2 27.5 %all-gather.9.cloned.1.call-start = ((), (), s32[]{:S(2)}) async-start(), calls=%async_computation.15 | async-start | bytes 1474560 | tf_op jit(solution)/shard_map/all_gather | solution.py:180
  14.4 39.9 %all-gather.11.cloned.1.call-start = ((), (), s32[]{:S(2)}) async-start(), calls=%async_computation.16 | async-start | bytes 1474560 | tf_op jit(solution)/shard_map/all_gather | solution.py:180
  15.2 58.7 %all-gather.13.cloned.1.call-start = ((), (), s32[]{:S(2)}) async-start(), calls=%async_computation.17 | async-start | bytes 1474560 | tf_op jit(solution)/shard_map/all_gather | solution.py:180
  16.1 212.6 %all-gather.15.cloned.1.call-start = ((), (), s32[]{:S(2)}) async-start(), calls=%async_computation.18 | async-start | bytes 1474560 | tf_op jit(solution)/shard_map/all_gather | solution.py:180
  16.7 219.6 %all-gather.17.cloned.1.call-start = ((), (), s32[]{:S(2)}) async-start(), calls=%async_computation.19 | async-start | bytes 4423680 | tf_op jit(solution)/shard_map/all_gather | solution.py:180
  83.7 25.1 %all-to-all-start.4 = ((bf16[4,3,64,512]{3,2,1,0:T(8,128)(2,1)}), bf16[4,3,64,512]{3,2,1,0:T(8,128)(2,1)S(1)}, u32[]{:S(2)}, u32[]{:S(2)}) async-start(bf16[4,3,64,512]{3,2,1,0:T(8,128)(2,1)} %pad_maximum_fusion.2), calls=%async_computation.4 | async-start | bytes 1572864 | tf_op jit(solution)/shard_map/all_to_all | solution.py:163
  108.8 23.1 %all-to-all-start.2 = ((bf16[4,3,64,512]{3,2,1,0:T(8,128)(2,1)}), bf16[4,3,64,512]{3,2,1,0:T(8,128)(2,1)S(1)}, u32[]{:S(2)}, u32[]{:S(2)}) async-start(bf16[4,3,64,512]{3,2,1,0:T(8,128)(2,1)} %copy.248), calls=%async_computation.2 | async-start | bytes 1572864 | tf_op jit(solution)/shard_map/all_to_all | solution.py:163
  131.9 25.4 %all-to-all-start = ((bf16[4,3,64,512]{3,2,1,0:T(8,128)(2,1)}), bf16[4,3,64,512]{3,2,1,0:T(8,128)(2,1)S(1)}, u32[]{:S(2)}, u32[]{:S(2)}) async-start(bf16[4,3,64,512]{3,2,1,0:T(8,128)(2,1)} %copy.241), calls=%async_computation | async-start | bytes 1572864 | tf_op jit(solution)/shard_map/all_to_all | solution.py:163
  135.4 114.1 %all-gather.19.cloned.1.call-start = ((), (), s32[]{:S(2)}) async-start(), calls=%async_computation.20 | async-start | bytes 2211840 | tf_op jit(solution)/shard_map/all_gather | solution.py:180
  136.5 21.4 %collective-permute-start.4 = (bf16[4,2,64,512]{3,2,1,0:T(8,128)(2,1)}, bf16[4,2,64,512]{3,2,1,0:T(8,128)(2,1)S(1)}, u32[]{:S(2)}, u32[]{:S(2)}) collective-permute-start(bf16[4,2,64,512]{3,2,1,0:T(8,128)(2,1)} %slice.260), channel_id=1, source_target_pairs={{0,4},{4,0},{8,12},{12,8},{16,20},{20,16},{24,28},{28,24},{1,5},{5... | collective-permute-start | bytes 1572872 | tf_op jit(solution)/shard_map/ppermute | solution.py:176
  138.0 9.9 %collective-permute-start = (s32[1,1]{0,1:T(1,128)}, s32[1,1]{0,1:T(1,128)}, u32[]{:S(2)}, u32[]{:S(2)}) collective-permute-start(s32[1,1]{0,1:T(1,128)} %bitcast.14), channel_id=1, source_target_pairs={{0,8},{4,12},{8,0},{12,4},{16,24},{20,28},{24,16},{28,20},{1,9},{5... | collective-permute-start | bytes 20 | tf_op jit(solution)/shard_map/ppermute | solution.py:190
  148.7 6.5 %collective-permute-start.1 = (s32[2,1]{0,1:T(1,128)S(1)}, s32[2,1]{0,1:T(1,128)S(1)}, u32[]{:S(2)}, u32[]{:S(2)}) collective-permute-start(s32[2,1]{0,1:T(1,128)S(1)} %broadcast_select_fusion), channel_id=1, source_target_pairs={{0,16},{4,20},{8,24},{12,28},{16,0},{20,4},{24,8},{28,12},{1,17},{... | collective-permute-start | bytes 32 | tf_op jit(solution)/shard_map/ppermute | solution.py:190
  155.8 24.8 %collective-permute-start.3 = (bf16[4,2,64,512]{3,2,1,0:T(8,128)(2,1)S(1)}, bf16[4,2,64,512]{3,2,1,0:T(8,128)(2,1)}, u32[]{:S(2)}, u32[]{:S(2)}) collective-permute-start(bf16[4,2,64,512]{3,2,1,0:T(8,128)(2,1)S(1)} %slice.251), channel_id=1, source_target_pairs={{0,4},{4,0},{8,12},{12,8},{16,20},{20,16},{24,28},{28,24},{1,5},{5... | collective-permute-start | bytes 1572872 | tf_op jit(solution)/shard_map/ppermute | solution.py:176
  157.4 46.3 %collective-permute-start.2 = (bf16[4,2,64,512]{3,2,1,0:T(8,128)(2,1)S(1)}, bf16[4,2,64,512]{3,2,1,0:T(8,128)(2,1)}, u32[]{:S(2)}, u32[]{:S(2)}) collective-permute-start(bf16[4,2,64,512]{3,2,1,0:T(8,128)(2,1)S(1)} %slice.189), channel_id=1, source_target_pairs={{0,4},{4,0},{8,12},{12,8},{16,20},{20,16},{24,28},{28,24},{1,5},{5... | collective-permute-start | bytes 1572872 | tf_op jit(solution)/shard_map/ppermute | solution.py:176
  176.8 21.8 %all-to-all-start.5 = ((bf16[4,64,512]{2,1,0:T(8,128)(2,1)}), bf16[4,64,512]{2,1,0:T(8,128)(2,1)S(1)}, u32[]{:S(2)}, u32[]{:S(2)}) async-start(bf16[4,64,512]{2,1,0:T(8,128)(2,1)} %get-tuple-element.54), calls=%async_computation.5 | async-start | bytes 524288 | tf_op jit(solution)/shard_map/all_to_all | solution.py:163
  198.6 23.2 %all-to-all-start.3 = ((bf16[4,64,512]{2,1,0:T(8,128)(2,1)}), bf16[4,64,512]{2,1,0:T(8,128)(2,1)S(1)}, u32[]{:S(2)}, u32[]{:S(2)}) async-start(bf16[4,64,512]{2,1,0:T(8,128)(2,1)} %get-tuple-element.51), calls=%async_computation.3 | async-start | bytes 524288 | tf_op jit(solution)/shard_map/all_to_all | solution.py:163
  221.8 11.9 %all-to-all-start.1 = ((bf16[4,64,512]{2,1,0:T(8,128)(2,1)}), bf16[4,64,512]{2,1,0:T(8,128)(2,1)S(1)}, u32[]{:S(2)}, u32[]{:S(2)}) async-start(bf16[4,64,512]{2,1,0:T(8,128)(2,1)} %get-tuple-element.48), calls=%async_computation.1 | async-start | bytes 524288 | tf_op jit(solution)/shard_map/all_to_all | solution.py:163
  226.9 66.3 %all-gather.21.cloned.1.call-start = ((), (), s32[]{:S(2)}) async-start(), calls=%async_computation.21 | async-start | bytes 3932160 | tf_op jit(solution)/shard_map/all_gather | solution.py:278
  228.2 317.9 %reduce-scatter.4.cloned.1.call-start = ((), (), s32[]{:S(2)}) async-start(), calls=%async_computation.22 | async-start | bytes 1474560 | tf_op jit(solution)/shard_map/reduce_scatter | solution.py:184
  262.6 283.5 %reduce-scatter.8.cloned.1.call-start = ((), (), s32[]{:S(2)}) async-start(), calls=%async_computation.24 | async-start | bytes 2211840 | tf_op jit(solution)/shard_map/reduce_scatter | solution.py:184
  302.6 14.2 %all-to-all-start.7 = ((bf16[4,64,512]{2,1,0:T(8,128)(2,1)}), bf16[4,64,512]{2,1,0:T(8,128)(2,1)S(1)}, u32[]{:S(2)}, u32[]{:S(2)}) async-start(bf16[4,64,512]{2,1,0:T(8,128)(2,1)} %bitcast.44), calls=%async_computation.7 | async-start | bytes 524288 | tf_op jit(solution)/shard_map/all_to_all | solution.py:163
  306.1 240.1 %reduce-scatter.6.cloned.1.call-start = ((), (), s32[]{:S(2)}) async-start(), calls=%async_computation.23 | async-start | bytes 4423680 | tf_op jit(solution)/shard_map/reduce_scatter | solution.py:184
  316.8 32.9 %all-to-all-start.9 = ((bf16[4,64,512]{2,1,0:T(8,128)(2,1)}), bf16[4,64,512]{2,1,0:T(8,128)(2,1)S(1)}, u32[]{:S(2)}, u32[]{:S(2)}) async-start(bf16[4,64,512]{2,1,0:T(8,128)(2,1)} %bitcast.53), calls=%async_computation.9 | async-start | bytes 524288 | tf_op jit(solution)/shard_map/all_to_all | solution.py:163
  348.2 34.6 %collective-permute-start.5 = (bf16[4,2,64,512]{3,2,0,1:T(8,128)(2,1)S(1)}, bf16[4,2,64,512]{3,2,0,1:T(8,128)(2,1)S(1)}, u32[]{:S(2)}, u32[]{:S(2)}) collective-permute-start(bf16[4,2,64,512]{3,2,0,1:T(8,128)(2,1)S(1)} %copy.257), channel_id=1, source_target_pairs={{0,4},{4,0},{8,12},{12,8},{16,20},{20,16},{24,28},{28,24},{1,5},{5... | collective-permute-start | bytes 1572872 | tf_op jit(solution)/shard_map/ppermute | solution.py:176
  349.7 39.2 %all-to-all-start.6 = ((bf16[4,64,512]{2,1,0:T(8,128)(2,1)}), bf16[4,64,512]{2,1,0:T(8,128)(2,1)S(1)}, u32[]{:S(2)}, u32[]{:S(2)}) async-start(bf16[4,64,512]{2,1,0:T(8,128)(2,1)} %bitcast.43), calls=%async_computation.6 | async-start | bytes 524288 | tf_op jit(solution)/shard_map/all_to_all | solution.py:163
  382.2 32.9 %collective-permute-start.6 = (bf16[4,2,64,512]{3,2,0,1:T(8,128)(2,1)}, bf16[4,2,64,512]{3,2,0,1:T(8,128)(2,1)}, u32[]{:S(2)}, u32[]{:S(2)}) collective-permute-start(bf16[4,2,64,512]{3,2,0,1:T(8,128)(2,1)} %copy.262), channel_id=1, source_target_pairs={{0,4},{4,0},{8,12},{12,8},{16,20},{20,16},{24,28},{28,24},{1,5},{5... | collective-permute-start | bytes 1572872 | tf_op jit(solution)/shard_map/ppermute | solution.py:176
  415.2 57.2 %collective-permute-start.7 = (bf16[4,2,64,512]{3,2,1,0:T(8,128)(2,1)}, bf16[4,2,64,512]{3,2,1,0:T(8,128)(2,1)}, u32[]{:S(2)}, u32[]{:S(2)}) collective-permute-start(bf16[4,2,64,512]{3,2,1,0:T(8,128)(2,1)} %get-tuple-element.77), channel_id=1, source_target_pairs={{0,4},{4,0},{8,12},{12,8},{16,20},{20,16},{24,28},{28,24},{1,5},{5... | collective-permute-start | bytes 1572872 | tf_op jit(solution)/shard_map/ppermute | solution.py:176
  426.9 5.2 collective-permute-start.14
  432.1 4.7 collective-permute-start.15
  436.8 8.3 %collective-permute-start.16 = (bf16[1,192,192]{1,2,0:T(8,128)(2,1)S(1)}, bf16[1,192,192]{1,2,0:T(8,128)(2,1)S(1)}, u32[]{:S(2)}, u32[]{:S(2)}) collective-permute-start(bf16[1,192,192]{1,2,0:T(8,128)(2,1)S(1)} %bitcast.289), channel_id=1, source_target_pairs={{0,8},{4,12},{8,0},{12,4},{16,24},{20,28},{24,16},{28,20},{1,9},{5... | collective-permute-start | bytes 221192 | tf_op jit(solution)/shard_map/ppermute | solution.py:190
  440.9 40.9 %all-to-all-start.8 = ((bf16[4,3,64,512]{3,2,1,0:T(8,128)(2,1)}), bf16[4,3,64,512]{3,2,1,0:T(8,128)(2,1)}, u32[]{:S(2)}, u32[]{:S(2)}) async-start(bf16[4,3,64,512]{3,2,1,0:T(8,128)(2,1)} %copy.259), calls=%async_computation.8 | async-start | bytes 1572864 | tf_op jit(solution)/shard_map/all_to_all | solution.py:163
  445.2 27.0 %collective-permute-start.17 = (bf16[2,192,192]{1,2,0:T(8,128)(2,1)S(1)}, bf16[2,192,192]{1,2,0:T(8,128)(2,1)S(1)}, u32[]{:S(2)}, u32[]{:S(2)}) collective-permute-start(bf16[2,192,192]{1,2,0:T(8,128)(2,1)S(1)} %maximum_select_fusion.3), channel_id=1, source_target_pairs={{0,16},{4,20},{8,24},{12,28},{16,0},{20,4},{24,8},{28,12},{1,17},{... | collective-permute-start | bytes 442376 | tf_op jit(solution)/shard_map/ppermute | solution.py:190
  479.3 6.1 collective-permute-start.23
  481.4 5.5 collective-permute-start.18
  481.8 24.5 %all-to-all-start.10 = ((bf16[4,3,64,512]{3,2,1,0:T(8,128)(2,1)}), bf16[4,3,64,512]{3,2,1,0:T(8,128)(2,1)S(1)}, u32[]{:S(2)}, u32[]{:S(2)}) async-start(bf16[4,3,64,512]{3,2,1,0:T(8,128)(2,1)} %copy.264), calls=%async_computation.10 | async-start | bytes 1572864 | tf_op jit(solution)/shard_map/all_to_all | solution.py:163
  485.4 5.7 collective-permute-start.24
  487.0 5.8 collective-permute-start.19
  491.2 5.4 collective-permute-start.25
  492.8 17.4 %collective-permute-start.20 = (bf16[192,192]{0,1:T(8,128)(2,1)S(1)}, bf16[192,192]{0,1:T(8,128)(2,1)S(1)}, u32[]{:S(2)}, u32[]{:S(2)}) collective-permute-start(bf16[192,192]{0,1:T(8,128)(2,1)S(1)} %fusion.91), channel_id=1, source_target_pairs={{0,4},{4,0},{8,12},{12,8},{16,20},{20,16},{24,28},{28,24},{1,5},{5... | collective-permute-start | bytes 221192 | tf_op jit(solution)/shard_map/ppermute | solution.py:190
  496.7 15.6 %collective-permute-start.26 = (bf16[1,192,192]{1,2,0:T(8,128)(2,1)S(1)}, bf16[1,192,192]{1,2,0:T(8,128)(2,1)S(1)}, u32[]{:S(2)}, u32[]{:S(2)}) collective-permute-start(bf16[1,192,192]{1,2,0:T(8,128)(2,1)S(1)} %bitcast.286), channel_id=1, source_target_pairs={{0,8},{4,12},{8,0},{12,4},{16,24},{20,28},{24,16},{28,20},{1,9},{5... | collective-permute-start | bytes 221192 | tf_op jit(solution)/shard_map/ppermute | solution.py:190
  506.4 33.1 %all-to-all-start.11 = ((bf16[4,3,64,512]{3,2,1,0:T(8,128)(2,1)}), bf16[4,3,64,512]{3,2,1,0:T(8,128)(2,1)S(1)}, u32[]{:S(2)}, u32[]{:S(2)}) async-start(bf16[4,3,64,512]{3,2,1,0:T(8,128)(2,1)} %pad_maximum_fusion.4), calls=%async_computation.11 | async-start | bytes 1572864 | tf_op jit(solution)/shard_map/all_to_all | solution.py:163
  509.9 126.0 %all-reduce.5.cloned.1.call-start = ((), (), s32[]{:S(2)}) async-start(), calls=%async_computation.25 | async-start | bytes 3244032 | tf_op jit(solution)/shard_map/psum | solution.py:185
  510.3 15.7 %collective-permute-start.21 = (bf16[1,192,192]{1,2,0:T(8,128)(2,1)S(1)}, bf16[1,192,192]{1,2,0:T(8,128)(2,1)S(1)}, u32[]{:S(2)}, u32[]{:S(2)}) collective-permute-start(bf16[1,192,192]{1,2,0:T(8,128)(2,1)S(1)} %bitcast.292), channel_id=1, source_target_pairs={{0,8},{4,12},{8,0},{12,4},{16,24},{20,28},{24,16},{28,20},{1,9},{5... | collective-permute-start | bytes 221192 | tf_op jit(solution)/shard_map/ppermute | solution.py:190
  512.3 32.6 %collective-permute-start.27 = (bf16[2,192,192]{1,2,0:T(8,128)(2,1)S(1)}, bf16[2,192,192]{1,2,0:T(8,128)(2,1)}, u32[]{:S(2)}, u32[]{:S(2)}) collective-permute-start(bf16[2,192,192]{1,2,0:T(8,128)(2,1)S(1)} %maximum_select_fusion.7), channel_id=1, source_target_pairs={{0,16},{4,20},{8,24},{12,28},{16,0},{20,4},{24,8},{28,12},{1,17},{... | collective-permute-start | bytes 442376 | tf_op jit(solution)/shard_map/ppermute | solution.py:190
  526.7 22.3 %collective-permute-start.22 = (bf16[2,192,192]{1,2,0:T(8,128)(2,1)}, bf16[2,192,192]{1,2,0:T(8,128)(2,1)}, u32[]{:S(2)}, u32[]{:S(2)}) collective-permute-start(bf16[2,192,192]{1,2,0:T(8,128)(2,1)} %maximum_select_fusion.5), channel_id=1, source_target_pairs={{0,16},{4,20},{8,24},{12,28},{16,0},{20,4},{24,8},{28,12},{1,17},{... | collective-permute-start | bytes 442376 | tf_op jit(solution)/shard_map/ppermute | solution.py:190
  551.9 5.3 collective-permute-start.10
  557.2 4.3 collective-permute-start.11
  561.6 5.2 collective-permute-start.12
  (70 other events, 643.2 us)
Sparse Core Ops, SparseCore 0:
  14.5 20.1 all-gather.8
  36.8 17.4 all-gather.10
  56.4 17.4 all-gather.12
  75.3 17.4 all-gather.14
  94.2 30.7 all-gather.16
  140.1 18.8 all-gather.18
  229.2 63.9 all-gather.20
  295.8 24.2 reduce-scatter.3
  323.2 29.1 reduce-scatter.7
  354.8 40.3 reduce-scatter.5
  546.3 89.4 all-reduce.4

commit v4 on v3

--- a/solution.py
+++ b/solution.py
@@ -206,7 +206,7 @@
     return value
 
 
-def reduced_heads(value):
+def halved_over_dp(value):
     size = lax.axis_size("dp")
     place = lax.axis_index("dp")
     value = value.reshape(size, value.shape[0] // size, value.shape[1])
@@ -218,13 +218,20 @@
         send = lax.dynamic_index_in_dim(value, 1 - mine, 1, keepdims=False)
         value = keep + swapped(send.astype(jnp.bfloat16), "dp", bit).astype(jnp.float32)
         bit *= 2
-    value = value[0]
-    count = lax.axis_size("ctx") // GROUPS
+    return value[0]
+
+
+def summed_over_ctx(value, count):
     bit = 1
     while bit < count:
         value = value.astype(jnp.bfloat16)
         value = value.astype(jnp.float32) + swapped(value, "ctx", bit).astype(jnp.float32)
         bit *= 2
+    return value
+
+
+def reduced_heads(value):
+    value = summed_over_ctx(halved_over_dp(value), lax.axis_size("ctx") // GROUPS)
     return by_group(value.astype(jnp.bfloat16)).astype(jnp.float32)
 
 
@@ -302,11 +309,13 @@
         .reshape(CHUNKS, GROUPS, HEAD_DIM, t)
     )
     total_in = reduced(product(mlp_normed, grad_up_gate, 0, 0))
-    total_out = reduced(product(attended, residual_low, 1, 0))
-
-    ups = []
-    for i in range(CHUNKS):
-        ups.append(exchange(grad_attended[i]))
+    total_out = summed_over_ctx(
+        halved_over_dp(product(attended, residual_low, 1, 0)), lax.axis_size("ctx")
+    )
+
+    ups = [exchange(grad_attended[0])]
+    later = exchange(grad_attended[1:].transpose(1, 0, 2, 3))
+    ups += [later[:, i] for i in range(CHUNKS - 1)]
     grad_normed = 0.0
     totals_qkv, packs, grads, parts = [], [], [], []
 

time: 659 us -> 668 us (1.014)
  local copies, waits for them, and re-layouts: 57.8 us -> 65.9 us
    all_to_all x12 -> x11, waiting for transfers between devices: 53.2 us -> 105 us  [exchange(): return lax.all_to_all(values, 'ctx', 0, 0, axis_index_groups=alike())]
    all_gather x1, waiting for transfers between devices: 29.7 us -> 0.02 us  [layer(): lax.all_gather(normed, 'ctx', axis=0, axis_index_groups=alike())]
    ppermute x22 -> x27, waiting for transfers between devices: 63.5 us -> 42.6 us  [swapped(): return lax.ppermute(values, axis, [(i, i ^ bit) for i in range(count)])]
    ppermute x6, waiting for transfers between devices: 0.02 us -> 8.44 us  [across(): return lax.ppermute(values, 'ctx', pairs)]
    ppermute x22 -> x27, starting transfers between devices: 30.6 us -> 28.4 us  [swapped(): return lax.ppermute(values, axis, [(i, i ^ bit) for i in range(count)])]
    all_to_all x12 -> x11, starting transfers between devices: 50.4 us -> 49.3 us  [exchange(): return lax.all_to_all(values, 'ctx', 0, 0, axis_index_groups=alike())]
  transfers between devices with their start and end apart: 51 -> 54, of which waited for: 23 -> 21; matrix products, arithmetic and copies ran while one was open for 19% -> 20% of each run, Pallas kernels for 20% -> 20%
where the time goes in v4:
time: 668 us; the launch traced here: 657 us
  waiting for transfers between devices  259 us (39%)
  Pallas kernels  131 us (20%)
  starting transfers between devices  86.5 us (13%)
  local copies, waits for them, and re-layouts  65.9 us (10%)
  matrix products  47.2 us (7%)
  other arithmetic  45.8 us (7%)
  between operations  16.5 us (2%)
    all_to_all x11, waiting for transfers between devices, exchange(): return lax.all_to_all(values, 'ctx', 0, 0, axis_index_groups=alike())  105 us
    pallas_call x3, Pallas kernels, attend_back(): pl.pallas_call(functools.partial(backward_kernel, m), out_shape=(jax.Shap...  76.4 us
    psum x1, waiting for transfers between devices, reduced(): return lax.psum(part, 'ctx').astype(jnp.float32)  63.8 us
    pallas_call x3, Pallas kernels, attend(): pl.pallas_call(functools.partial(forward_kernel, m), out_shape=(jax.Shape...  54.2 us
    all_to_all x11, starting transfers between devices, exchange(): return lax.all_to_all(values, 'ctx', 0, 0, axis_index_groups=alike())  49.3 us
    ppermute x27, waiting for transfers between devices, swapped(): return lax.ppermute(values, axis, [(i, i ^ bit) for i in range(count)])  42.6 us
    dot_general x15, matrix products, product(): lax.dot_general(left, right, (((left_dim,), (right_dim,)), ((), ())), pre...  40.7 us
    all_gather x6, waiting for transfers between devices, gathered(): return lax.all_gather(value, 'dp', axis=0, tiled=True)  36.6 us
  transfers between devices with their start and end apart: 54, of which 21 were waited for; matrix products, arithmetic and copies ran while one was open for 20% of the time, Pallas kernels for 20%

profile of v4, /device:TPU:0, one launch (start us, length us, event | category | flops | bytes accessed | tf_op | source)
XLA Modules:
  0.0 657.1 jit_solution(229119883133471581)
XLA Ops:
  9.4 4.2 slice_reduce_fusion
  16.8 6.0 all-gather
  26.6 8.1 %all-gather.9.cloned.1.call-done = bf16[768,768]{1,0:T(8,128)(2,1)} async-done(((bf16[192,768]{1,0:T(8,128)(2,1)}), bf16[768,768]{1,0:T(8,128)(2,1)}) %all-gather.9.cloned.1.call-update) | async-done | bytes 1179664 | tf_op jit(solution)/shard_map/all_gather | solution.py:180
  40.1 14.2 %all-gather.11.cloned.1.call-done = bf16[768,768]{1,0:T(8,128)(2,1)} async-done(((bf16[192,768]{1,0:T(8,128)(2,1)}), bf16[768,768]{1,0:T(8,128)(2,1)}) %all-gather.11.cloned.1.call-update) | async-done | bytes 1179664 | tf_op jit(solution)/shard_map/all_gather | solution.py:180
  59.7 14.3 %all-gather.13.cloned.1.call-done = bf16[768,768]{1,0:T(8,128)(2,1)} async-done(((bf16[192,768]{1,0:T(8,128)(2,1)}), bf16[768,768]{1,0:T(8,128)(2,1)}) %all-gather.13.cloned.1.call-update) | async-done | bytes 1179664 | tf_op jit(solution)/shard_map/all_gather | solution.py:180
  83.7 4.6 all-to-all-start.4
  89.8 28.1 %all-to-all-done.4.own = bf16[4,3,64,512]{3,2,1,0:T(8,128)(2,1)S(1)} async-done(((bf16[4,3,64,512]{3,2,1,0:T(8,128)(2,1)}), bf16[4,3,64,512]{3,2,1,0:T(8,128)(2,1)S(1)}, u32[]{:S(2)}, u32[]{:S(2)}) %all-to-all-start.4) | async-done | bytes 786464 | tf_op jit(solution)/shard_map/all_to_all | solution.py:163
  118.0 3.6 all-to-all-start.2
  122.6 39.0 %all-to-all-done.2.own = bf16[4,3,64,512]{3,2,1,0:T(8,128)(2,1)S(1)} async-done(((bf16[4,3,64,512]{3,2,1,0:T(8,128)(2,1)}), bf16[4,3,64,512]{3,2,1,0:T(8,128)(2,1)S(1)}, u32[]{:S(2)}, u32[]{:S(2)}) %all-to-all-start.2) | async-done | bytes 786464 | tf_op jit(solution)/shard_map/all_to_all | solution.py:163
  161.6 5.5 all-to-all-start
  171.6 9.2 %collective-permute-done = s32[1,1]{0,1:T(1,128)} collective-permute-done((s32[1,1]{0,1:T(1,128)}, s32[1,1]{0,1:T(1,128)}, u32[]{:S(2)}, u32[]{:S(2)}) %collective-permute-start) | collective-permute-done | bytes 36 | tf_op jit(solution)/shard_map/ppermute | solution.py:190
  181.4 3.8 collective-permute-start.1
  185.9 7.5 %collective-permute-done.1 = s32[2,1]{0,1:T(1,128)S(1)} collective-permute-done((s32[2,1]{0,1:T(1,128)S(1)}, s32[2,1]{0,1:T(1,128)S(1)}, u32[]{:S(2)}, u32[]{:S(2)}) %collective-permute-start.1) | collective-permute-done | bytes 40 | tf_op jit(solution)/shard_map/ppermute | solution.py:190
  196.6 18.1 %attend.5 = (f32[4,64,512]{2,1,0:T(8,128)}, bf16[4,64,512]{2,1,0:T(8,128)(2,1)}, f32[4,1,512]{2,1,0:T(1,128)}) custom-call(bf16[4,3,64,512]{3,2,1,0:T(8,128)(2,1)} %copy-done.12, bf16[4,2,64,512]{3,2,1,0:T(8,128)(2,1)} %copy-done.60), custom_call_target="tpu_custom_call" | custom-call | flops 8589934592 | bytes 2000000 | tf_op jit(solution)/shard_map/attend/pallas_call | solution.py:90
  214.7 3.4 all-to-all-start.5
  218.1 18.1 %attend.4 = (f32[4,64,512]{2,1,0:T(8,128)}, bf16[4,64,512]{2,1,0:T(8,128)(2,1)}, f32[4,1,512]{2,1,0:T(1,128)}) custom-call(bf16[4,3,64,512]{3,2,1,0:T(8,128)(2,1)} %copy-done.13, bf16[4,2,64,512]{3,2,1,0:T(8,128)(2,1)} %collective-permute-done.3.rest_0_), custom_call_target="tpu_custom_call" | custom-call | flops 8589934592 | bytes 2000000 | tf_op jit(solution)/shard_map/attend/pallas_call | solution.py:90
  236.2 5.1 all-to-all-start.3
  241.2 18.1 %attend.3 = (f32[4,64,512]{2,1,0:T(8,128)}, bf16[4,64,512]{2,1,0:T(8,128)(2,1)}, f32[4,1,512]{2,1,0:T(1,128)}) custom-call(bf16[4,3,64,512]{3,2,1,0:T(8,128)(2,1)} %copy-done.14, bf16[4,2,64,512]{3,2,1,0:T(8,128)(2,1)} %collective-permute-done.2.rest_0_), custom_call_target="tpu_custom_call" | custom-call | flops 8589934592 | bytes 2000000 | tf_op jit(solution)/shard_map/attend/pallas_call | solution.py:90
  259.3 5.1 all-to-all-start.1
  265.7 5.5 all-to-all-done.1
  273.8 4.8 copy.290
  278.5 4.1 fusion.109
  282.7 6.0 multiply_convert_fusion
  292.1 5.6 fusion.27
  306.3 3.6 all-to-all-start.7
  314.4 4.1 convolution_convert_fusion
  319.8 3.6 fusion.24
  324.1 5.1 all-to-all-start.6
  329.1 25.6 %attend_back.3 = (f32[4,64,512]{2,1,0:T(8,128)}, bf16[4,2,64,512]{3,2,1,0:T(8,128)(2,1)}, bf16[4,2,64,512]{3,2,1,0:T(8,128)(2,1)}) custom-call(bf16[4,3,64,512]{3,2,1,0:T(8,128)(2,1)} %copy-done.14, bf16[4,2,64,512]{3,2,1,0:T(8,128)(2,1)} %collective-permute-done.2.rest_0_, bf16[4,64,512]{2,1,0:T(8,128)(2,1)} %copy-done.36, ...), custom_call_target="tpu_custom_call" | custom-call | flops 21474836480 | bytes 4000000 | tf_op jit(solution)/shard_map/attend_back/pallas_call | solution.py:145
  361.6 8.4 %collective-permute-done.5 = bf16[4,2,64,512]{3,2,0,1:T(8,128)(2,1)} collective-permute-done((bf16[4,2,64,512]{3,2,0,1:T(8,128)(2,1)S(1)}, bf16[4,2,64,512]{3,2,0,1:T(8,128)(2,1)}, u32[]{:S(2)}, u32[]{:S(2)}) %collective-permute-start.5) | collective-permute-done | bytes 524320 | tf_op jit(solution)/shard_map/ppermute | solution.py:176
  376.6 2.7 reshape_reshape.10
  380.9 25.6 %attend_back.4 = (f32[4,64,512]{2,1,0:T(8,128)}, bf16[4,2,64,512]{3,2,1,0:T(8,128)(2,1)}, bf16[4,2,64,512]{3,2,1,0:T(8,128)(2,1)}) custom-call(bf16[4,3,64,512]{3,2,1,0:T(8,128)(2,1)} %copy-done.13, bf16[4,2,64,512]{3,2,1,0:T(8,128)(2,1)} %collective-permute-done.3.rest_0_, bf16[4,64,512]{2,1,0:T(8,128)(2,1)} %get-tuple-element.163.rest_1_, ...), custom_call_target="tpu_custom_call" | custom-call | flops 21474836480 | bytes 4000000 | tf_op jit(solution)/shard_map/attend_back/pallas_call | solution.py:145
  413.7 2.7 collective-permute-done.14
  417.2 25.2 %attend_back.5 = (f32[4,64,512]{2,1,0:T(8,128)}, bf16[4,2,64,512]{3,2,1,0:T(8,128)(2,1)}, bf16[4,2,64,512]{3,2,1,0:T(8,128)(2,1)}) custom-call(bf16[4,3,64,512]{3,2,1,0:T(8,128)(2,1)} %copy-done.12, bf16[4,2,64,512]{3,2,1,0:T(8,128)(2,1)} %copy-done.60, bf16[4,64,512]{2,1,0:T(8,128)(2,1)} %get-tuple-element.68.rest_1_, ...), custom_call_target="tpu_custom_call" | custom-call | flops 21474836480 | bytes 4000000 | tf_op jit(solution)/shard_map/attend_back/pallas_call | solution.py:145
  445.8 5.1 all-to-all-start.8
  455.3 11.7 %collective-permute-done.16 = bf16[1,192,192]{1,2,0:T(8,128)(2,1)S(1)} collective-permute-done((bf16[1,192,192]{1,2,0:T(8,128)(2,1)S(1)}, bf16[1,192,192]{1,2,0:T(8,128)(2,1)S(1)}, u32[]{:S(2)}, u32[]{:S(2)}) %collective-permute-start.16) | collective-permute-done | bytes 73760 | tf_op jit(solution)/shard_map/ppermute | solution.py:190
  467.1 4.9 collective-permute-start.17
  475.7 2.8 convolution_bitcast_fusion.3
  490.6 4.8 all-to-all-start.9
  507.9 14.3 %all-to-all-done.9 = bf16[4,3,64,512]{3,2,1,0:T(8,128)(2,1)S(1)} async-done(((bf16[4,3,64,512]{3,2,1,0:T(8,128)(2,1)}), bf16[4,3,64,512]{3,2,1,0:T(8,128)(2,1)S(1)}, u32[]{:S(2)}, u32[]{:S(2)}) %all-to-all-start.9) | async-done | bytes 786464 | tf_op jit(solution)/shard_map/all_to_all | solution.py:163
  522.2 3.5 all-to-all-start.10
  526.8 2.9 collective-permute-start.27
  537.1 18.2 %all-to-all-done.10 = bf16[4,3,64,512]{3,2,1,0:T(8,128)(2,1)S(1)} async-done(((bf16[4,3,64,512]{3,2,1,0:T(8,128)(2,1)}), bf16[4,3,64,512]{3,2,1,0:T(8,128)(2,1)S(1)}, u32[]{:S(2)}, u32[]{:S(2)}) %all-to-all-start.10) | async-done | bytes 786464 | tf_op jit(solution)/shard_map/all_to_all | solution.py:163
  555.5 3.3 fusion.20
  569.7 3.0 copy.302
  573.4 3.7 collective-permute-done.11
  577.6 3.3 add_bitcast_fusion
  582.7 63.8 %all-reduce.5.cloned.1.call-done = (bf16[192,2304]{1,0:T(8,128)(2,1)}, bf16[288,768]{1,0:T(8,128)(2,1)}) async-done(((bf16[192,2304]{1,0:T(8,128)(2,1)}, bf16[288,768]{1,0:T(8,128)(2,1)}), (bf16[192,2304]{1,0:T(8,128)(2,1)}, bf16[288,768]{1,0:T(8,128)(2,1)})) %all-reduce.5.cloned.1.call-update) | async-done | bytes 1327120 | tf_op jit(solution)/shard_map/psum | solution.py:185
  (381 shorter events, 146.9 us)
Async XLA Ops:
  7.2 27.6 %all-gather.9.cloned.1.call-start = ((), (), s32[]{:S(2)}) async-start(), calls=%async_computation.13 | async-start | bytes 1474560 | tf_op jit(solution)/shard_map/all_gather | solution.py:180
  14.4 39.9 %all-gather.11.cloned.1.call-start = ((), (), s32[]{:S(2)}) async-start(), calls=%async_computation.14 | async-start | bytes 1474560 | tf_op jit(solution)/shard_map/all_gather | solution.py:180
  15.2 58.7 %all-gather.13.cloned.1.call-start = ((), (), s32[]{:S(2)}) async-start(), calls=%async_computation.15 | async-start | bytes 1474560 | tf_op jit(solution)/shard_map/all_gather | solution.py:180
  16.1 249.6 %all-gather.15.cloned.1.call-start = ((), (), s32[]{:S(2)}) async-start(), calls=%async_computation.16 | async-start | bytes 1474560 | tf_op jit(solution)/shard_map/all_gather | solution.py:180
  16.7 257.1 %all-gather.21.cloned.1.call-start = ((), (), s32[]{:S(2)}) async-start(), calls=%async_computation.19 | async-start | bytes 3932160 | tf_op jit(solution)/shard_map/all_gather | solution.py:285
  83.7 34.2 %all-to-all-start.4 = ((bf16[4,3,64,512]{3,2,1,0:T(8,128)(2,1)}), bf16[4,3,64,512]{3,2,1,0:T(8,128)(2,1)S(1)}, u32[]{:S(2)}, u32[]{:S(2)}) async-start(bf16[4,3,64,512]{3,2,1,0:T(8,128)(2,1)} %pad_maximum_fusion.2), calls=%async_computation.4 | async-start | bytes 1572864 | tf_op jit(solution)/shard_map/all_to_all | solution.py:163
  88.3 190.2 %all-gather.17.cloned.1.call-start = ((), (), s32[]{:S(2)}) async-start(), calls=%async_computation.17 | async-start | bytes 4423680 | tf_op jit(solution)/shard_map/all_gather | solution.py:180
  118.0 43.6 %all-to-all-start.2 = ((bf16[4,3,64,512]{3,2,1,0:T(8,128)(2,1)}), bf16[4,3,64,512]{3,2,1,0:T(8,128)(2,1)S(1)}, u32[]{:S(2)}, u32[]{:S(2)}) async-start(bf16[4,3,64,512]{3,2,1,0:T(8,128)(2,1)} %copy.250), calls=%async_computation.2 | async-start | bytes 1572864 | tf_op jit(solution)/shard_map/all_to_all | solution.py:163
  161.6 33.6 %all-to-all-start = ((bf16[4,3,64,512]{3,2,1,0:T(8,128)(2,1)}), bf16[4,3,64,512]{3,2,1,0:T(8,128)(2,1)S(1)}, u32[]{:S(2)}, u32[]{:S(2)}) async-start(bf16[4,3,64,512]{3,2,1,0:T(8,128)(2,1)} %copy.243), calls=%async_computation | async-start | bytes 1572864 | tf_op jit(solution)/shard_map/all_to_all | solution.py:163
  167.9 27.9 %collective-permute-start.4 = (bf16[4,2,64,512]{3,2,1,0:T(8,128)(2,1)}, bf16[4,2,64,512]{3,2,1,0:T(8,128)(2,1)S(1)}, u32[]{:S(2)}, u32[]{:S(2)}) collective-permute-start(bf16[4,2,64,512]{3,2,1,0:T(8,128)(2,1)} %slice.266), channel_id=1, source_target_pairs={{0,4},{4,0},{8,12},{12,8},{16,20},{20,16},{24,28},{28,24},{1,5},{5... | collective-permute-start | bytes 1572872 | tf_op jit(solution)/shard_map/ppermute | solution.py:176
  169.6 11.2 %collective-permute-start = (s32[1,1]{0,1:T(1,128)}, s32[1,1]{0,1:T(1,128)}, u32[]{:S(2)}, u32[]{:S(2)}) collective-permute-start(s32[1,1]{0,1:T(1,128)} %bitcast.14), channel_id=1, source_target_pairs={{0,8},{4,12},{8,0},{12,4},{16,24},{20,28},{24,16},{28,20},{1,9},{5... | collective-permute-start | bytes 20 | tf_op jit(solution)/shard_map/ppermute | solution.py:190
  181.4 12.0 %collective-permute-start.1 = (s32[2,1]{0,1:T(1,128)S(1)}, s32[2,1]{0,1:T(1,128)S(1)}, u32[]{:S(2)}, u32[]{:S(2)}) collective-permute-start(s32[2,1]{0,1:T(1,128)S(1)} %broadcast_select_fusion), channel_id=1, source_target_pairs={{0,16},{4,20},{8,24},{12,28},{16,0},{20,4},{24,8},{28,12},{1,17},{... | collective-permute-start | bytes 32 | tf_op jit(solution)/shard_map/ppermute | solution.py:190
  193.6 24.5 %collective-permute-start.3 = (bf16[4,2,64,512]{3,2,1,0:T(8,128)(2,1)S(1)}, bf16[4,2,64,512]{3,2,1,0:T(8,128)(2,1)}, u32[]{:S(2)}, u32[]{:S(2)}) collective-permute-start(bf16[4,2,64,512]{3,2,1,0:T(8,128)(2,1)S(1)} %slice.257), channel_id=1, source_target_pairs={{0,4},{4,0},{8,12},{12,8},{16,20},{20,16},{24,28},{28,24},{1,5},{5... | collective-permute-start | bytes 1572872 | tf_op jit(solution)/shard_map/ppermute | solution.py:176
  195.2 46.1 %collective-permute-start.2 = (bf16[4,2,64,512]{3,2,1,0:T(8,128)(2,1)S(1)}, bf16[4,2,64,512]{3,2,1,0:T(8,128)(2,1)}, u32[]{:S(2)}, u32[]{:S(2)}) collective-permute-start(bf16[4,2,64,512]{3,2,1,0:T(8,128)(2,1)S(1)} %slice.193), channel_id=1, source_target_pairs={{0,4},{4,0},{8,12},{12,8},{16,20},{20,16},{24,28},{28,24},{1,5},{5... | collective-permute-start | bytes 1572872 | tf_op jit(solution)/shard_map/ppermute | solution.py:176
  214.7 21.5 %all-to-all-start.5 = ((bf16[4,64,512]{2,1,0:T(8,128)(2,1)}), bf16[4,64,512]{2,1,0:T(8,128)(2,1)S(1)}, u32[]{:S(2)}, u32[]{:S(2)}) async-start(bf16[4,64,512]{2,1,0:T(8,128)(2,1)} %get-tuple-element.54), calls=%async_computation.5 | async-start | bytes 524288 | tf_op jit(solution)/shard_map/all_to_all | solution.py:163
  236.2 23.1 %all-to-all-start.3 = ((bf16[4,64,512]{2,1,0:T(8,128)(2,1)}), bf16[4,64,512]{2,1,0:T(8,128)(2,1)S(1)}, u32[]{:S(2)}, u32[]{:S(2)}) async-start(bf16[4,64,512]{2,1,0:T(8,128)(2,1)} %get-tuple-element.51), calls=%async_computation.3 | async-start | bytes 524288 | tf_op jit(solution)/shard_map/all_to_all | solution.py:163
  259.3 11.9 %all-to-all-start.1 = ((bf16[4,64,512]{2,1,0:T(8,128)(2,1)}), bf16[4,64,512]{2,1,0:T(8,128)(2,1)S(1)}, u32[]{:S(2)}, u32[]{:S(2)}) async-start(bf16[4,64,512]{2,1,0:T(8,128)(2,1)} %get-tuple-element.48), calls=%async_computation.1 | async-start | bytes 524288 | tf_op jit(solution)/shard_map/all_to_all | solution.py:163
  264.4 27.7 %all-gather.19.cloned.1.call-start = ((), (), s32[]{:S(2)}) async-start(), calls=%async_computation.18 | async-start | bytes 2211840 | tf_op jit(solution)/shard_map/all_gather | solution.py:180
  265.1 298.9 %reduce-scatter.5.cloned.1.call-start = ((), (), s32[]{:S(2)}) async-start(), calls=%async_computation.21 | async-start | bytes 2211840 | tf_op jit(solution)/shard_map/reduce_scatter | solution.py:184
  306.3 17.1 %all-to-all-start.7 = ((bf16[4,64,512]{2,1,0:T(8,128)(2,1)}), bf16[4,64,512]{2,1,0:T(8,128)(2,1)S(1)}, u32[]{:S(2)}, u32[]{:S(2)}) async-start(bf16[4,64,512]{2,1,0:T(8,128)(2,1)} %bitcast.46), calls=%async_computation.7 | async-start | bytes 524288 | tf_op jit(solution)/shard_map/all_to_all | solution.py:163
  309.8 254.2 %reduce-scatter.3.cloned.1.call-start = ((), (), s32[]{:S(2)}) async-start(), calls=%async_computation.20 | async-start | bytes 4423680 | tf_op jit(solution)/shard_map/reduce_scatter | solution.py:184
  314.4 42.8 %collective-permute-start.28 = (bf16[2,192,768]{2,1,0:T(8,128)(2,1)}, bf16[2,192,768]{2,1,0:T(8,128)(2,1)}, u32[]{:S(2)}, u32[]{:S(2)}) collective-permute-start(bf16[2,192,768]{2,1,0:T(8,128)(2,1)} %fusion.28), channel_id=1, source_target_pairs={{0,1},{1,0},{2,3},{3,2},{4,5},{5,4},{6,7},{7,6},{8,9},{9,8},{10,11... | collective-permute-start | bytes 1769480 | tf_op jit(solution)/shard_map/ppermute | solution.py:190
  324.1 36.7 %all-to-all-start.6 = ((bf16[4,2,64,512]{3,2,1,0:T(8,128)(2,1)}), bf16[4,2,64,512]{3,2,1,0:T(8,128)(2,1)S(1)}, u32[]{:S(2)}, u32[]{:S(2)}) async-start(bf16[4,2,64,512]{3,2,1,0:T(8,128)(2,1)} %copy.257), calls=%async_computation.6 | async-start | bytes 1048576 | tf_op jit(solution)/shard_map/all_to_all | solution.py:163
  355.8 14.2 %collective-permute-start.5 = (bf16[4,2,64,512]{3,2,0,1:T(8,128)(2,1)S(1)}, bf16[4,2,64,512]{3,2,0,1:T(8,128)(2,1)}, u32[]{:S(2)}, u32[]{:S(2)}) collective-permute-start(bf16[4,2,64,512]{3,2,0,1:T(8,128)(2,1)S(1)} %copy.261), channel_id=1, source_target_pairs={{0,4},{4,0},{8,12},{12,8},{16,20},{20,16},{24,28},{28,24},{1,5},{5... | collective-permute-start | bytes 1572872 | tf_op jit(solution)/shard_map/ppermute | solution.py:176
  360.1 52.0 %collective-permute-start.29 = (bf16[1,192,768]{2,1,0:T(8,128)(2,1)}, bf16[1,192,768]{2,1,0:T(8,128)(2,1)}, u32[]{:S(2)}, u32[]{:S(2)}) collective-permute-start(bf16[1,192,768]{2,1,0:T(8,128)(2,1)} %dynamic-slice_convert_fusion), channel_id=1, source_target_pairs={{0,2},{1,3},{2,0},{3,1},{4,6},{5,7},{6,4},{7,5},{8,10},{9,11},{10,... | collective-permute-start | bytes 884744 | tf_op jit(solution)/shard_map/ppermute | solution.py:190
  380.9 30.5 %collective-permute-start.13 = (bf16[2,192,192]{1,2,0:T(8,128)(2,1)S(1)}, bf16[2,192,192]{1,2,0:T(8,128)(2,1)S(1)}, u32[]{:S(2)}, u32[]{:S(2)}) collective-permute-start(bf16[2,192,192]{1,2,0:T(8,128)(2,1)S(1)} %bitcast.330), channel_id=1, source_target_pairs={{0,1},{1,0},{2,3},{3,2},{4,5},{5,4},{6,7},{7,6},{8,9},{9,8},{10,11... | collective-permute-start | bytes 442376 | tf_op jit(solution)/shard_map/ppermute | solution.py:190
  408.6 63.4 %collective-permute-start.6 = (bf16[4,2,64,512]{3,2,0,1:T(8,128)(2,1)}, bf16[4,2,64,512]{3,2,0,1:T(8,128)(2,1)}, u32[]{:S(2)}, u32[]{:S(2)}) collective-permute-start(bf16[4,2,64,512]{3,2,0,1:T(8,128)(2,1)} %copy.266), channel_id=1, source_target_pairs={{0,4},{4,0},{8,12},{12,8},{16,20},{20,16},{24,28},{28,24},{1,5},{5... | collective-permute-start | bytes 1572872 | tf_op jit(solution)/shard_map/ppermute | solution.py:176
  411.5 5.0 collective-permute-start.14
  413.1 41.0 %collective-permute-start.30 = (bf16[192,768]{1,0:T(8,128)(2,1)S(1)}, bf16[192,768]{1,0:T(8,128)(2,1)}, u32[]{:S(2)}, u32[]{:S(2)}) collective-permute-start(bf16[192,768]{1,0:T(8,128)(2,1)S(1)} %fusion.57), channel_id=1, source_target_pairs={{0,4},{4,0},{8,12},{12,8},{16,20},{20,16},{24,28},{28,24},{1,5},{5... | collective-permute-start | bytes 884744 | tf_op jit(solution)/shard_map/ppermute | solution.py:190
  416.5 34.5 %collective-permute-start.15 = (bf16[192,192]{0,1:T(8,128)(2,1)S(1)}, bf16[192,192]{0,1:T(8,128)(2,1)}, u32[]{:S(2)}, u32[]{:S(2)}) collective-permute-start(bf16[192,192]{0,1:T(8,128)(2,1)S(1)} %fusion.93), channel_id=1, source_target_pairs={{0,4},{4,0},{8,12},{12,8},{16,20},{20,16},{24,28},{28,24},{1,5},{5... | collective-permute-start | bytes 221192 | tf_op jit(solution)/shard_map/ppermute | solution.py:190
  442.4 36.2 %collective-permute-start.7 = (bf16[4,2,64,512]{3,2,1,0:T(8,128)(2,1)}, bf16[4,2,64,512]{3,2,1,0:T(8,128)(2,1)}, u32[]{:S(2)}, u32[]{:S(2)}) collective-permute-start(bf16[4,2,64,512]{3,2,1,0:T(8,128)(2,1)} %get-tuple-element.77), channel_id=1, source_target_pairs={{0,4},{4,0},{8,12},{12,8},{16,20},{20,16},{24,28},{28,24},{1,5},{5... | collective-permute-start | bytes 1572872 | tf_op jit(solution)/shard_map/ppermute | solution.py:176
  445.8 44.8 %all-to-all-start.8 = ((bf16[4,3,64,512]{3,2,1,0:T(8,128)(2,1)}), bf16[4,3,64,512]{3,2,1,0:T(8,128)(2,1)}, u32[]{:S(2)}, u32[]{:S(2)}) async-start(bf16[4,3,64,512]{3,2,1,0:T(8,128)(2,1)} %copy.263), calls=%async_computation.8 | async-start | bytes 1572864 | tf_op jit(solution)/shard_map/all_to_all | solution.py:163
  452.0 15.1 %collective-permute-start.16 = (bf16[1,192,192]{1,2,0:T(8,128)(2,1)S(1)}, bf16[1,192,192]{1,2,0:T(8,128)(2,1)S(1)}, u32[]{:S(2)}, u32[]{:S(2)}) collective-permute-start(bf16[1,192,192]{1,2,0:T(8,128)(2,1)S(1)} %bitcast.315), channel_id=1, source_target_pairs={{0,8},{4,12},{8,0},{12,4},{16,24},{20,28},{24,16},{28,20},{1,9},{5... | collective-permute-start | bytes 221192 | tf_op jit(solution)/shard_map/ppermute | solution.py:190
  455.2 32.4 %collective-permute-start.31 = (bf16[192,768]{1,0:T(8,128)(2,1)S(1)}, bf16[192,768]{1,0:T(8,128)(2,1)}, u32[]{:S(2)}, u32[]{:S(2)}) collective-permute-start(bf16[192,768]{1,0:T(8,128)(2,1)S(1)} %add_convert_fusion.3), channel_id=1, source_target_pairs={{0,8},{4,12},{8,0},{12,4},{16,24},{20,28},{24,16},{28,20},{1,9},{5... | collective-permute-start | bytes 884744 | tf_op jit(solution)/shard_map/ppermute | solution.py:190
  467.1 11.4 %collective-permute-start.17 = (bf16[2,192,192]{1,2,0:T(8,128)(2,1)S(1)}, bf16[2,192,192]{1,2,0:T(8,128)(2,1)S(1)}, u32[]{:S(2)}, u32[]{:S(2)}) collective-permute-start(bf16[2,192,192]{1,2,0:T(8,128)(2,1)S(1)} %maximum_select_fusion.3), channel_id=1, source_target_pairs={{0,16},{4,20},{8,24},{12,28},{16,0},{20,4},{24,8},{28,12},{1,17},{... | collective-permute-start | bytes 442376 | tf_op jit(solution)/shard_map/ppermute | solution.py:190
  487.2 8.2 %collective-permute-start.18 = (bf16[2,192,192]{1,2,0:T(8,128)(2,1)}, bf16[2,192,192]{1,2,0:T(8,128)(2,1)}, u32[]{:S(2)}, u32[]{:S(2)}) collective-permute-start(bf16[2,192,192]{1,2,0:T(8,128)(2,1)} %bitcast.279), channel_id=1, source_target_pairs={{0,1},{1,0},{2,3},{3,2},{4,5},{5,4},{6,7},{7,6},{8,9},{9,8},{10,11... | collective-permute-start | bytes 442376 | tf_op jit(solution)/shard_map/ppermute | solution.py:190
  488.6 37.2 %collective-permute-start.32 = (bf16[192,768]{1,0:T(8,128)(2,1)S(1)}, bf16[192,768]{1,0:T(8,128)(2,1)S(1)}, u32[]{:S(2)}, u32[]{:S(2)}) collective-permute-start(bf16[192,768]{1,0:T(8,128)(2,1)S(1)} %add_convert_fusion.2), channel_id=1, source_target_pairs={{0,16},{4,20},{8,24},{12,28},{16,0},{20,4},{24,8},{28,12},{1,17},{... | collective-permute-start | bytes 884744 | tf_op jit(solution)/shard_map/ppermute | solution.py:190
  490.2 7.9 %collective-permute-start.24 = (bf16[1,192,192]{1,2,0:T(8,128)(2,1)S(1)}, bf16[1,192,192]{1,2,0:T(8,128)(2,1)S(1)}, u32[]{:S(2)}, u32[]{:S(2)}) collective-permute-start(bf16[1,192,192]{1,2,0:T(8,128)(2,1)S(1)} %dynamic-slice_convert_fusion.2), channel_id=1, source_target_pairs={{0,2},{1,3},{2,0},{3,1},{4,6},{5,7},{6,4},{7,5},{8,10},{9,11},{10,... | collective-permute-start | bytes 221192 | tf_op jit(solution)/shard_map/ppermute | solution.py:190
  490.6 31.6 %all-to-all-start.9 = ((bf16[4,3,64,512]{3,2,1,0:T(8,128)(2,1)}), bf16[4,3,64,512]{3,2,1,0:T(8,128)(2,1)S(1)}, u32[]{:S(2)}, u32[]{:S(2)}) async-start(bf16[4,3,64,512]{3,2,1,0:T(8,128)(2,1)} %copy.268), calls=%async_computation.9 | async-start | bytes 1572864 | tf_op jit(solution)/shard_map/all_to_all | solution.py:163
  498.1 4.9 collective-permute-start.25
  503.1 23.6 %collective-permute-start.26 = (bf16[1,192,192]{1,2,0:T(8,128)(2,1)S(1)}, bf16[1,192,192]{1,2,0:T(8,128)(2,1)S(1)}, u32[]{:S(2)}, u32[]{:S(2)}) collective-permute-start(bf16[1,192,192]{1,2,0:T(8,128)(2,1)S(1)} %bitcast.309), channel_id=1, source_target_pairs={{0,8},{4,12},{8,0},{12,4},{16,24},{20,28},{24,16},{28,20},{1,9},{5... | collective-permute-start | bytes 221192 | tf_op jit(solution)/shard_map/ppermute | solution.py:190
  505.8 23.8 %collective-permute-start.21 = (bf16[1,192,192]{1,2,0:T(8,128)(2,1)S(1)}, bf16[1,192,192]{1,2,0:T(8,128)(2,1)S(1)}, u32[]{:S(2)}, u32[]{:S(2)}) collective-permute-start(bf16[1,192,192]{1,2,0:T(8,128)(2,1)S(1)} %bitcast.312), channel_id=1, source_target_pairs={{0,8},{4,12},{8,0},{12,4},{16,24},{20,28},{24,16},{28,20},{1,9},{5... | collective-permute-start | bytes 221192 | tf_op jit(solution)/shard_map/ppermute | solution.py:190
  522.2 33.1 %all-to-all-start.10 = ((bf16[4,3,64,512]{3,2,1,0:T(8,128)(2,1)}), bf16[4,3,64,512]{3,2,1,0:T(8,128)(2,1)S(1)}, u32[]{:S(2)}, u32[]{:S(2)}) async-start(bf16[4,3,64,512]{3,2,1,0:T(8,128)(2,1)} %pad_maximum_fusion.4), calls=%async_computation.10 | async-start | bytes 1572864 | tf_op jit(solution)/shard_map/all_to_all | solution.py:163
  525.7 120.8 %all-reduce.5.cloned.1.call-start = ((), (), s32[]{:S(2)}) async-start(), calls=%async_computation.22 | async-start | bytes 2654208 | tf_op jit(solution)/shard_map/psum | solution.py:185
  526.8 33.6 %collective-permute-start.27 = (bf16[2,192,192]{1,2,0:T(8,128)(2,1)S(1)}, bf16[2,192,192]{1,2,0:T(8,128)(2,1)}, u32[]{:S(2)}, u32[]{:S(2)}) collective-permute-start(bf16[2,192,192]{1,2,0:T(8,128)(2,1)S(1)} %maximum_select_fusion.7), channel_id=1, source_target_pairs={{0,16},{4,20},{8,24},{12,28},{16,0},{20,4},{24,8},{28,12},{1,17},{... | collective-permute-start | bytes 442376 | tf_op jit(solution)/shard_map/ppermute | solution.py:190
  529.7 33.2 %collective-permute-start.22 = (bf16[2,192,192]{1,2,0:T(8,128)(2,1)S(1)}, bf16[2,192,192]{1,2,0:T(8,128)(2,1)}, u32[]{:S(2)}, u32[]{:S(2)}) collective-permute-start(bf16[2,192,192]{1,2,0:T(8,128)(2,1)S(1)} %maximum_select_fusion.5), channel_id=1, source_target_pairs={{0,16},{4,20},{8,24},{12,28},{16,0},{20,4},{24,8},{28,12},{1,17},{... | collective-permute-start | bytes 442376 | tf_op jit(solution)/shard_map/ppermute | solution.py:190
  567.4 5.3 collective-permute-start.10
  577.1 5.0 collective-permute-start.12
  (74 other events, 733.6 us)
Sparse Core Ops, SparseCore 0:
  14.5 20.1 all-gather.8
  36.9 17.4 all-gather.10
  56.5 17.4 all-gather.12
  75.3 17.4 all-gather.14
  94.8 98.5 all-gather.20
  194.8 28.7 all-gather.16
  266.7 21.2 all-gather.18
  292.1 28.1 reduce-scatter.4
  322.9 40.3 reduce-scatter.2
  564.2 82.2 all-reduce.4
